TPU v7x, 128 devices: a whole 4x4x4 slice. The times are simulated.
128 devices in a mesh: tm: 32 (over x, z, core), tp: 4 (over y).
Axes of the slice: x: 4, y: 4, z: 4, core: 2. Of those that a mesh axis runs over, the one named last changes fastest.
Arguments:
- trajectory: float32 [64, 128, 3072], P('tm', None, 'tp'), may hold values from -6 to 6
- offset: int32 [1], replicated, may hold values from 0 to 63
- step_gaps: int32 [64], P('tm'), may hold values from 1 to 4, as said below
- qkv_weight: bfloat16 [3072, 3, 3072], P(None, None, 'tp')
- out_weight: bfloat16 [3072, 3072], P('tp'), may hold values from -4 to 4
- mod_weight: bfloat16 [256, 3, 3072], P(None, None, 'tp'), may hold values from -0.375 to 0.375
Outputs:
- advanced: float32 [64, 128, 3072], P('tm', None, 'tp')
Inputs may be any that keep to these rules, and one draw needn't show every extreme that they name: `step_gaps`: in aligned blocks of 2 timesteps, the gaps of block b sum to an even number for even b and to an odd number for odd b.
All inputs are finite; a program needn't handle non-finite values.
Results may differ from a plain program's by a relative error of at most 0.007.
Values may be sent and summed in bfloat16 or wider, within the bound.
No kernel may reach another device: no remote copies, remote signals or barrier semaphores. Data moves between devices by JAX's collectives and lax.ppermute only.
A program may use at most 128 MiB of HBM per device.

v0:
```python
import math

import jax
import jax.numpy as jnp
from jax import lax
from jax.sharding import PartitionSpec as P

HD = 128
FREQ = 256
ITERS = 2


def prefix(array, axis, combine, identity):
    size, place = (lax.axis_size(axis), lax.axis_index(axis))
    everything = lax.all_gather(array, axis)
    start = jnp.broadcast_to(jnp.asarray(identity, array.dtype), array.shape)

    def turn(k, before):
        reached = k < place
        new = combine(before, everything[k])
        return jnp.where(reached, new, before)

    return lax.fori_loop(0, size, turn, start)


def broadcast(block, axis, holder):
    block = jnp.where(lax.axis_index(axis) == holder, block, jnp.zeros_like(block))
    return lax.psum(block, axis)


def prefix_2(array, axis, join, neutral):
    place = lax.axis_index(axis)
    gathered = lax.all_gather(array.astype(jnp.bfloat16), axis)
    state = jnp.zeros_like(array) + jnp.asarray(neutral, array.dtype)

    def one(turn, state):
        return join(state, lax.dynamic_index_in_dim(gathered, turn, 0, False).astype(array.dtype))

    return lax.fori_loop(0, place, one, state)


def add_up(earlier, later):
    return earlier + later


def embedding(sigma):
    half_freq = FREQ // 2
    frequencies = jnp.exp(-math.log(10000.0) * jnp.arange(half_freq, dtype=jnp.float32) / half_freq)
    angles = 1000.0 * sigma[:, None] * frequencies[None, :]
    return jnp.concatenate([jnp.cos(angles), jnp.sin(angles)], -1).astype(jnp.bfloat16)


def body(trajectory, offset, step_gaps, qkv_weight, out_weight, mod_weight):
    steps_here, tok_count, col_count = trajectory.shape
    full_width = qkv_weight.shape[0]
    time_count = steps_here * lax.axis_size("tm")
    level_count = 5 * time_count
    before = prefix(jnp.sum(step_gaps), "tm", add_up, jnp.int32(0))
    levels = (offset[0] + before + jnp.cumsum(step_gaps) - step_gaps).astype(jnp.float32)
    sigma = 1.0 - levels / level_count
    step_size = step_gaps.astype(jnp.float32) / level_count
    embed_rows = embedding(sigma)
    full_mod = lax.all_gather(mod_weight, "tp", axis=2, tiled=True)
    modulation = jnp.dot(
        embed_rows, full_mod.reshape(FREQ, 3 * full_width), preferred_element_type=jnp.float32
    ).reshape(steps_here, 3, full_width)
    gate_rows = lax.dynamic_slice_in_dim(
        modulation[:, 2], lax.axis_index("tp") * col_count, col_count, 1
    )
    base_point = broadcast(trajectory[0], "tm", 0)
    flat_qkv = qkv_weight.reshape(full_width, -1)
    states = trajectory
    points = trajectory
    for sweep in range(ITERS):
        whole_rows = lax.all_gather(states, "tp", axis=2, tiled=True)
        row_mean = jnp.sum(whole_rows, -1, keepdims=True) / full_width
        variance = (
            jnp.sum(whole_rows * whole_rows, -1, keepdims=True) / full_width - row_mean * row_mean
        )
        inv_std = lax.rsqrt(variance + 1e-06)
        normed = (
            (whole_rows - row_mean) * inv_std * (1.0 + modulation[:, 1][:, None, :])
            + modulation[:, 0][:, None, :]
        ).astype(jnp.bfloat16)
        projected = jnp.einsum("std,de->ste", normed, flat_qkv, preferred_element_type=jnp.float32)
        projected = projected.astype(jnp.bfloat16).reshape(steps_here, tok_count, 3, -1, HD)
        queries = projected[:, :, 0]
        key_rows = projected[:, :, 1]
        values = projected[:, :, 2]
        scores = jnp.einsum(
            "sqhd,skhd->shqk", queries, key_rows, preferred_element_type=jnp.float32
        ) * (1.0 / math.sqrt(HD))
        row_max = jnp.max(scores, -1, keepdims=True)
        weights_exp = jnp.exp(scores - row_max)
        probs = (weights_exp / jnp.sum(weights_exp, -1, keepdims=True)).astype(jnp.bfloat16)
        attended = jnp.einsum(
            "shqk,skhd->sqhd", probs, values, preferred_element_type=jnp.float32
        ).astype(jnp.bfloat16)
        attended = attended.reshape(steps_here, tok_count, -1)
        head_out = jnp.einsum(
            "sqe,ed->sqd", attended, out_weight, preferred_element_type=jnp.float32
        )
        col_share = lax.psum_scatter(
            head_out.astype(jnp.bfloat16), "tp", scatter_dimension=2, tiled=True
        ).astype(jnp.float32)
        drifts = gate_rows[:, None, :] * col_share
        increments = -step_size[:, None, None] * drifts
        local_cum = jnp.cumsum(increments, 0)
        prefix_sum = prefix_2(
            local_cum[-1], "tm", add_up, jnp.zeros((tok_count, col_count), jnp.float32)
        )
        entry_point = prefix_sum + base_point
        points = entry_point[None] + local_cum
        states = jnp.concatenate([entry_point[None], points[:-1]], 0)
    return points


def solution(mesh):
    placed = (
        P("tm", None, "tp"),
        P(),
        P("tm"),
        P(None, None, "tp"),
        P("tp", None),
        P(None, None, "tp"),
    )
    return jax.shard_map(
        body, mesh=mesh, in_specs=placed, out_specs=P("tm", None, "tp"), check_vma=False
    )
```

profile of v0, /device:TPU:103, one launch (start us, length us, event | category | flops | bytes accessed | tf_op | source)
XLA Modules:
  0.0 483.2 jit_solution(12489201418532556773)
XLA Ops:
  7.3 2.4 copy.33
  11.3 18.7 %copy.34 = bf16[3072,3,768]{0,2,1:T(8,128)(2,1)} copy(bf16[3072,3,768]{2,0,1:T(8,128)(2,1)} %param.15) | data formatting | bytes 28311552 | tf_op args[3]
  30.7 1.4 dynamic-update-slice
  32.0 8.7 %all-reduce = s32[32]{0:T(128)S(1)} all-reduce(s32[32]{0:T(128)S(1)} %dynamic-update-slice), channel_id=1, replica_groups=mesh['tm'=32,'tp'=4] {'tm'}, use_global_device_ids=true, to_apply=%add | all-reduce | flops 32 | bytes 256
  40.7 40.6 %while.33 = (s32[]{:T(128)}, s32[]{:T(128)}, s32[]{:T(128)}, s32[32]{0:T(128)S(1)}, s32[]{:T(128)}) while((s32[]{:T(128)}, s32[]{:T(128)}, s32[]{:T(128)}, s32[32]{0:T(128)S(1)}, s32[]{:T(128)}) %tuple.62), condition=%wide.region_2.3_spmd, body=%wide.region_1.2_spmd.sunk | while | flops 5 | bytes 107 | solution.py:23
  81.5 2.5 fusion.55
  84.0 20.4 %all-gather.6.cloned.1.call-done = bf16[256,3,3072]{0,2,1:T(8,128)(2,1)} async-done(((bf16[256,3,768]{0,2,1:T(8,128)(2,1)}), bf16[256,3,3072]{0,2,1:T(8,128)(2,1)}) %all-gather.6.cloned.1.call-update) | async-done | bytes 4718608 | tf_op jit(solution)/shard_map/all_gather | solution.py:63
  104.4 3.6 fusion.2
  108.1 10.1 %convolution_convert_fusion.1 = bf16[2,128,2304]{2,1,0:T(8,128)(2,1)} fusion(bf16[3072,2304,1]{0,1,2:T(8,128)(2,1)} %bitcast.116, f32[2,128,3072]{2,1,0:T(8,128)S(1)} %copy-done, f32[2,3072]{1,0:T(2,128)S(1)} %get-tuple-element.162, f32[2,3072]{1,0:T(2,128)S(1)} %get-tuple-element.163, f32[2,128]{1,0:T(2,128)S(1)} %get-tuple-element.167, ...), kind=kOutput, calls=%fused_computation.13 | convolution fusion | flops 3628400640 | bytes 18532352 | tf_op jit(solution)/shard_map/std,de->ste/dot_general | solution.py:85
  118.2 1.7 copy.36
  121.0 4.9 %fusion.8 = bf16[2,128,3072]{2,1,0:T(8,128)(2,1)} fusion(bf16[2,128,768]{1,2,0:T(8,128)(2,1)S(1)} %bitcast.125, bf16[768,3072]{1,0:T(8,128)(2,1)} %param.16), kind=kOutput, calls=%fused_computation.10 | convolution fusion | flops 1208745984 | bytes 6684672 | tf_op jit(solution)/shard_map/sqe,ed->sqd/dot_general | solution.py:100
  126.0 25.2 %reduce-scatter.3.cloned.1.call-done = bf16[2,128,768]{2,1,0:T(8,128)(2,1)} async-done(((bf16[2,128,3072]{2,1,0:T(8,128)(2,1)}), bf16[2,128,768]{2,1,0:T(8,128)(2,1)}) %reduce-scatter.3.cloned.1.call-update) | async-done | bytes 393232 | tf_op jit(solution)/shard_map/reduce_scatter | solution.py:103
  151.2 1.1 fusion.30
  154.0 47.3 %all-gather.10.cloned.1.call-done = bf16[32,128,768]{2,1,0:T(8,128)(2,1)} async-done(((bf16[1,128,768]{2,1,0:T(8,128)(2,1)}), bf16[32,128,768]{2,1,0:T(8,128)(2,1)}) %all-gather.10.cloned.1.call-update) | async-done | bytes 6291472 | tf_op jit(solution)/shard_map/all_gather | solution.py:33
  201.3 31.9 %while.34 = (s32[]{:T(128)}, f32[128,768]{1,0:T(8,128)S(1)}, s32[]{:T(128)}, bf16[32,128,768]{2,1,0:T(8,128)(2,1)}, s32[]{:T(128)}, /*index=5*/s32[]{:T(128)}, s32[]{:T(128)}) while((s32[]{:T(128)}, f32[128,768]{1,0:T(8,128)S(1)}, s32[]{:T(128)}, bf16[32,128,768]{2,1,0:T(8,128)(2,1)}, s32[]{:T(128)}, /*index=5*/s32[]{:T(128)}, ...), condition=%wide.region_11.12_spmd, body=%wide.region_10.11_spmd.sunk | while | flops 196613 | bytes 983155 | solution.py:39
  201.3 1.0 convert_add_fusion.4
  202.4 1.0 convert_add_fusion.4
  203.4 1.0 convert_add_fusion.4
  204.4 1.0 convert_add_fusion.4
  205.5 1.0 convert_add_fusion.4
  206.5 1.0 convert_add_fusion.4
  207.5 1.0 convert_add_fusion.4
  208.5 1.0 convert_add_fusion.4
  209.6 1.0 convert_add_fusion.4
  211.6 1.0 convert_add_fusion.4
  212.7 1.0 convert_add_fusion.4
  213.7 1.0 convert_add_fusion.4
  214.7 1.0 convert_add_fusion.4
  215.7 1.0 convert_add_fusion.4
  216.8 1.0 convert_add_fusion.4
  217.8 1.0 convert_add_fusion.4
  218.8 1.0 convert_add_fusion.4
  219.9 1.0 convert_add_fusion.4
  220.9 1.0 convert_add_fusion.4
  221.9 1.0 convert_add_fusion.4
  223.0 1.0 convert_add_fusion.4
  224.0 1.0 convert_add_fusion.4
  225.0 1.0 convert_add_fusion.4
  226.0 1.0 convert_add_fusion.4
  227.1 1.0 convert_add_fusion.4
  228.1 1.0 convert_add_fusion.4
  229.1 1.0 convert_add_fusion.4
  230.2 1.0 convert_add_fusion.4
  231.2 1.0 convert_add_fusion.4
  232.2 1.0 convert_add_fusion.4
  233.2 73.6 %all-reduce.3.cloned.1.call-done = f32[128,768]{1,0:T(8,128)} async-done(((f32[128,768]{1,0:T(8,128)}), f32[128,768]{1,0:T(8,128)}) %all-reduce.3.cloned.1.call-update) | async-done | bytes 393232 | tf_op jit(solution)/shard_map/psum | solution.py:28
  306.8 1.0 add.136
  309.1 40.2 %all-gather.12.cloned.1.call-done = f32[2,128,3072]{2,1,0:T(8,128)} async-done(((f32[2,128,768]{2,1,0:T(8,128)}), f32[2,128,3072]{2,1,0:T(8,128)}) %all-gather.12.cloned.1.call-update) | async-done | bytes 3145744 | tf_op jit(solution)/shard_map/all_gather | solution.py:75
  349.3 2.6 fusion.54
  352.1 9.1 %convolution_convert_fusion = bf16[2,128,2304]{2,1,0:T(8,128)(2,1)S(1)} fusion(bf16[3072,2304,1]{0,1,2:T(8,128)(2,1)} %bitcast.117, f32[2,128,3072]{2,1,0:T(8,128)S(1)} %copy-done.1, f32[2,128]{1,0:T(2,128)S(1)} %get-tuple-element.165, f32[2,128]{1,0:T(2,128)S(1)} %get-tuple-element.164, f32[2,3072]{1,0:T(2,128)S(1)} %get-tuple-element.162, ...), kind=kOutput, calls=%fused_computation.12 | convolution fusion | flops 3628400640 | bytes 18532352 | tf_op jit(solution)/shard_map/std,de->ste/dot_general | solution.py:85
  363.1 4.9 %fusion.11 = bf16[2,128,3072]{2,1,0:T(8,128)(2,1)} fusion(bf16[2,128,768]{1,2,0:T(8,128)(2,1)S(1)} %bitcast.126, bf16[768,3072]{1,0:T(8,128)(2,1)} %param.16), kind=kOutput, calls=%fused_computation.11 | convolution fusion | flops 1208745984 | bytes 6684672 | tf_op jit(solution)/shard_map/sqe,ed->sqd/dot_general | solution.py:100
  368.1 25.1 %reduce-scatter.5.cloned.1.call-done = bf16[2,128,768]{2,1,0:T(8,128)(2,1)} async-done(((bf16[2,128,3072]{2,1,0:T(8,128)(2,1)}), bf16[2,128,768]{2,1,0:T(8,128)(2,1)}) %reduce-scatter.5.cloned.1.call-update) | async-done | bytes 393232 | tf_op jit(solution)/shard_map/reduce_scatter | solution.py:103
  393.2 1.1 fusion.26
  395.0 48.4 %all-gather.14.cloned.1.call-done = bf16[32,128,768]{2,1,0:T(8,128)(2,1)} async-done(((bf16[1,128,768]{2,1,0:T(8,128)(2,1)}), bf16[32,128,768]{2,1,0:T(8,128)(2,1)}) %all-gather.14.cloned.1.call-update) | async-done | bytes 6291472 | tf_op jit(solution)/shard_map/all_gather | solution.py:33
  443.5 31.9 %while.35 = (s32[]{:T(128)}, f32[128,768]{1,0:T(8,128)S(1)}, s32[]{:T(128)}, bf16[32,128,768]{2,1,0:T(8,128)(2,1)}, s32[]{:T(128)}, /*index=5*/s32[]{:T(128)}, s32[]{:T(128)}) while((s32[]{:T(128)}, f32[128,768]{1,0:T(8,128)S(1)}, s32[]{:T(128)}, bf16[32,128,768]{2,1,0:T(8,128)(2,1)}, s32[]{:T(128)}, /*index=5*/s32[]{:T(128)}, ...), condition=%wide.region_20.21_spmd, body=%wide.region_19.20_spmd.sunk | while | flops 196613 | bytes 983155 | solution.py:39
  443.5 1.0 convert_add_fusion.5
  444.5 1.0 convert_add_fusion.5
  445.5 1.0 convert_add_fusion.5
  447.6 1.0 convert_add_fusion.5
  448.6 1.0 convert_add_fusion.5
  449.7 1.0 convert_add_fusion.5
  450.7 1.0 convert_add_fusion.5
  451.7 1.0 convert_add_fusion.5
  452.7 1.0 convert_add_fusion.5
  (111 shorter events, 52.9 us)
Async XLA Ops:
  6.5 3.3 copy-start.4
  6.5 75.0 %all-gather.8.cloned.1.call-start = ((), (), s32[]{:S(2)}) async-start(), calls=%async_computation.3 | async-start | bytes 3932160 | tf_op jit(solution)/shard_map/all_gather | solution.py:75
  7.3 97.2 %all-gather.6.cloned.1.call-start = ((), (), s32[]{:S(2)}) async-start(), calls=%async_computation.2 | async-start | bytes 5898240 | tf_op jit(solution)/shard_map/all_gather | solution.py:63
  9.7 141.5 %reduce-scatter.3.cloned.1.call-start = ((), (), s32[]{:S(2)}) async-start(), calls=%async_computation.4 | async-start | bytes 1966080 | tf_op jit(solution)/shard_map/reduce_scatter | solution.py:103
  11.3 18.7 %copy-start.5 = (u32[128]{0:T(128)S(1)}, u32[128]{0:T(128)}, u32[]{:S(2)}) copy-start(u32[128]{0:T(128)} %constant.91) | copy-start | bytes 1540
  84.0 24.1 %copy-start = (f32[2,128,3072]{2,1,0:T(8,128)S(1)}, f32[2,128,3072]{2,1,0:T(8,128)}, u32[]{:S(2)}) copy-start(f32[2,128,3072]{2,1,0:T(8,128)} %all-gather.8.cloned.1.call-done) | copy-start | bytes 9437188
  125.9 27.2 %copy-start.2 = (f32[2,128,768]{2,1,0:T(8,128)S(1)}, f32[2,128,768]{2,1,0:T(8,128)}, u32[]{:S(2)}) copy-start(f32[2,128,768]{2,1,0:T(8,128)} %param.12) | copy-start | bytes 2359300
  125.9 75.4 %all-gather.10.cloned.1.call-start = ((), (), s32[]{:S(2)}) async-start(), calls=%async_computation.5 | async-start | bytes 6488064 | tf_op jit(solution)/shard_map/all_gather | solution.py:33
  153.0 153.8 %all-reduce.3.cloned.1.call-start = ((), (), s32[]{:S(2)}) async-start(), calls=%async_computation.6 | async-start | bytes 786432 | tf_op jit(solution)/shard_map/psum | solution.py:28
  153.9 195.4 %all-gather.12.cloned.1.call-start = ((), (), s32[]{:S(2)}) async-start(), calls=%async_computation.7 | async-start | bytes 3932160 | tf_op jit(solution)/shard_map/all_gather | solution.py:75
  308.9 84.3 %reduce-scatter.5.cloned.1.call-start = ((), (), s32[]{:S(2)}) async-start(), calls=%async_computation.8 | async-start | bytes 1966080 | tf_op jit(solution)/shard_map/reduce_scatter | solution.py:103
  349.3 2.8 copy-start.1
  368.1 75.4 %all-gather.14.cloned.1.call-start = ((), (), s32[]{:S(2)}) async-start(), calls=%async_computation.9 | async-start | bytes 6488064 | tf_op jit(solution)/shard_map/all_gather | solution.py:33
  394.3 81.1 %copy-start.3 = (f32[128,768]{1,0:T(8,128)S(1)}, f32[128,768]{1,0:T(8,128)}, u32[]{:S(2)}) copy-start(f32[128,768]{1,0:T(8,128)} %all-reduce.3.cloned.1.call-done) | copy-start | bytes 1179652
Sparse Core Ops, SparseCore 0:
  9.0 40.7 all-gather.7
  51.5 52.8 all-gather.5
  126.0 25.1 reduce-scatter.2
  153.3 47.9 all-gather.9
  204.4 102.4 all-reduce.2
  309.0 40.2 all-gather.11
  368.2 24.9 reduce-scatter.4
  395.4 47.9 all-gather.13
where the time goes:
time: 486 us; the launch traced here: 483 us
  waiting for transfers between devices  281 us (58%)
  other arithmetic  74.2 us (15%)
  local copies, waits for them, and re-layouts  46.7 us (10%)
  matrix products  34.9 us (7%)
  loops' own time  22.8 us (5%)
  between operations  14.4 us (3%)
  blocking collectives  8.69 us (2%)
    all_gather x2, waiting for transfers between devices, prefix_2(): gathered = lax.all_gather(array.astype(jnp.bfloat16), axis)  95.7 us
    psum x1, waiting for transfers between devices, broadcast(): return lax.psum(block, axis)  73.6 us
    add x62, other arithmetic, add_up(): return earlier + later  62.1 us
    reduce_scatter x2, waiting for transfers between devices, body(): lax.psum_scatter(head_out.astype(jnp.bfloat16), 'tp', scatter_dimension=2...  50.3 us
    all_gather x2, waiting for transfers between devices, body(): whole_rows = lax.all_gather(states, 'tp', axis=2, tiled=True)  40.2 us
    unnamed x17, local copies, waits for them, and re-layouts  23.4 us
    another operation x1, loops' own time, prefix(): return lax.fori_loop(0, size, turn, start)  21.1 us
    all_gather x1, waiting for transfers between devices, body(): full_mod = lax.all_gather(mod_weight, 'tp', axis=2, tiled=True)  20.4 us
  transfers between devices with their start and end apart: 8, of which 7 were waited for; matrix products, arithmetic and copies ran while one was open for 16% of the time, Pallas kernels for 0%

commit v1 on v0

v1 whole, which is shorter than its diff:
```python
import math

import jax
import jax.numpy as jnp
from jax import lax
from jax.experimental import pallas as pl
from jax.experimental.pallas import tpu as pltpu
from jax.sharding import PartitionSpec as P

HD = 128
FREQ = 256
ITERS = 2
NX, NZ, NC, NY = 4, 4, 2, 4
BF = jnp.bfloat16
F32 = jnp.float32


def ring(k):
    return [(i, (i + k) % NY) for i in range(NY)]


def place(x, z, c):
    return (x * NZ + z) * NC + c


CHIPS = [(x, z, c) for x in range(NX) for z in range(NZ) for c in range(NC)]
SWAP = [(place(x, z, c), place(x, z, 1 - c)) for x, z, c in CHIPS]


def z_shift(k):
    return [(place(x, z, c), place(x, (z + k) % NZ, c)) for x, z, c in CHIPS]


def x_shift(k):
    return [(place(x, z, c), place((x + k) % NX, z, c)) for x, z, c in CHIPS]


def spread(array):
    return [array] + [lax.ppermute(array, "tp", ring(k)) for k in (1, 2, 3)]


def deliver(own, blocks):
    total = own
    for k, block in zip((1, 2, 3), blocks, strict=True):
        total = total + lax.ppermute(block, "tp", ring(k)).astype(F32)
    return total


def embedding(sigma):
    half_freq = FREQ // 2
    frequencies = jnp.exp(-math.log(10000.0) * jnp.arange(half_freq, dtype=F32) / half_freq)
    angles = 1000.0 * sigma[:, None] * frequencies[None, :]
    return jnp.concatenate([jnp.cos(angles), jnp.sin(angles)], -1).astype(BF)


def block_body(first, tok, cols, me_ref, neg_ref, *refs):
    if first:
        states, refs = refs[:4], refs[4:]
        incs = means = None
    else:
        states, incs, means, refs = refs[:4], refs[4:8], refs[8:12], refs[12:]
    mods, (qkv_hbm, out_hbm), refs = refs[:4], refs[4:6], refs[6:]
    tots, ins, refs = refs[:4], refs[4:8], refs[8:]
    wv, wo, nrm, qkv, att, sems = refs
    me = me_ref[0]
    copies = []
    for p in range(3):
        for k in range(NY):
            src = lax.rem(me + NY - k, NY) * cols
            copies.append(
                pltpu.make_async_copy(
                    qkv_hbm.at[p, pl.ds(src, cols), :], wv.at[p, pl.ds(k * cols, cols), :], sems.at[p * NY + k]
                )
            )
    for k in range(NY):
        dst = lax.rem(me + k, NY) * cols
        copies.append(pltpu.make_async_copy(out_hbm.at[:, pl.ds(dst, cols)], wo.at[k], sems.at[3 * NY + k]))
    for copy in copies:
        copy.start()
    width = NY * cols
    for s in range(2):
        rows = pl.ds(s * tok, tok)
        parts = []
        for k in range(NY):
            if first:
                centre = jnp.transpose(mods[k][:, s * tok : (s + 1) * tok])[:, 6:7]
                x = states[k][rows, :].astype(F32) + centre
            else:
                centre = jnp.transpose(means[k][...])[:, 0:1]
                x = states[k][...].astype(F32) + centre
                if s == 1:
                    x = x + incs[k][...].astype(F32)
            parts.append(x)
        mean = sum(jnp.sum(x, -1, keepdims=True) for x in parts) / width
        var = sum(jnp.sum((x - mean) * (x - mean), -1, keepdims=True) for x in parts) / width
        inv = lax.rsqrt(var + 1e-06)
        for k in range(NY):
            shift = mods[k][3 * s : 3 * s + 1, :]
            scale = mods[k][3 * s + 1 : 3 * s + 2, :]
            normed = (parts[k] - mean) * inv * (1.0 + scale) + shift
            nrm[rows, k * cols : (k + 1) * cols] = normed.astype(BF)
    for p in range(3):
        for k in range(NY):
            copies[p * NY + k].wait()
        qkv[p] = jnp.dot(nrm[...], wv[p], preferred_element_type=F32).astype(BF)
    for s in range(2):
        rows = pl.ds(s * tok, tok)
        for h in range(cols // HD):
            lanes = pl.ds(h * HD, HD)
            scores = lax.dot_general(
                qkv[0, rows, lanes], qkv[1, rows, lanes], (((1,), (1,)), ((), ())), preferred_element_type=F32
            ) * (1.0 / math.sqrt(HD))
            weights = jnp.exp(scores - jnp.max(scores, -1, keepdims=True))
            probs = (weights * (1.0 / jnp.sum(weights, -1, keepdims=True))).astype(BF)
            att[rows, lanes] = jnp.dot(probs, qkv[2, rows, lanes], preferred_element_type=F32).astype(BF)
    for k in (1, 2, 3, 0):
        copies[3 * NY + k].wait()
        made = jnp.dot(att[...], wo[k], preferred_element_type=F32)
        gates = mods[(NY - k) % NY]
        inc0 = made[:tok] * (gates[2:3, :] * neg_ref[0])
        inc1 = made[tok:] * (gates[5:6, :] * neg_ref[1])
        tots[k][...] = (inc0 + inc1).astype(tots[k].dtype)
        ins[k][...] = inc0.astype(ins[k].dtype)


def block(first, me, neg, states, mods, qkv_weight, out_weight):
    cols, width = out_weight.shape
    tok = states[0].shape[0] // (2 if first else 1)
    n_arrays = len(states)
    outs = [jax.ShapeDtypeStruct((tok, cols), F32 if k == 0 else BF) for k in range(NY)]

    def body(*refs):
        block_body(first, tok, cols, *refs)

    vmem = pl.BlockSpec(memory_space=pltpu.VMEM)
    smem = pl.BlockSpec(memory_space=pltpu.SMEM)
    hbm = pl.BlockSpec(memory_space=pl.ANY)
    made = pl.pallas_call(
        body,
        out_shape=outs + outs,
        in_specs=[smem, smem] + [vmem] * (n_arrays + NY) + [hbm, hbm],
        out_specs=[vmem] * (2 * NY),
        scratch_shapes=[
            pltpu.VMEM((3, width, cols), BF),
            pltpu.VMEM((NY, cols, cols), BF),
            pltpu.VMEM((2 * tok, width), BF),
            pltpu.VMEM((3, 2 * tok, cols), BF),
            pltpu.VMEM((2 * tok, cols), BF),
            pltpu.SemaphoreType.DMA((4 * NY,)),
        ],
        compiler_params=pltpu.CompilerParams(vmem_limit_bytes=48 * 2**20),
        cost_estimate=pl.CostEstimate(
            flops=2 * 2 * tok * width * 4 * cols, bytes_accessed=8 * width * cols, transcendentals=0
        ),
        name="block",
    )(me, neg, *states, *mods, qkv_weight, out_weight)
    return made[:NY], made[NY:]


def body(trajectory, offset, step_gaps, qkv_weight, out_weight, mod_weight):
    steps_here, tok, cols = trajectory.shape
    width = qkv_weight.shape[0]
    tm, tp = lax.axis_index("tm"), lax.axis_index("tp")
    x_at, z_at, core = tm // (NZ * NC), (tm // NC) % NZ, tm % NC
    time_count = steps_here * lax.axis_size("tm")
    level_count = 5 * time_count
    half = tok // 2

    means = jnp.sum(trajectory, -1) / cols
    centred = (trajectory - means[:, :, None]).astype(BF).reshape(steps_here * tok, cols)
    first_states = spread(centred)

    gap_sum = jnp.sum(step_gaps)
    all_gaps = lax.all_to_all(jnp.broadcast_to(gap_sum, (NX * NZ * NC, 1, 128)), "tm", 0, 0)[:, 0, 0]
    before = jnp.sum(jnp.where(jnp.arange(NX * NZ * NC) < tm, all_gaps, 0))
    gap0, gap1 = step_gaps[0], step_gaps[1]
    levels = (offset[0] + before + jnp.stack([jnp.zeros_like(gap0), gap0])).astype(F32)
    sigma = 1.0 - levels / level_count
    step_size = jnp.stack([gap0, gap1]).astype(F32) / level_count
    flat_mod = jnp.transpose(mod_weight, (1, 0, 2))
    modulation = jnp.stack(
        [jnp.dot(embedding(sigma), flat_mod[p], preferred_element_type=F32) for p in range(3)], 1
    ).reshape(6, cols)
    mean_row = jnp.pad(means.reshape(1, steps_here * tok), ((0, 1), (0, cols - steps_here * tok)))
    mods = spread(jnp.concatenate([modulation, mean_row], 0))

    base = jnp.where(tm == 0, trajectory[0], 0.0)
    for pairs in (
        [(place(0, 0, 0), place(1, 0, 0))],
        [(place(0, 0, 0), place(3, 0, 0)), (place(1, 0, 0), place(2, 0, 0))],
        [(place(x, 0, 0), place(x, 1, 0)) for x in range(NX)],
        [(place(x, a, 0), place(x, b, 0)) for x in range(NX) for a, b in ((0, 3), (1, 2))],
        [(place(x, z, 0), place(x, z, 1)) for x in range(NX) for z in range(NZ)],
    ):
        base = base + lax.ppermute(base, "tm", pairs)
    base_mean = jnp.sum(base, -1) / cols
    base_means = spread(jnp.broadcast_to(base_mean[None], (8, tok)))

    me = jnp.reshape(tp, (1,)).astype(jnp.int32)
    neg = -step_size
    weights = (jnp.transpose(qkv_weight, (1, 0, 2)), out_weight)

    def scan(total):
        sent = total.astype(BF)
        other = lax.ppermute(sent, "tm", SWAP).astype(F32)
        chip = sent.astype(F32) + other
        mine = jnp.where(core == 0, chip[:half], chip[half:]).astype(BF)
        plane = mine.astype(F32)
        below = jnp.zeros_like(plane)
        for k in (1, 2, 3):
            came = lax.ppermute(mine, "tm", z_shift(k)).astype(F32)
            plane = plane + came
            below = below + jnp.where(z_at >= k, came, 0.0)
        plane = plane.astype(BF)
        for k in (1, 2, 3):
            came = lax.ppermute(plane, "tm", x_shift(k)).astype(F32)
            below = below + jnp.where(x_at >= k, came, 0.0)
        below = below.astype(BF)
        rest = lax.ppermute(below, "tm", SWAP)
        low = jnp.where(core == 0, below, rest)
        high = jnp.where(core == 0, rest, below)
        prefix = jnp.concatenate([low, high], 0).astype(F32)
        return base + prefix + jnp.where(core == 0, 0.0, other)

    states = first_states
    for sweep in range(ITERS):
        tots, incs = block(sweep == 0, me, neg, states, mods, *weights)
        total = deliver(tots[0], tots[1:])
        inc0 = deliver(incs[0], incs[1:])
        entry = scan(total)
        if sweep + 1 < ITERS:
            states = (
                spread((entry - base_mean[:, None]).astype(BF)) + spread(inc0.astype(BF)) + base_means
            )
    return jnp.stack([entry + inc0, entry + total])


def solution(mesh):
    placed = (
        P("tm", None, "tp"),
        P(),
        P("tm"),
        P(None, None, "tp"),
        P("tp", None),
        P(None, None, "tp"),
    )
    return jax.shard_map(
        body, mesh=mesh, in_specs=placed, out_specs=P("tm", None, "tp"), check_vma=False
    )
```

time: 486 us -> 174 us (0.36)
  the two profiles are of different devices: /device:TPU:103 before, /device:TPU:1 now
where the time goes in v1:
time: 174 us
  starting transfers between devices  74.8 us (43%)
  waiting for transfers between devices  56 us (32%)
  Pallas kernels  29.5 us (17%)
  other arithmetic  6.2 us (4%)
  matrix products  3.52 us (2%)
  local copies, waits for them, and re-layouts  1.97 us (1%)
    pallas_call x2, Pallas kernels, block(): pl.pallas_call(body, out_shape=outs + outs, in_specs=[smem, smem] + [vmem...  29.5 us
    ppermute x12, waiting for transfers between devices, deliver(): total = total + lax.ppermute(block, 'tp', ring(k)).astype(F32)  20.5 us
    ppermute x15, starting transfers between devices, spread(): return [array] + [lax.ppermute(array, 'tp', ring(k)) for k in (1, 2, 3)]  15.6 us
    ppermute x15, waiting for transfers between devices, spread(): return [array] + [lax.ppermute(array, 'tp', ring(k)) for k in (1, 2, 3)]  14.9 us
    ppermute x2, starting transfers between devices, scan(): other = lax.ppermute(sent, 'tm', SWAP).astype(F32)  11.9 us
    ppermute x12, starting transfers between devices, deliver(): total = total + lax.ppermute(block, 'tp', ring(k)).astype(F32)  11.3 us
    all_to_all x1, starting transfers between devices, body(): lax.all_to_all(jnp.broadcast_to(gap_sum, (NX * NZ * NC, 1, 128)), 'tm', 0...  9.44 us
    ppermute x6, starting transfers between devices, scan(): came = lax.ppermute(mine, 'tm', z_shift(k)).astype(F32)  8.29 us
  transfers between devices with their start and end apart: 49, of which 26 were waited for; matrix products, arithmetic and copies ran while one was open for 5% of the time, Pallas kernels for 8%

profile of v1, /device:TPU:1, one launch (start us, length us, event | category | flops | bytes accessed | tf_op | source)
XLA Modules:
  0.0 173.6 jit_solution(3807679137509190556)
XLA Ops:
  0.0 1.3 reduce_sum.36
  1.5 2.2 %collective-permute-start.5 = (bf16[256,768]{1,0:T(8,128)(2,1)S(1)}, bf16[256,768]{1,0:T(8,128)(2,1)S(1)}, u32[]{:S(2)}, u32[]{:S(2)}) collective-permute-start(bf16[256,768]{1,0:T(8,128)(2,1)S(1)} %bitcast.31), channel_id=1, source_target_pairs={{0,1},{1,2},{2,3},{3,0},{4,5},{5,6},{6,7},{7,4},{8,9},{9,10},{10,1... | collective-permute-start | bytes 1179656 | tf_op jit(solution)/shard_map/ppermute | solution.py:39
  3.7 2.6 %collective-permute-start.6 = (bf16[256,768]{1,0:T(8,128)(2,1)S(1)}, bf16[256,768]{1,0:T(8,128)(2,1)S(1)}, u32[]{:S(2)}, u32[]{:S(2)}) collective-permute-start(bf16[256,768]{1,0:T(8,128)(2,1)S(1)} %bitcast.32), channel_id=1, source_target_pairs={{0,2},{1,3},{2,0},{3,1},{4,6},{5,7},{6,4},{7,5},{8,10},{9,11},{10,... | collective-permute-start | bytes 1179656 | tf_op jit(solution)/shard_map/ppermute | solution.py:39
  6.3 1.1 collective-permute-start.7
  8.0 1.2 broadcast_in_dim.46
  9.2 9.4 %all-to-all-start = ((s32[32,1,128]{2,1,0:T(1,128)}), s32[32,1,128]{2,1,0:T(1,128)S(1)}, u32[]{:S(2)}, u32[]{:S(2)}) async-start(s32[32,1,128]{2,1,0:T(1,128)} %broadcast_in_dim.46), calls=%async_computation | async-start | bytes 32768 | tf_op jit(solution)/shard_map/all_to_all | solution.py:174
  19.4 6.2 %all-to-all-done = s32[32,1,128]{2,1,0:T(1,128)S(1)} async-done(((s32[32,1,128]{2,1,0:T(1,128)}), s32[32,1,128]{2,1,0:T(1,128)S(1)}, u32[]{:S(2)}, u32[]{:S(2)}) %all-to-all-start) | async-done | bytes 16416 | tf_op jit(solution)/shard_map/all_to_all | solution.py:174
  25.6 0.7 slice_reduce_fusion
  26.2 0.6 fusion.23
  27.8 1.2 convolution_bitcast_fusion
  28.9 1.2 convolution_bitcast_fusion.1
  30.1 1.2 convolution_bitcast_fusion.2
  31.4 0.8 select_bitcast_fusion
  32.2 1.5 collective-permute-start.8
  34.6 1.5 collective-permute-done.8.refs_7_.refs_15_
  36.1 0.7 collective-permute-start
  36.8 1.5 collective-permute-done.9.refs_8_.refs_16_
  38.3 14.7 %block.2 = (f32[128,768]{1,0:T(8,128)S(1)}, bf16[128,768]{1,0:T(8,128)(2,1)S(1)}, bf16[128,768]{1,0:T(8,128)(2,1)S(1)}, bf16[128,768]{1,0:T(8,128)(2,1)S(1)}, f3...) custom-call(s32[1]{0:T(128)} %bitcast.1.refs_0_, ...), custom_call_target="tpu_custom_call" | custom-call | flops 4831838208 | bytes 18874368 | tf_op jit(solution)/shard_map/block/pallas_call | solution.py:138
  53.4 2.0 %collective-permute-start.12 = (bf16[128,768]{1,0:T(8,128)(2,1)S(1)}, bf16[128,768]{1,0:T(8,128)(2,1)S(1)}, u32[]{:S(2)}, u32[]{:S(2)}) collective-permute-start(bf16[128,768]{1,0:T(8,128)(2,1)S(1)} %get-tuple-element.23), channel_id=1, source_target_pairs={{0,2},{1,3},{2,0},{3,1},{4,6},{5,7},{6,4},{7,5},{8,10},{9,11},{10,... | collective-permute-start | bytes 589832 | tf_op jit(solution)/shard_map/ppermute | solution.py:45
  56.0 0.7 collective-permute-start.1
  56.7 3.4 %collective-permute-done.11 = bf16[128,768]{1,0:T(8,128)(2,1)S(1)} collective-permute-done((bf16[128,768]{1,0:T(8,128)(2,1)S(1)}, bf16[128,768]{1,0:T(8,128)(2,1)S(1)}, u32[]{:S(2)}, u32[]{:S(2)}) %collective-permute-start.11) | collective-permute-done | bytes 196640 | tf_op jit(solution)/shard_map/ppermute | solution.py:45
  60.1 1.7 collective-permute-done.12
  62.4 4.2 %collective-permute-start.14 = (bf16[128,768]{1,0:T(8,128)(2,1)S(1)}, bf16[128,768]{1,0:T(8,128)(2,1)S(1)}, u32[]{:S(2)}, u32[]{:S(2)}) collective-permute-start(bf16[128,768]{1,0:T(8,128)(2,1)S(1)} %add_convert_fusion.1), channel_id=1, source_target_pairs={{0,4},{4,0},{8,12},{12,8},{16,20},{20,16},{24,28},{28,24},{32,36},... | collective-permute-start | bytes 589832 | tf_op jit(solution)/shard_map/ppermute | solution.py:205
  66.7 0.7 collective-permute-start.2
  68.1 1.8 %collective-permute-start.16 = (bf16[64,768]{1,0:T(8,128)(2,1)S(1)}, bf16[64,768]{1,0:T(8,128)(2,1)S(1)}, u32[]{:S(2)}, u32[]{:S(2)}) collective-permute-start(bf16[64,768]{1,0:T(8,128)(2,1)S(1)} %fusion.19), channel_id=1, source_target_pairs={{0,16},{4,20},{8,24},{12,28},{16,0},{20,4},{24,8},{28,12},{32,48},... | collective-permute-start | bytes 294920 | tf_op jit(solution)/shard_map/ppermute | solution.py:211
  69.9 0.9 collective-permute-start.17
  70.9 0.7 collective-permute-start.3
  71.6 1.3 collective-permute-done.15
  72.9 1.5 collective-permute-done.16
  74.9 1.5 collective-permute-start.19
  76.4 1.0 collective-permute-start.20
  77.5 2.9 %collective-permute-done.18 = bf16[64,768]{1,0:T(8,128)(2,1)S(1)} collective-permute-done((bf16[64,768]{1,0:T(8,128)(2,1)S(1)}, bf16[64,768]{1,0:T(8,128)(2,1)S(1)}, u32[]{:S(2)}, u32[]{:S(2)}) %collective-permute-start.18) | collective-permute-done | bytes 98336 | tf_op jit(solution)/shard_map/ppermute | solution.py:216
  81.0 1.5 collective-permute-start.27
  82.7 5.4 %collective-permute-start.21 = (bf16[64,768]{1,0:T(8,128)(2,1)S(1)}, bf16[64,768]{1,0:T(8,128)(2,1)S(1)}, u32[]{:S(2)}, u32[]{:S(2)}) collective-permute-start(bf16[64,768]{1,0:T(8,128)(2,1)S(1)} %fusion.9), channel_id=1, source_target_pairs={{0,4},{4,0},{8,12},{12,8},{16,20},{20,16},{24,28},{28,24},{32,36},... | collective-permute-start | bytes 294920 | tf_op jit(solution)/shard_map/ppermute | solution.py:219
  88.1 1.3 collective-permute-start.4
  89.8 2.3 %collective-permute-start.29 = (bf16[128,768]{1,0:T(8,128)(2,1)S(1)}, bf16[128,768]{1,0:T(8,128)(2,1)S(1)}, u32[]{:S(2)}, u32[]{:S(2)}) collective-permute-start(bf16[128,768]{1,0:T(8,128)(2,1)S(1)} %add_convert_fusion.refs_6_), channel_id=1, source_target_pairs={{0,2},{1,3},{2,0},{3,1},{4,6},{5,7},{6,4},{7,5},{8,10},{9,11},{10,... | collective-permute-start | bytes 589832 | tf_op jit(solution)/shard_map/ppermute | solution.py:39
  92.1 1.2 collective-permute-start.30
  93.9 1.2 collective-permute-start.23
  95.1 2.4 %collective-permute-done.28.refs_7_ = bf16[128,768]{1,0:T(8,128)(2,1)S(1)} collective-permute-done((bf16[128,768]{1,0:T(8,128)(2,1)S(1)}, bf16[128,768]{1,0:T(8,128)(2,1)S(1)}, u32[]{:S(2)}, u32[]{:S(2)}) %collective-permute-start.28) | collective-permute-done | bytes 196640 | tf_op jit(solution)/shard_map/ppermute | solution.py:39
  97.5 1.5 collective-permute-start.31
  98.9 1.0 collective-permute-start.32
  100.0 6.3 %collective-permute-done.31.refs_11_ = f32[8,128]{1,0:T(8,128)S(1)} collective-permute-done((f32[8,128]{1,0:T(8,128)S(1)}, f32[8,128]{1,0:T(8,128)S(1)}, u32[]{:S(2)}, u32[]{:S(2)}) %collective-permute-start.31) | collective-permute-done | bytes 4128 | tf_op jit(solution)/shard_map/ppermute | solution.py:39
  106.2 2.8 %collective-permute-done.33.refs_13_ = f32[8,128]{1,0:T(8,128)S(1)} collective-permute-done((f32[8,128]{1,0:T(8,128)S(1)}, f32[8,128]{1,0:T(8,128)S(1)}, u32[]{:S(2)}, u32[]{:S(2)}) %collective-permute-start.33) | collective-permute-done | bytes 4128 | tf_op jit(solution)/shard_map/ppermute | solution.py:39
  109.0 14.8 %block.3 = (f32[128,768]{1,0:T(8,128)S(1)}, bf16[128,768]{1,0:T(8,128)(2,1)S(1)}, bf16[128,768]{1,0:T(8,128)(2,1)S(1)}, bf16[128,768]{1,0:T(8,128)(2,1)S(1)}, f3...) custom-call(s32[1]{0:T(128)} %bitcast.1.refs_0_, ...), custom_call_target="tpu_custom_call" | custom-call | flops 4831838208 | bytes 18874368 | tf_op jit(solution)/shard_map/block/pallas_call | solution.py:138
  123.9 2.8 %collective-permute-start.35 = (bf16[128,768]{1,0:T(8,128)(2,1)S(1)}, bf16[128,768]{1,0:T(8,128)(2,1)S(1)}, u32[]{:S(2)}, u32[]{:S(2)}) collective-permute-start(bf16[128,768]{1,0:T(8,128)(2,1)S(1)} %get-tuple-element.31), channel_id=1, source_target_pairs={{0,2},{1,3},{2,0},{3,1},{4,6},{5,7},{6,4},{7,5},{8,10},{9,11},{10,... | collective-permute-start | bytes 589832 | tf_op jit(solution)/shard_map/ppermute | solution.py:45
  126.7 2.9 %collective-permute-done.34 = bf16[128,768]{1,0:T(8,128)(2,1)S(1)} collective-permute-done((bf16[128,768]{1,0:T(8,128)(2,1)S(1)}, bf16[128,768]{1,0:T(8,128)(2,1)S(1)}, u32[]{:S(2)}, u32[]{:S(2)}) %collective-permute-start.34) | collective-permute-done | bytes 196640 | tf_op jit(solution)/shard_map/ppermute | solution.py:45
  129.6 2.2 %collective-permute-done.35 = bf16[128,768]{1,0:T(8,128)(2,1)S(1)} collective-permute-done((bf16[128,768]{1,0:T(8,128)(2,1)S(1)}, bf16[128,768]{1,0:T(8,128)(2,1)S(1)}, u32[]{:S(2)}, u32[]{:S(2)}) %collective-permute-start.35) | collective-permute-done | bytes 196640 | tf_op jit(solution)/shard_map/ppermute | solution.py:45
  132.4 7.7 %collective-permute-start.37 = (bf16[128,768]{1,0:T(8,128)(2,1)S(1)}, bf16[128,768]{1,0:T(8,128)(2,1)S(1)}, u32[]{:S(2)}, u32[]{:S(2)}) collective-permute-start(bf16[128,768]{1,0:T(8,128)(2,1)S(1)} %fusion.20), channel_id=1, source_target_pairs={{0,4},{4,0},{8,12},{12,8},{16,20},{20,16},{24,28},{28,24},{32,36},... | collective-permute-start | bytes 589832 | tf_op jit(solution)/shard_map/ppermute | solution.py:205
  140.1 1.1 collective-permute-done.37
  141.2 1.3 collective-permute-start.38
  142.6 3.2 %collective-permute-start.39 = (bf16[64,768]{1,0:T(8,128)(2,1)S(1)}, bf16[64,768]{1,0:T(8,128)(2,1)S(1)}, u32[]{:S(2)}, u32[]{:S(2)}) collective-permute-start(bf16[64,768]{1,0:T(8,128)(2,1)S(1)} %fusion.18), channel_id=1, source_target_pairs={{0,16},{4,20},{8,24},{12,28},{16,0},{20,4},{24,8},{28,12},{32,48},... | collective-permute-start | bytes 294920 | tf_op jit(solution)/shard_map/ppermute | solution.py:211
  145.8 0.7 collective-permute-start.40
  146.5 0.9 collective-permute-done.38
  147.5 3.0 %collective-permute-done.39 = bf16[64,768]{1,0:T(8,128)(2,1)S(1)} collective-permute-done((bf16[64,768]{1,0:T(8,128)(2,1)S(1)}, bf16[64,768]{1,0:T(8,128)(2,1)S(1)}, u32[]{:S(2)}, u32[]{:S(2)}) %collective-permute-start.39) | collective-permute-done | bytes 98336 | tf_op jit(solution)/shard_map/ppermute | solution.py:211
  150.5 1.0 collective-permute-start.41
  151.5 0.8 collective-permute-start.42
  152.3 1.7 collective-permute-start.43
  154.0 1.3 collective-permute-done.41
  155.3 1.5 collective-permute-done.42
  157.4 2.5 %collective-permute-start.44 = (bf16[64,768]{1,0:T(8,128)(2,1)S(1)}, bf16[64,768]{1,0:T(8,128)(2,1)S(1)}, u32[]{:S(2)}, u32[]{:S(2)}) collective-permute-start(bf16[64,768]{1,0:T(8,128)(2,1)S(1)} %fusion.16), channel_id=1, source_target_pairs={{0,4},{4,0},{8,12},{12,8},{16,20},{20,16},{24,28},{28,24},{32,36},... | collective-permute-start | bytes 294920 | tf_op jit(solution)/shard_map/ppermute | solution.py:219
  159.9 3.3 %collective-permute-start.46 = (bf16[128,768]{1,0:T(8,128)(2,1)S(1)}, bf16[128,768]{1,0:T(8,128)(2,1)S(1)}, u32[]{:S(2)}, u32[]{:S(2)}) collective-permute-start(bf16[128,768]{1,0:T(8,128)(2,1)S(1)} %get-tuple-element.35), channel_id=1, source_target_pairs={{0,2},{1,3},{2,0},{3,1},{4,6},{5,7},{6,4},{7,5},{8,10},{9,11},{10,... | collective-permute-start | bytes 589832 | tf_op jit(solution)/shard_map/ppermute | solution.py:45
  163.2 4.4 %collective-permute-done.45 = bf16[128,768]{1,0:T(8,128)(2,1)S(1)} collective-permute-done((bf16[128,768]{1,0:T(8,128)(2,1)S(1)}, bf16[128,768]{1,0:T(8,128)(2,1)S(1)}, u32[]{:S(2)}, u32[]{:S(2)}) %collective-permute-start.45) | collective-permute-done | bytes 196640 | tf_op jit(solution)/shard_map/ppermute | solution.py:45
  167.6 4.8 %collective-permute-done.46 = bf16[128,768]{1,0:T(8,128)(2,1)S(1)} collective-permute-done((bf16[128,768]{1,0:T(8,128)(2,1)S(1)}, bf16[128,768]{1,0:T(8,128)(2,1)S(1)}, u32[]{:S(2)}, u32[]{:S(2)}) %collective-permute-start.46) | collective-permute-done | bytes 196640 | tf_op jit(solution)/shard_map/ppermute | solution.py:45
  172.6 0.9 pad_maximum_fusion
  (82 shorter events, 8.6 us)
Async XLA Ops:
  0.0 1.4 copy-start
  0.0 7.4 %copy-start.1 = (s32[2]{0:T(128)S(1)}, s32[2]{0:T(128)}, u32[]{:S(2)}) copy-start(s32[2]{0:T(128)} %param.8) | copy-start | bytes 28
  1.5 36.8 %collective-permute-start.5 = (bf16[256,768]{1,0:T(8,128)(2,1)S(1)}, bf16[256,768]{1,0:T(8,128)(2,1)S(1)}, u32[]{:S(2)}, u32[]{:S(2)}) collective-permute-start(bf16[256,768]{1,0:T(8,128)(2,1)S(1)} %bitcast.31), channel_id=1, source_target_pairs={{0,1},{1,2},{2,3},{3,0},{4,5},{5,6},{6,7},{7,4},{8,9},{9,10},{10,1... | collective-permute-start | bytes 1179656 | tf_op jit(solution)/shard_map/ppermute | solution.py:39
  3.7 34.6 %collective-permute-start.6 = (bf16[256,768]{1,0:T(8,128)(2,1)S(1)}, bf16[256,768]{1,0:T(8,128)(2,1)S(1)}, u32[]{:S(2)}, u32[]{:S(2)}) collective-permute-start(bf16[256,768]{1,0:T(8,128)(2,1)S(1)} %bitcast.32), channel_id=1, source_target_pairs={{0,2},{1,3},{2,0},{3,1},{4,6},{5,7},{6,4},{7,5},{8,10},{9,11},{10,... | collective-permute-start | bytes 1179656 | tf_op jit(solution)/shard_map/ppermute | solution.py:39
  6.3 32.0 %collective-permute-start.7 = (bf16[256,768]{1,0:T(8,128)(2,1)S(1)}, bf16[256,768]{1,0:T(8,128)(2,1)S(1)}, u32[]{:S(2)}, u32[]{:S(2)}) collective-permute-start(bf16[256,768]{1,0:T(8,128)(2,1)S(1)} %bitcast.33), channel_id=1, source_target_pairs={{0,3},{1,0},{2,1},{3,2},{4,7},{5,4},{6,5},{7,6},{8,11},{9,8},{10,9... | collective-permute-start | bytes 1179656 | tf_op jit(solution)/shard_map/ppermute | solution.py:39
  9.2 16.3 %all-to-all-start = ((s32[32,1,128]{2,1,0:T(1,128)}), s32[32,1,128]{2,1,0:T(1,128)S(1)}, u32[]{:S(2)}, u32[]{:S(2)}) async-start(s32[32,1,128]{2,1,0:T(1,128)} %broadcast_in_dim.46), calls=%async_computation | async-start | bytes 32768 | tf_op jit(solution)/shard_map/all_to_all | solution.py:174
  31.4 2.7 %collective-permute-start.10 = (f32[8,768]{1,0:T(8,128)S(1)}, f32[8,768]{1,0:T(8,128)S(1)}, u32[]{:S(2)}, u32[]{:S(2)}) collective-permute-start(f32[8,768]{1,0:T(8,128)S(1)} %select_maximum_fusion.refs_6_.refs_14_), channel_id=1, source_target_pairs={{0,3},{1,0},{2,1},{3,2},{4,7},{5,4},{6,5},{7,6},{8,11},{9,8},{10,9... | collective-permute-start | bytes 73736 | tf_op jit(solution)/shard_map/ppermute | solution.py:39
  32.2 3.9 %collective-permute-start.8 = (f32[8,768]{1,0:T(8,128)S(1)}, f32[8,768]{1,0:T(8,128)S(1)}, u32[]{:S(2)}, u32[]{:S(2)}) collective-permute-start(f32[8,768]{1,0:T(8,128)S(1)} %select_maximum_fusion.refs_6_.refs_14_), channel_id=1, source_target_pairs={{0,1},{1,2},{2,3},{3,0},{4,5},{5,6},{6,7},{7,4},{8,9},{9,10},{10,1... | collective-permute-start | bytes 73736 | tf_op jit(solution)/shard_map/ppermute | solution.py:39
  34.1 4.2 %collective-permute-start.9 = (f32[8,768]{1,0:T(8,128)S(1)}, f32[8,768]{1,0:T(8,128)S(1)}, u32[]{:S(2)}, u32[]{:S(2)}) collective-permute-start(f32[8,768]{1,0:T(8,128)S(1)} %select_maximum_fusion.refs_6_.refs_14_), channel_id=1, source_target_pairs={{0,2},{1,3},{2,0},{3,1},{4,6},{5,7},{6,4},{7,5},{8,10},{9,11},{10,... | collective-permute-start | bytes 73736 | tf_op jit(solution)/shard_map/ppermute | solution.py:39
  36.1 19.8 %collective-permute-start = (f32[128,768]{1,0:T(8,128)}, f32[128,768]{1,0:T(8,128)S(1)}, u32[]{:S(2)}, u32[]{:S(2)}) collective-permute-start(f32[128,768]{1,0:T(8,128)} %select_bitcast_fusion), channel_id=1, source_target_pairs={{0,32},{1,33},{2,34},{3,35}} | collective-permute-start | bytes 1179656 | tf_op jit(solution)/shard_map/ppermute | solution.py:195
  53.0 7.1 %collective-permute-start.11 = (bf16[128,768]{1,0:T(8,128)(2,1)S(1)}, bf16[128,768]{1,0:T(8,128)(2,1)S(1)}, u32[]{:S(2)}, u32[]{:S(2)}) collective-permute-start(bf16[128,768]{1,0:T(8,128)(2,1)S(1)} %get-tuple-element.22), channel_id=1, source_target_pairs={{0,1},{1,2},{2,3},{3,0},{4,5},{5,6},{6,7},{7,4},{8,9},{9,10},{10,1... | collective-permute-start | bytes 589832 | tf_op jit(solution)/shard_map/ppermute | solution.py:45
  53.4 8.3 %collective-permute-start.12 = (bf16[128,768]{1,0:T(8,128)(2,1)S(1)}, bf16[128,768]{1,0:T(8,128)(2,1)S(1)}, u32[]{:S(2)}, u32[]{:S(2)}) collective-permute-start(bf16[128,768]{1,0:T(8,128)(2,1)S(1)} %get-tuple-element.23), channel_id=1, source_target_pairs={{0,2},{1,3},{2,0},{3,1},{4,6},{5,7},{6,4},{7,5},{8,10},{9,11},{10,... | collective-permute-start | bytes 589832 | tf_op jit(solution)/shard_map/ppermute | solution.py:45
  55.5 6.9 %collective-permute-start.13 = (bf16[128,768]{1,0:T(8,128)(2,1)S(1)}, bf16[128,768]{1,0:T(8,128)(2,1)S(1)}, u32[]{:S(2)}, u32[]{:S(2)}) collective-permute-start(bf16[128,768]{1,0:T(8,128)(2,1)S(1)} %get-tuple-element.24), channel_id=1, source_target_pairs={{0,3},{1,0},{2,1},{3,2},{4,7},{5,4},{6,5},{7,6},{8,11},{9,8},{10,9... | collective-permute-start | bytes 589832 | tf_op jit(solution)/shard_map/ppermute | solution.py:45
  56.0 10.7 %collective-permute-start.1 = (f32[128,768]{1,0:T(8,128)S(1)}, f32[128,768]{1,0:T(8,128)S(1)}, u32[]{:S(2)}, u32[]{:S(2)}) collective-permute-start(f32[128,768]{1,0:T(8,128)S(1)} %fusion.29), channel_id=1, source_target_pairs={{0,96},{32,64},{1,97},{33,65},{2,98},{34,66},{3,99},{35,67}} | collective-permute-start | bytes 1179656 | tf_op jit(solution)/shard_map/ppermute | solution.py:195
  62.4 5.3 %collective-permute-start.14 = (bf16[128,768]{1,0:T(8,128)(2,1)S(1)}, bf16[128,768]{1,0:T(8,128)(2,1)S(1)}, u32[]{:S(2)}, u32[]{:S(2)}) collective-permute-start(bf16[128,768]{1,0:T(8,128)(2,1)S(1)} %add_convert_fusion.1), channel_id=1, source_target_pairs={{0,4},{4,0},{8,12},{12,8},{16,20},{20,16},{24,28},{28,24},{32,36},... | collective-permute-start | bytes 589832 | tf_op jit(solution)/shard_map/ppermute | solution.py:205
  66.7 4.1 %collective-permute-start.2 = (f32[128,768]{1,0:T(8,128)S(1)}, f32[128,768]{1,0:T(8,128)S(1)}, u32[]{:S(2)}, u32[]{:S(2)}) collective-permute-start(f32[128,768]{1,0:T(8,128)S(1)} %add.148), channel_id=1, source_target_pairs={{0,8},{32,40},{64,72},{96,104},{1,9},{33,41},{65,73},{97,105},{2,1... | collective-permute-start | bytes 1179656 | tf_op jit(solution)/shard_map/ppermute | solution.py:195
  67.8 5.1 %collective-permute-start.15 = (bf16[64,768]{1,0:T(8,128)(2,1)S(1)}, bf16[64,768]{1,0:T(8,128)(2,1)S(1)}, u32[]{:S(2)}, u32[]{:S(2)}) collective-permute-start(bf16[64,768]{1,0:T(8,128)(2,1)S(1)} %fusion.19), channel_id=1, source_target_pairs={{0,8},{4,12},{8,16},{12,20},{16,24},{20,28},{24,0},{28,4},{32,40},... | collective-permute-start | bytes 294920 | tf_op jit(solution)/shard_map/ppermute | solution.py:211
  68.1 6.3 %collective-permute-start.16 = (bf16[64,768]{1,0:T(8,128)(2,1)S(1)}, bf16[64,768]{1,0:T(8,128)(2,1)S(1)}, u32[]{:S(2)}, u32[]{:S(2)}) collective-permute-start(bf16[64,768]{1,0:T(8,128)(2,1)S(1)} %fusion.19), channel_id=1, source_target_pairs={{0,16},{4,20},{8,24},{12,28},{16,0},{20,4},{24,8},{28,12},{32,48},... | collective-permute-start | bytes 294920 | tf_op jit(solution)/shard_map/ppermute | solution.py:211
  69.9 4.6 %collective-permute-start.17 = (bf16[64,768]{1,0:T(8,128)(2,1)S(1)}, bf16[64,768]{1,0:T(8,128)(2,1)S(1)}, u32[]{:S(2)}, u32[]{:S(2)}) collective-permute-start(bf16[64,768]{1,0:T(8,128)(2,1)S(1)} %fusion.19), channel_id=1, source_target_pairs={{0,24},{4,28},{8,0},{12,4},{16,8},{20,12},{24,16},{28,20},{32,56},... | collective-permute-start | bytes 294920 | tf_op jit(solution)/shard_map/ppermute | solution.py:211
  70.9 17.2 %collective-permute-start.3 = (f32[128,768]{1,0:T(8,128)S(1)}, f32[128,768]{1,0:T(8,128)S(1)}, u32[]{:S(2)}, u32[]{:S(2)}) collective-permute-start(f32[128,768]{1,0:T(8,128)S(1)} %add.149), channel_id=1, source_target_pairs={{0,24},{8,16},{32,56},{40,48},{64,88},{72,80},{96,120},{104,112},{... | collective-permute-start | bytes 1179656 | tf_op jit(solution)/shard_map/ppermute | solution.py:195
  74.6 5.8 %collective-permute-start.18 = (bf16[64,768]{1,0:T(8,128)(2,1)S(1)}, bf16[64,768]{1,0:T(8,128)(2,1)S(1)}, u32[]{:S(2)}, u32[]{:S(2)}) collective-permute-start(bf16[64,768]{1,0:T(8,128)(2,1)S(1)} %fusion.10), channel_id=1, source_target_pairs={{0,32},{4,36},{8,40},{12,44},{16,48},{20,52},{24,56},{28,60},{32,6... | collective-permute-start | bytes 294920 | tf_op jit(solution)/shard_map/ppermute | solution.py:216
  74.9 6.1 %collective-permute-start.19 = (bf16[64,768]{1,0:T(8,128)(2,1)S(1)}, bf16[64,768]{1,0:T(8,128)(2,1)S(1)}, u32[]{:S(2)}, u32[]{:S(2)}) collective-permute-start(bf16[64,768]{1,0:T(8,128)(2,1)S(1)} %fusion.10), channel_id=1, source_target_pairs={{0,64},{4,68},{8,72},{12,76},{16,80},{20,84},{24,88},{28,92},{32,9... | collective-permute-start | bytes 294920 | tf_op jit(solution)/shard_map/ppermute | solution.py:216
  76.4 6.2 %collective-permute-start.20 = (bf16[64,768]{1,0:T(8,128)(2,1)S(1)}, bf16[64,768]{1,0:T(8,128)(2,1)S(1)}, u32[]{:S(2)}, u32[]{:S(2)}) collective-permute-start(bf16[64,768]{1,0:T(8,128)(2,1)S(1)} %fusion.10), channel_id=1, source_target_pairs={{0,96},{4,100},{8,104},{12,108},{16,112},{20,116},{24,120},{28,124... | collective-permute-start | bytes 294920 | tf_op jit(solution)/shard_map/ppermute | solution.py:216
  77.4 12.0 %collective-permute-start.25 = (bf16[128,768]{1,0:T(8,128)(2,1)S(1)}, bf16[128,768]{1,0:T(8,128)(2,1)S(1)}, u32[]{:S(2)}, u32[]{:S(2)}) collective-permute-start(bf16[128,768]{1,0:T(8,128)(2,1)S(1)} %get-tuple-element.26), channel_id=1, source_target_pairs={{0,1},{1,2},{2,3},{3,0},{4,5},{5,6},{6,7},{7,4},{8,9},{9,10},{10,1... | collective-permute-start | bytes 589832 | tf_op jit(solution)/shard_map/ppermute | solution.py:45
  80.4 9.0 %collective-permute-start.26 = (bf16[128,768]{1,0:T(8,128)(2,1)S(1)}, bf16[128,768]{1,0:T(8,128)(2,1)S(1)}, u32[]{:S(2)}, u32[]{:S(2)}) collective-permute-start(bf16[128,768]{1,0:T(8,128)(2,1)S(1)} %get-tuple-element.27), channel_id=1, source_target_pairs={{0,2},{1,3},{2,0},{3,1},{4,6},{5,7},{6,4},{7,5},{8,10},{9,11},{10,... | collective-permute-start | bytes 589832 | tf_op jit(solution)/shard_map/ppermute | solution.py:45
  81.0 8.4 %collective-permute-start.27 = (bf16[128,768]{1,0:T(8,128)(2,1)S(1)}, bf16[128,768]{1,0:T(8,128)(2,1)S(1)}, u32[]{:S(2)}, u32[]{:S(2)}) collective-permute-start(bf16[128,768]{1,0:T(8,128)(2,1)S(1)} %get-tuple-element.28), channel_id=1, source_target_pairs={{0,3},{1,0},{2,1},{3,2},{4,7},{5,4},{6,5},{7,6},{8,11},{9,8},{10,9... | collective-permute-start | bytes 589832 | tf_op jit(solution)/shard_map/ppermute | solution.py:45
  82.7 10.7 %collective-permute-start.21 = (bf16[64,768]{1,0:T(8,128)(2,1)S(1)}, bf16[64,768]{1,0:T(8,128)(2,1)S(1)}, u32[]{:S(2)}, u32[]{:S(2)}) collective-permute-start(bf16[64,768]{1,0:T(8,128)(2,1)S(1)} %fusion.9), channel_id=1, source_target_pairs={{0,4},{4,0},{8,12},{12,8},{16,20},{20,16},{24,28},{28,24},{32,36},... | collective-permute-start | bytes 294920 | tf_op jit(solution)/shard_map/ppermute | solution.py:219
  88.1 5.2 %collective-permute-start.4 = (f32[128,768]{1,0:T(8,128)S(1)}, f32[128,768]{1,0:T(8,128)S(1)}, u32[]{:S(2)}, u32[]{:S(2)}) collective-permute-start(f32[128,768]{1,0:T(8,128)S(1)} %add.150), channel_id=1, source_target_pairs={{0,4},{8,12},{16,20},{24,28},{32,36},{40,44},{48,52},{56,60},{64,6... | collective-permute-start | bytes 1179656 | tf_op jit(solution)/shard_map/ppermute | solution.py:195
  89.6 7.9 %collective-permute-start.28 = (bf16[128,768]{1,0:T(8,128)(2,1)S(1)}, bf16[128,768]{1,0:T(8,128)(2,1)S(1)}, u32[]{:S(2)}, u32[]{:S(2)}) collective-permute-start(bf16[128,768]{1,0:T(8,128)(2,1)S(1)} %add_convert_fusion.refs_6_), channel_id=1, source_target_pairs={{0,1},{1,2},{2,3},{3,0},{4,5},{5,6},{6,7},{7,4},{8,9},{9,10},{10,1... | collective-permute-start | bytes 589832 | tf_op jit(solution)/shard_map/ppermute | solution.py:39
  89.8 7.7 %collective-permute-start.29 = (bf16[128,768]{1,0:T(8,128)(2,1)S(1)}, bf16[128,768]{1,0:T(8,128)(2,1)S(1)}, u32[]{:S(2)}, u32[]{:S(2)}) collective-permute-start(bf16[128,768]{1,0:T(8,128)(2,1)S(1)} %add_convert_fusion.refs_6_), channel_id=1, source_target_pairs={{0,2},{1,3},{2,0},{3,1},{4,6},{5,7},{6,4},{7,5},{8,10},{9,11},{10,... | collective-permute-start | bytes 589832 | tf_op jit(solution)/shard_map/ppermute | solution.py:39
  92.1 6.8 %collective-permute-start.30 = (bf16[128,768]{1,0:T(8,128)(2,1)S(1)}, bf16[128,768]{1,0:T(8,128)(2,1)S(1)}, u32[]{:S(2)}, u32[]{:S(2)}) collective-permute-start(bf16[128,768]{1,0:T(8,128)(2,1)S(1)} %add_convert_fusion.refs_6_), channel_id=1, source_target_pairs={{0,3},{1,0},{2,1},{3,2},{4,7},{5,4},{6,5},{7,6},{8,11},{9,8},{10,9... | collective-permute-start | bytes 589832 | tf_op jit(solution)/shard_map/ppermute | solution.py:39
  93.6 15.4 %collective-permute-start.22 = (bf16[128,768]{1,0:T(8,128)(2,1)S(1)}, bf16[128,768]{1,0:T(8,128)(2,1)S(1)}, u32[]{:S(2)}, u32[]{:S(2)}) collective-permute-start(bf16[128,768]{1,0:T(8,128)(2,1)S(1)} %fusion.2.refs_2_), channel_id=1, source_target_pairs={{0,1},{1,2},{2,3},{3,0},{4,5},{5,6},{6,7},{7,4},{8,9},{9,10},{10,1... | collective-permute-start | bytes 589832 | tf_op jit(solution)/shard_map/ppermute | solution.py:39
  93.9 15.1 %collective-permute-start.23 = (bf16[128,768]{1,0:T(8,128)(2,1)S(1)}, bf16[128,768]{1,0:T(8,128)(2,1)S(1)}, u32[]{:S(2)}, u32[]{:S(2)}) collective-permute-start(bf16[128,768]{1,0:T(8,128)(2,1)S(1)} %fusion.2.refs_2_), channel_id=1, source_target_pairs={{0,2},{1,3},{2,0},{3,1},{4,6},{5,7},{6,4},{7,5},{8,10},{9,11},{10,... | collective-permute-start | bytes 589832 | tf_op jit(solution)/shard_map/ppermute | solution.py:39
  97.5 11.5 %collective-permute-start.24 = (bf16[128,768]{1,0:T(8,128)(2,1)S(1)}, bf16[128,768]{1,0:T(8,128)(2,1)S(1)}, u32[]{:S(2)}, u32[]{:S(2)}) collective-permute-start(bf16[128,768]{1,0:T(8,128)(2,1)S(1)} %fusion.2.refs_2_), channel_id=1, source_target_pairs={{0,3},{1,0},{2,1},{3,2},{4,7},{5,4},{6,5},{7,6},{8,11},{9,8},{10,9... | collective-permute-start | bytes 589832 | tf_op jit(solution)/shard_map/ppermute | solution.py:39
  97.5 8.8 %collective-permute-start.31 = (f32[8,128]{1,0:T(8,128)S(1)}, f32[8,128]{1,0:T(8,128)S(1)}, u32[]{:S(2)}, u32[]{:S(2)}) collective-permute-start(f32[8,128]{1,0:T(8,128)S(1)} %broadcast_in_dim.50.refs_10_), channel_id=1, source_target_pairs={{0,1},{1,2},{2,3},{3,0},{4,5},{5,6},{6,7},{7,4},{8,9},{9,10},{10,1... | collective-permute-start | bytes 12296 | tf_op jit(solution)/shard_map/ppermute | solution.py:39
  98.9 7.3 %collective-permute-start.32 = (f32[8,128]{1,0:T(8,128)S(1)}, f32[8,128]{1,0:T(8,128)S(1)}, u32[]{:S(2)}, u32[]{:S(2)}) collective-permute-start(f32[8,128]{1,0:T(8,128)S(1)} %broadcast_in_dim.50.refs_10_), channel_id=1, source_target_pairs={{0,2},{1,3},{2,0},{3,1},{4,6},{5,7},{6,4},{7,5},{8,10},{9,11},{10,... | collective-permute-start | bytes 12296 | tf_op jit(solution)/shard_map/ppermute | solution.py:39
  106.2 2.8 %collective-permute-start.33 = (f32[8,128]{1,0:T(8,128)S(1)}, f32[8,128]{1,0:T(8,128)S(1)}, u32[]{:S(2)}, u32[]{:S(2)}) collective-permute-start(f32[8,128]{1,0:T(8,128)S(1)} %broadcast_in_dim.50.refs_10_), channel_id=1, source_target_pairs={{0,3},{1,0},{2,1},{3,2},{4,7},{5,4},{6,5},{7,6},{8,11},{9,8},{10,9... | collective-permute-start | bytes 12296 | tf_op jit(solution)/shard_map/ppermute | solution.py:39
  123.8 5.8 %collective-permute-start.34 = (bf16[128,768]{1,0:T(8,128)(2,1)S(1)}, bf16[128,768]{1,0:T(8,128)(2,1)S(1)}, u32[]{:S(2)}, u32[]{:S(2)}) collective-permute-start(bf16[128,768]{1,0:T(8,128)(2,1)S(1)} %get-tuple-element.30), channel_id=1, source_target_pairs={{0,1},{1,2},{2,3},{3,0},{4,5},{5,6},{6,7},{7,4},{8,9},{9,10},{10,1... | collective-permute-start | bytes 589832 | tf_op jit(solution)/shard_map/ppermute | solution.py:45
  123.9 7.9 %collective-permute-start.35 = (bf16[128,768]{1,0:T(8,128)(2,1)S(1)}, bf16[128,768]{1,0:T(8,128)(2,1)S(1)}, u32[]{:S(2)}, u32[]{:S(2)}) collective-permute-start(bf16[128,768]{1,0:T(8,128)(2,1)S(1)} %get-tuple-element.31), channel_id=1, source_target_pairs={{0,2},{1,3},{2,0},{3,1},{4,6},{5,7},{6,4},{7,5},{8,10},{9,11},{10,... | collective-permute-start | bytes 589832 | tf_op jit(solution)/shard_map/ppermute | solution.py:45
  126.6 5.7 %collective-permute-start.36 = (bf16[128,768]{1,0:T(8,128)(2,1)S(1)}, bf16[128,768]{1,0:T(8,128)(2,1)S(1)}, u32[]{:S(2)}, u32[]{:S(2)}) collective-permute-start(bf16[128,768]{1,0:T(8,128)(2,1)S(1)} %get-tuple-element.32), channel_id=1, source_target_pairs={{0,3},{1,0},{2,1},{3,2},{4,7},{5,4},{6,5},{7,6},{8,11},{9,8},{10,9... | collective-permute-start | bytes 589832 | tf_op jit(solution)/shard_map/ppermute | solution.py:45
  132.4 8.7 %collective-permute-start.37 = (bf16[128,768]{1,0:T(8,128)(2,1)S(1)}, bf16[128,768]{1,0:T(8,128)(2,1)S(1)}, u32[]{:S(2)}, u32[]{:S(2)}) collective-permute-start(bf16[128,768]{1,0:T(8,128)(2,1)S(1)} %fusion.20), channel_id=1, source_target_pairs={{0,4},{4,0},{8,12},{12,8},{16,20},{20,16},{24,28},{28,24},{32,36},... | collective-permute-start | bytes 589832 | tf_op jit(solution)/shard_map/ppermute | solution.py:205
  141.2 6.2 %collective-permute-start.38 = (bf16[64,768]{1,0:T(8,128)(2,1)S(1)}, bf16[64,768]{1,0:T(8,128)(2,1)S(1)}, u32[]{:S(2)}, u32[]{:S(2)}) collective-permute-start(bf16[64,768]{1,0:T(8,128)(2,1)S(1)} %fusion.18), channel_id=1, source_target_pairs={{0,8},{4,12},{8,16},{12,20},{16,24},{20,28},{24,0},{28,4},{32,40},... | collective-permute-start | bytes 294920 | tf_op jit(solution)/shard_map/ppermute | solution.py:211
  142.6 7.9 %collective-permute-start.39 = (bf16[64,768]{1,0:T(8,128)(2,1)S(1)}, bf16[64,768]{1,0:T(8,128)(2,1)S(1)}, u32[]{:S(2)}, u32[]{:S(2)}) collective-permute-start(bf16[64,768]{1,0:T(8,128)(2,1)S(1)} %fusion.18), channel_id=1, source_target_pairs={{0,16},{4,20},{8,24},{12,28},{16,0},{20,4},{24,8},{28,12},{32,48},... | collective-permute-start | bytes 294920 | tf_op jit(solution)/shard_map/ppermute | solution.py:211
  145.8 4.7 %collective-permute-start.40 = (bf16[64,768]{1,0:T(8,128)(2,1)S(1)}, bf16[64,768]{1,0:T(8,128)(2,1)S(1)}, u32[]{:S(2)}, u32[]{:S(2)}) collective-permute-start(bf16[64,768]{1,0:T(8,128)(2,1)S(1)} %fusion.18), channel_id=1, source_target_pairs={{0,24},{4,28},{8,0},{12,4},{16,8},{20,12},{24,16},{28,20},{32,56},... | collective-permute-start | bytes 294920 | tf_op jit(solution)/shard_map/ppermute | solution.py:211
  150.5 4.7 %collective-permute-start.41 = (bf16[64,768]{1,0:T(8,128)(2,1)S(1)}, bf16[64,768]{1,0:T(8,128)(2,1)S(1)}, u32[]{:S(2)}, u32[]{:S(2)}) collective-permute-start(bf16[64,768]{1,0:T(8,128)(2,1)S(1)} %fusion.17), channel_id=1, source_target_pairs={{0,32},{4,36},{8,40},{12,44},{16,48},{20,52},{24,56},{28,60},{32,6... | collective-permute-start | bytes 294920 | tf_op jit(solution)/shard_map/ppermute | solution.py:216
  151.5 5.2 %collective-permute-start.42 = (bf16[64,768]{1,0:T(8,128)(2,1)S(1)}, bf16[64,768]{1,0:T(8,128)(2,1)S(1)}, u32[]{:S(2)}, u32[]{:S(2)}) collective-permute-start(bf16[64,768]{1,0:T(8,128)(2,1)S(1)} %fusion.17), channel_id=1, source_target_pairs={{0,64},{4,68},{8,72},{12,76},{16,80},{20,84},{24,88},{28,92},{32,9... | collective-permute-start | bytes 294920 | tf_op jit(solution)/shard_map/ppermute | solution.py:216
  152.3 5.0 %collective-permute-start.43 = (bf16[64,768]{1,0:T(8,128)(2,1)S(1)}, bf16[64,768]{1,0:T(8,128)(2,1)S(1)}, u32[]{:S(2)}, u32[]{:S(2)}) collective-permute-start(bf16[64,768]{1,0:T(8,128)(2,1)S(1)} %fusion.17), channel_id=1, source_target_pairs={{0,96},{4,100},{8,104},{12,108},{16,112},{20,116},{24,120},{28,124... | collective-permute-start | bytes 294920 | tf_op jit(solution)/shard_map/ppermute | solution.py:216
  157.4 5.7 %collective-permute-start.44 = (bf16[64,768]{1,0:T(8,128)(2,1)S(1)}, bf16[64,768]{1,0:T(8,128)(2,1)S(1)}, u32[]{:S(2)}, u32[]{:S(2)}) collective-permute-start(bf16[64,768]{1,0:T(8,128)(2,1)S(1)} %fusion.16), channel_id=1, source_target_pairs={{0,4},{4,0},{8,12},{12,8},{16,20},{20,16},{24,28},{28,24},{32,36},... | collective-permute-start | bytes 294920 | tf_op jit(solution)/shard_map/ppermute | solution.py:219
  159.9 7.7 %collective-permute-start.45 = (bf16[128,768]{1,0:T(8,128)(2,1)S(1)}, bf16[128,768]{1,0:T(8,128)(2,1)S(1)}, u32[]{:S(2)}, u32[]{:S(2)}) collective-permute-start(bf16[128,768]{1,0:T(8,128)(2,1)S(1)} %get-tuple-element.34), channel_id=1, source_target_pairs={{0,1},{1,2},{2,3},{3,0},{4,5},{5,6},{6,7},{7,4},{8,9},{9,10},{10,1... | collective-permute-start | bytes 589832 | tf_op jit(solution)/shard_map/ppermute | solution.py:45
  159.9 12.5 %collective-permute-start.46 = (bf16[128,768]{1,0:T(8,128)(2,1)S(1)}, bf16[128,768]{1,0:T(8,128)(2,1)S(1)}, u32[]{:S(2)}, u32[]{:S(2)}) collective-permute-start(bf16[128,768]{1,0:T(8,128)(2,1)S(1)} %get-tuple-element.35), channel_id=1, source_target_pairs={{0,2},{1,3},{2,0},{3,1},{4,6},{5,7},{6,4},{7,5},{8,10},{9,11},{10,... | collective-permute-start | bytes 589832 | tf_op jit(solution)/shard_map/ppermute | solution.py:45
  163.1 9.2 %collective-permute-start.47 = (bf16[128,768]{1,0:T(8,128)(2,1)S(1)}, bf16[128,768]{1,0:T(8,128)(2,1)S(1)}, u32[]{:S(2)}, u32[]{:S(2)}) collective-permute-start(bf16[128,768]{1,0:T(8,128)(2,1)S(1)} %get-tuple-element.36), channel_id=1, source_target_pairs={{0,3},{1,0},{2,1},{3,2},{4,7},{5,4},{6,5},{7,6},{8,11},{9,8},{10,9... | collective-permute-start | bytes 589832 | tf_op jit(solution)/shard_map/ppermute | solution.py:45

commit v2 on v1

v2 whole, which is shorter than its diff:
```python
import math

import jax
import jax.numpy as jnp
from jax import lax
from jax.experimental import pallas as pl
from jax.experimental.pallas import tpu as pltpu
from jax.sharding import PartitionSpec as P

HD = 128
FREQ = 256
EXTRA = 8
LIMIT = 48
CUTS = 1
LEVELS = 320
NX, NZ, NC, NY = 4, 4, 2, 4
BF = jnp.bfloat16
F32 = jnp.float32


def ring(k):
    return [(i, (i + k) % NY) for i in range(NY)]


def place(x, z, c):
    return (x * NZ + z) * NC + c


CHIPS = [(x, z, c) for x in range(NX) for z in range(NZ) for c in range(NC)]
SWAP = [(place(x, z, c), place(x, z, 1 - c)) for x, z, c in CHIPS]


def z_shift(k):
    return [(place(x, z, c), place(x, (z + k) % NZ, c)) for x, z, c in CHIPS]


def x_shift(k):
    return [(place(x, z, c), place((x + k) % NX, z, c)) for x, z, c in CHIPS]


def spread(array):
    return [array] + [lax.ppermute(array, "tp", ring(k)) for k in (1, 2, 3)]


def modulation_body(facts, all_gaps, mod_ref, out_ref):
    half_freq = FREQ // 2
    gaps = all_gaps[...]
    earlier = lax.broadcasted_iota(jnp.int32, gaps.shape, 0) < facts[0]
    before = jnp.sum(jnp.where(earlier, gaps, 0), 0)
    level = before[:, 0:1] + before[:, 1:2] + facts[2]
    lane = lax.broadcasted_iota(jnp.int32, (1, half_freq), 1).astype(F32)
    frequencies = jnp.exp(-math.log(10000.0) * lane / half_freq)
    rows = []
    for here in (level, level + facts[3]):
        angles = 1000.0 * (1.0 - here.astype(F32) / LEVELS) * frequencies
        rows.append(jnp.concatenate([jnp.cos(angles), jnp.sin(angles)], -1))
    index = lax.broadcasted_iota(jnp.int32, (8, FREQ), 0)
    embed_rows = jnp.where(index == 0, rows[0], jnp.where(index == 1, rows[1], 0.0)).astype(BF)
    out_ref[...] = jnp.zeros_like(out_ref)
    for p in range(3):
        made = jnp.dot(embed_rows, mod_ref[p], preferred_element_type=F32)
        for s in range(2):
            for y in range(NY):
                out_ref[y, 3 * s + p : 3 * s + p + 1, :] = made[s : s + 1]


def modulation(facts, all_gaps, mod_weight):
    vmem = pl.BlockSpec(memory_space=pltpu.VMEM)
    smem = pl.BlockSpec(memory_space=pltpu.SMEM)
    return pl.pallas_call(
        modulation_body,
        out_shape=jax.ShapeDtypeStruct((NY, 8, mod_weight.shape[-1]), F32),
        in_specs=[smem, vmem, vmem],
        out_specs=vmem,
        compiler_params=pltpu.CompilerParams(vmem_limit_bytes=8 * 2**20),
        name="modulation",
    )(facts, all_gaps, mod_weight)


def centre_body(x_ref, out_ref):
    rows, cols = x_ref.shape
    x = x_ref[...]
    mean = (jnp.sum(x, -1, keepdims=True) / cols).astype(BF).astype(F32)
    out_ref[:rows, :] = (x - mean).astype(BF)
    along = jnp.transpose(jnp.broadcast_to(mean, (rows, HD)))
    out_ref[rows : rows + EXTRA, :] = jnp.zeros((EXTRA, cols), BF)
    out_ref[rows : rows + EXTRA, :rows] = along[:EXTRA].astype(BF)


def centre(x):
    rows, cols = x.shape
    vmem = pl.BlockSpec(memory_space=pltpu.VMEM)
    return pl.pallas_call(
        centre_body,
        out_shape=jax.ShapeDtypeStruct((rows + EXTRA, cols), BF),
        in_specs=[vmem],
        out_specs=vmem,
        compiler_params=pltpu.CompilerParams(vmem_limit_bytes=8 * 2**20),
        name="centre",
    )(x)


def block_body(first, tok, cols, facts, *refs):
    states, refs = refs[:4], refs[4:]
    if not first:
        incs, refs = refs[:4], refs[4:]
    mods, qkv_hbm, out_hbm, refs = refs[0], refs[1], refs[2], refs[3:]
    tots, ins, (wv, wo, nrm, qkv, att, sems) = refs[:4], refs[4:8], refs[8:]
    width = NY * cols
    depth = width // CUTS
    copies = [
        pltpu.make_async_copy(qkv_hbm.at[p, pl.ds(c * depth, depth)], wv.at[p, pl.ds(c * depth, depth)], sems.at[p * CUTS + c])
        for p in range(3)
        for c in range(CUTS)
    ]
    copies.append(pltpu.make_async_copy(out_hbm, wo, sems.at[3 * CUTS]))
    for copy in copies:
        copy.start()
    me = facts[1]
    n_rows = 2 * tok if first else tok
    centres = [jnp.transpose(states[k][n_rows:, :n_rows].astype(F32))[:, 0:1] for k in range(NY)]
    for s in range(2):
        rows = pl.ds(s * tok, tok)
        parts = []
        for k in range(NY):
            if first:
                x = states[k][rows, :].astype(F32) + centres[k][s * tok : (s + 1) * tok]
            else:
                x = states[k][:tok, :].astype(F32) + centres[k]
                if s == 1:
                    x = x + incs[k][...].astype(F32)
            parts.append(x)
        mean = sum(jnp.sum(x, -1, keepdims=True) for x in parts) / width
        var = sum(jnp.sum((x - mean) * (x - mean), -1, keepdims=True) for x in parts) / width
        inv = lax.rsqrt(var + 1e-06)
        for k in range(NY):
            src = lax.rem(me + NY - k, NY)
            shift = mods[src, 3 * s : 3 * s + 1, :]
            scale = mods[src, 3 * s + 1 : 3 * s + 2, :]
            normed = (parts[k] - mean) * inv * (1.0 + scale) + shift
            at = pl.multiple_of(src * cols, cols)
            nrm[rows, pl.ds(at, cols)] = normed.astype(BF)
    for p in range(3):
        for copy in copies[p * CUTS : (p + 1) * CUTS]:
            copy.wait()
        qkv[p] = jnp.dot(nrm[...], wv[p], preferred_element_type=F32).astype(BF)
    cells = [(pl.ds(s * tok, tok), pl.ds(h * HD, HD)) for s in range(2) for h in range(cols // HD)]
    scores = [
        lax.dot_general(
            qkv[0, rows, lanes], qkv[1, rows, lanes], (((1,), (1,)), ((), ())), preferred_element_type=F32
        )
        * (1.0 / math.sqrt(HD))
        for rows, lanes in cells
    ]
    weights = [jnp.exp(x - jnp.max(x, -1, keepdims=True)) for x in scores]
    probs = [(w * (1.0 / jnp.sum(w, -1, keepdims=True))).astype(BF) for w in weights]
    for (rows, lanes), prob in zip(cells, probs, strict=True):
        att[rows, lanes] = jnp.dot(prob, qkv[2, rows, lanes], preferred_element_type=F32).astype(BF)
    copies[-1].wait()
    neg = [-(facts[3 + s].astype(F32) / LEVELS) for s in range(2)]
    for k in (1, 2, 3, 0):
        dst = lax.rem(me + k, NY)
        at = pl.multiple_of(dst * cols, cols)
        made = jnp.dot(att[...], wo[:, pl.ds(at, cols)], preferred_element_type=F32)
        inc0 = made[:tok] * (mods[dst, 2:3, :] * neg[0])
        inc1 = made[tok:] * (mods[dst, 5:6, :] * neg[1])
        tots[k][...] = (inc0 + inc1).astype(tots[k].dtype)
        ins[k][...] = inc0.astype(ins[k].dtype)


def block(first, facts, states, mods, qkv_weight, out_weight):
    cols, width = out_weight.shape
    tok = (states[0].shape[0] - EXTRA) // (2 if first else 1)

    def body(*refs):
        block_body(first, tok, cols, *refs)

    vmem = pl.BlockSpec(memory_space=pltpu.VMEM)
    smem = pl.BlockSpec(memory_space=pltpu.SMEM)
    hbm = pl.BlockSpec(memory_space=pltpu.HBM)
    outs = [jax.ShapeDtypeStruct((tok, cols), F32 if k == 0 else BF) for k in range(NY)]
    made = pl.pallas_call(
        body,
        out_shape=outs + outs,
        in_specs=[smem] + [vmem] * (len(states) + 1) + [hbm, hbm],
        out_specs=[vmem] * (2 * NY),
        scratch_shapes=[
            pltpu.VMEM(qkv_weight.shape, BF),
            pltpu.VMEM(out_weight.shape, BF),
            pltpu.VMEM((2 * tok, width), BF),
            pltpu.VMEM((3, 2 * tok, cols), BF),
            pltpu.VMEM((2 * tok, cols), BF),
            pltpu.SemaphoreType.DMA((3 * CUTS + 1,)),
        ],
        compiler_params=pltpu.CompilerParams(vmem_limit_bytes=LIMIT * 2**20),
        cost_estimate=pl.CostEstimate(
            flops=2 * 2 * tok * width * 4 * cols, bytes_accessed=8 * width * cols, transcendentals=0
        ),
        name="block",
    )(facts, *states, mods, qkv_weight, out_weight)
    return made[:NY], made[NY:]


def body(trajectory, offset, step_gaps, qkv_weight, out_weight, mod_weight):
    steps_here, tok, cols = trajectory.shape
    tm, tp = lax.axis_index("tm"), lax.axis_index("tp")
    x_at, z_at, core = tm // (NZ * NC), (tm // NC) % NZ, tm % NC
    half = tok // 2

    sent = jnp.broadcast_to(step_gaps[None, None], (NX * NZ * NC, 1, steps_here))
    trajectory, sent = lax.optimization_barrier((trajectory, sent))
    all_gaps = lax.all_to_all(sent, "tm", 0, 0)
    states = spread(centre(trajectory.reshape(steps_here * tok, cols)))
    place_of = jnp.arange(8, dtype=jnp.int32)
    facts = jnp.where(place_of == 0, tm, jnp.where(place_of == 1, tp, jnp.where(place_of == 2, offset[0], 0)))
    facts = jnp.where(place_of == 3, step_gaps[0], jnp.where(place_of == 4, step_gaps[1], facts))
    weights = (jnp.transpose(qkv_weight, (1, 0, 2)), out_weight)
    made = modulation(facts, all_gaps, jnp.transpose(mod_weight, (1, 0, 2)))
    mods = lax.all_to_all(made, "tp", 0, 0)

    def deliver(own, shares):
        total = own
        for k in (1, 2, 3):
            total = total + lax.ppermute(shares[k], "tp", ring(k)).astype(F32)
        return total

    def before_me(sent, beside_z, beside_x):
        kind = sent.dtype
        other = lax.ppermute(sent, "tm", SWAP)
        chip = sent.astype(F32) + other.astype(F32)
        mine = jnp.where(core == 0, chip[:half], chip[half:]).astype(kind)
        plane = mine.astype(F32)
        below = jnp.zeros_like(plane)
        for k in (1, 2, 3):
            came = lax.ppermute(mine, "tm", z_shift(k)).astype(F32)
            plane = plane + came
            below = below + jnp.where(z_at >= k, came, 0.0)
        plane, beside_z = lax.optimization_barrier((plane.astype(kind), beside_z))
        made = beside_x(beside_z)
        for k in (1, 2, 3):
            came = lax.ppermute(plane, "tm", x_shift(k)).astype(F32)
            below = below + jnp.where(x_at >= k, came, 0.0)
        below, made = lax.optimization_barrier((below.astype(kind), made))
        rest = lax.ppermute(below, "tm", SWAP)
        low = jnp.where(core == 0, below, rest)
        high = jnp.where(core == 0, rest, below)
        prefix = jnp.concatenate([low, high], 0).astype(F32)
        return prefix, other.astype(F32), beside_z, made

    start = jnp.where(tm == 0, trajectory[0], 0.0)
    tots, ins = block(True, facts, states, mods, *weights)
    total = deliver(tots[0], tots)
    total, ins = lax.optimization_barrier((total, ins))
    prefix, other, _, incs = before_me(total + start, deliver(ins[0], ins), lambda inc: spread(inc.astype(BF)))
    entry = prefix + jnp.where(core == 0, start, other)
    tots, ins = block(False, facts, spread(centre(entry)) + incs, mods, *weights)
    total_2 = deliver(tots[0], tots)
    total_2, ins = lax.optimization_barrier((total_2, ins))
    prefix, other, inc0, _ = before_me((total_2 - total).astype(BF), deliver(ins[0], ins), lambda inc: ())
    entry = entry + prefix + jnp.where(core == 0, 0.0, other)
    return jnp.stack([entry + inc0, entry + total_2])


def solution(mesh):
    placed = (
        P("tm", None, "tp"),
        P(),
        P("tm"),
        P(None, None, "tp"),
        P("tp", None),
        P(None, None, "tp"),
    )
    return jax.shard_map(
        body, mesh=mesh, in_specs=placed, out_specs=P("tm", None, "tp"), check_vma=False
    )
```

time: 174 us -> 159 us (0.914)
  starting transfers between devices: 74.8 us -> 56.6 us
  blocking collectives: 0 us -> 7.7 us
  Pallas kernels: 29.5 us -> 23.6 us
  waiting for transfers between devices: 56 us -> 60.5 us
  local copies, waits for them, and re-layouts: 1.97 us -> 6.42 us
  matrix products: 3.52 us -> 0 us
  other arithmetic: 6.2 us -> 3.37 us
    ppermute x33 -> x28, starting transfers between devices: 49.7 us -> 33.5 us  [the longest x12 13.3 us: deliver(): total = total + lax.ppermute(shares[k], 'tp', ring(k)).astype(F32)]
    ppermute x33 -> x28, waiting for transfers between devices: 35 us -> 46.6 us  [the longest x12 30.4 us: deliver(): total = total + lax.ppermute(shares[k], 'tp', ring(k)).astype(F32)]
    all_to_all x0 -> x1, blocking collectives: none -> 7.7 us  [body(): mods = lax.all_to_all(made, 'tp', 0, 0)]
    pallas_call x2 -> x5, Pallas kernels: 29.5 us -> 23.6 us  [the longest x2 22.2 us: block(): pl.pallas_call(body, out_shape=outs + outs, in_specs=[smem] + [vmem] * (l...]
    ppermute x15 -> x9, waiting for transfers between devices: 14.9 us -> 10.4 us  [spread(): return [array] + [lax.ppermute(array, 'tp', ring(k)) for k in (1, 2, 3)]]
    unnamed x4 -> x12, local copies, waits for them, and re-layouts: 0.04 us -> 3.79 us
    dot_general x3 -> x0, matrix products: 3.52 us -> none  [body(): jnp.dot(embedding(sigma), flat_mod[p], preferred_element_type=F32)]
    reduce_sum x4 -> x0, other arithmetic: 2.73 us -> none  [the longest x1 1.33 us: body(): means = jnp.sum(trajectory, -1) / cols]
  transfers between devices with their start and end apart: 49 -> 38, of which waited for: 26 -> 22; matrix products, arithmetic and copies ran while one was open for 5% -> 2% of each run, Pallas kernels for 8% -> 1%
where the time goes in v2:
time: 159 us
  waiting for transfers between devices  60.5 us (38%)
  starting transfers between devices  56.6 us (36%)
  Pallas kernels  23.6 us (15%)
  blocking collectives  7.7 us (5%)
  local copies, waits for them, and re-layouts  6.42 us (4%)
  other arithmetic  3.37 us (2%)
    ppermute x12, waiting for transfers between devices, deliver(): total = total + lax.ppermute(shares[k], 'tp', ring(k)).astype(F32)  30.4 us
    pallas_call x2, Pallas kernels, block(): pl.pallas_call(body, out_shape=outs + outs, in_specs=[smem] + [vmem] * (l...  22.2 us
    ppermute x9, starting transfers between devices, spread(): return [array] + [lax.ppermute(array, 'tp', ring(k)) for k in (1, 2, 3)]  13.7 us
    ppermute x12, starting transfers between devices, deliver(): total = total + lax.ppermute(shares[k], 'tp', ring(k)).astype(F32)  13.3 us
    ppermute x6, waiting for transfers between devices, before_me(): came = lax.ppermute(plane, 'tm', x_shift(k)).astype(F32)  10.4 us
    ppermute x9, waiting for transfers between devices, spread(): return [array] + [lax.ppermute(array, 'tp', ring(k)) for k in (1, 2, 3)]  10.4 us
    all_to_all x1, starting transfers between devices, body(): all_gaps = lax.all_to_all(sent, 'tm', 0, 0)  9.44 us
    all_to_all x1, blocking collectives, body(): mods = lax.all_to_all(made, 'tp', 0, 0)  7.7 us
  transfers between devices with their start and end apart: 38, of which 22 were waited for; matrix products, arithmetic and copies ran while one was open for 2% of the time, Pallas kernels for 1%

profile of v2, /device:TPU:1, one launch (start us, length us, event | category | flops | bytes accessed | tf_op | source)
XLA Modules:
  0.0 159.0 jit_solution(10498104447492385609)
XLA Ops:
  0.0 1.3 broadcast_in_dim.53
  1.3 1.1 copy-done
  2.6 3.6 %collective-permute-start.2 = (bf16[264,768]{1,0:T(8,128)(2,1)S(1)}, bf16[264,768]{1,0:T(8,128)(2,1)S(1)}, u32[]{:S(2)}, u32[]{:S(2)}) collective-permute-start(bf16[264,768]{1,0:T(8,128)(2,1)S(1)} %centre.2.refs_1_), channel_id=1, source_target_pairs={{0,3},{1,0},{2,1},{3,2},{4,7},{5,4},{6,5},{7,6},{8,11},{9,8},{10,9... | collective-permute-start | bytes 1216520 | tf_op jit(solution)/shard_map/ppermute | solution.py:42
  6.2 0.3 collective-permute-start.1
  6.5 0.7 collective-permute-start
  7.2 9.4 %all-to-all-start = ((s32[32,1,2]{2,1,0:T(1,128)}), s32[32,1,2]{2,1,0:T(1,128)S(1)}, u32[]{:S(2)}, u32[]{:S(2)}) async-start(s32[32,1,2]{2,1,0:T(1,128)} %broadcast_in_dim.53), calls=%async_computation | async-start | bytes 32768 | tf_op jit(solution)/shard_map/all_to_all | solution.py:212
  17.3 1.4 fusion.9
  18.7 1.3 compare_select_fusion.4.facts.refs_0_
  20.0 3.6 %all-to-all-done.all_gaps = s32[32,1,2]{2,1,0:T(1,128)S(1)} async-done(((s32[32,1,2]{2,1,0:T(1,128)}), s32[32,1,2]{2,1,0:T(1,128)S(1)}, u32[]{:S(2)}, u32[]{:S(2)}) %all-to-all-start) | async-done | bytes 288 | tf_op jit(solution)/shard_map/all_to_all | solution.py:212
  23.5 1.3 copy-done.2
  24.8 1.0 modulation.1
  25.8 7.7 %all_to_all.10.refs_5_.refs_9_ = f32[4,8,768]{2,1,0:T(8,128)S(1)} all-to-all(f32[4,8,768]{2,1,0:T(8,128)S(1)} %modulation.1), channel_id=1, replica_groups=mesh['tm'=32,'tp'=4] {'tp'}, dimensions={0} | all-to-all | bytes 196608 | tf_op jit(solution)/shard_map/all_to_all | solution.py:219
  33.5 11.3 %block.2 = (f32[128,768]{1,0:T(8,128)S(1)}, bf16[128,768]{1,0:T(8,128)(2,1)}, bf16[128,768]{1,0:T(8,128)(2,1)}, bf16[128,768]{1,0:T(8,128)(2,1)}, f32[128,768]{1...) custom-call(s32[8]{0:T(128)S(1)} %compare_select_fusion.4.facts.refs_0_, ...), custom_call_target="tpu_custom_call" | custom-call | flops 4831838208 | bytes 18874368 | tf_op jit(solution)/shard_map/block/pallas_call | solution.py:182
  44.9 0.7 copy-done.3
  45.6 0.7 copy-done.4
  46.3 0.3 collective-permute-start.3
  46.5 1.8 %collective-permute-start.4 = (bf16[128,768]{1,0:T(8,128)(2,1)}, bf16[128,768]{1,0:T(8,128)(2,1)S(1)}, u32[]{:S(2)}, u32[]{:S(2)}) collective-permute-start(bf16[128,768]{1,0:T(8,128)(2,1)} %get-tuple-element.46), channel_id=1, source_target_pairs={{0,2},{1,3},{2,0},{3,1},{4,6},{5,7},{6,4},{7,5},{8,10},{9,11},{10,... | collective-permute-start | bytes 589832 | tf_op jit(solution)/shard_map/ppermute | solution.py:224
  48.3 0.6 collective-permute-start.5
  49.0 5.1 %collective-permute-done.3 = bf16[128,768]{1,0:T(8,128)(2,1)S(1)} collective-permute-done((bf16[128,768]{1,0:T(8,128)(2,1)}, bf16[128,768]{1,0:T(8,128)(2,1)S(1)}, u32[]{:S(2)}, u32[]{:S(2)}) %collective-permute-start.3) | collective-permute-done | bytes 196640 | tf_op jit(solution)/shard_map/ppermute | solution.py:224
  54.1 1.2 collective-permute-done.4
  55.3 1.7 %collective-permute-done.5 = bf16[128,768]{1,0:T(8,128)(2,1)S(1)} collective-permute-done((bf16[128,768]{1,0:T(8,128)(2,1)}, bf16[128,768]{1,0:T(8,128)(2,1)S(1)}, u32[]{:S(2)}, u32[]{:S(2)}) %collective-permute-start.5) | collective-permute-done | bytes 196640 | tf_op jit(solution)/shard_map/ppermute | solution.py:224
  57.2 2.9 %collective-permute-start.6 = (f32[128,768]{1,0:T(8,128)S(1)}, f32[128,768]{1,0:T(8,128)S(1)}, u32[]{:S(2)}, u32[]{:S(2)}) collective-permute-start(f32[128,768]{1,0:T(8,128)S(1)} %bitcast_add_fusion), channel_id=1, source_target_pairs={{0,4},{4,0},{8,12},{12,8},{16,20},{20,16},{24,28},{28,24},{32,36},... | collective-permute-start | bytes 1179656 | tf_op jit(solution)/shard_map/ppermute | solution.py:229
  60.1 3.3 %collective-permute-start.11 = (bf16[128,768]{1,0:T(8,128)(2,1)}, bf16[128,768]{1,0:T(8,128)(2,1)S(1)}, u32[]{:S(2)}, u32[]{:S(2)}) collective-permute-start(bf16[128,768]{1,0:T(8,128)(2,1)} %copy-done.3), channel_id=1, source_target_pairs={{0,2},{1,3},{2,0},{3,1},{4,6},{5,7},{6,4},{7,5},{8,10},{9,11},{10,... | collective-permute-start | bytes 589832 | tf_op jit(solution)/shard_map/ppermute | solution.py:224
  63.5 1.0 collective-permute-start.9
  64.4 1.2 collective-permute-start.8
  65.6 2.3 %collective-permute-done.10 = bf16[128,768]{1,0:T(8,128)(2,1)S(1)} collective-permute-done((bf16[128,768]{1,0:T(8,128)(2,1)}, bf16[128,768]{1,0:T(8,128)(2,1)S(1)}, u32[]{:S(2)}, u32[]{:S(2)}) %collective-permute-start.10) | collective-permute-done | bytes 196640 | tf_op jit(solution)/shard_map/ppermute | solution.py:224
  68.0 0.3 collective-permute-start.7
  68.2 4.5 %collective-permute-done.11 = bf16[128,768]{1,0:T(8,128)(2,1)S(1)} collective-permute-done((bf16[128,768]{1,0:T(8,128)(2,1)}, bf16[128,768]{1,0:T(8,128)(2,1)S(1)}, u32[]{:S(2)}, u32[]{:S(2)}) %collective-permute-start.11) | collective-permute-done | bytes 196640 | tf_op jit(solution)/shard_map/ppermute | solution.py:224
  72.9 3.7 %collective-permute-done.7 = f32[64,768]{1,0:T(8,128)S(1)} collective-permute-done((f32[64,768]{1,0:T(8,128)S(1)}, f32[64,768]{1,0:T(8,128)S(1)}, u32[]{:S(2)}, u32[]{:S(2)}) %collective-permute-start.7) | collective-permute-done | bytes 196640 | tf_op jit(solution)/shard_map/ppermute | solution.py:235
  76.6 0.9 collective-permute-start.15
  77.6 1.3 collective-permute-start.14
  78.8 3.5 %collective-permute-start.17 = (bf16[128,768]{1,0:T(8,128)(2,1)S(1)}, bf16[128,768]{1,0:T(8,128)(2,1)S(1)}, u32[]{:S(2)}, u32[]{:S(2)}) collective-permute-start(bf16[128,768]{1,0:T(8,128)(2,1)S(1)} %convert_add_fusion.3.refs_5_), channel_id=1, source_target_pairs={{0,2},{1,3},{2,0},{3,1},{4,6},{5,7},{6,4},{7,5},{8,10},{9,11},{10,... | collective-permute-start | bytes 589832 | tf_op jit(solution)/shard_map/ppermute | solution.py:42
  82.4 2.0 %collective-permute-start.16 = (bf16[128,768]{1,0:T(8,128)(2,1)S(1)}, bf16[128,768]{1,0:T(8,128)(2,1)S(1)}, u32[]{:S(2)}, u32[]{:S(2)}) collective-permute-start(bf16[128,768]{1,0:T(8,128)(2,1)S(1)} %convert_add_fusion.3.refs_5_), channel_id=1, source_target_pairs={{0,1},{1,2},{2,3},{3,0},{4,5},{5,6},{6,7},{7,4},{8,9},{9,10},{10,1... | collective-permute-start | bytes 589832 | tf_op jit(solution)/shard_map/ppermute | solution.py:42
  84.4 5.4 %collective-permute-done.13 = f32[64,768]{1,0:T(8,128)S(1)} collective-permute-done((f32[64,768]{1,0:T(8,128)S(1)}, f32[64,768]{1,0:T(8,128)S(1)}, u32[]{:S(2)}, u32[]{:S(2)}) %collective-permute-start.13) | collective-permute-done | bytes 196640 | tf_op jit(solution)/shard_map/ppermute | solution.py:241
  89.9 0.6 collective-permute-done.16.refs_6_
  90.5 2.3 %collective-permute-start.19 = (f32[64,768]{1,0:T(8,128)S(1)}, f32[64,768]{1,0:T(8,128)S(1)}, u32[]{:S(2)}, u32[]{:S(2)}) collective-permute-start(f32[64,768]{1,0:T(8,128)S(1)} %select_add_fusion), channel_id=1, source_target_pairs={{0,4},{4,0},{8,12},{12,8},{16,20},{20,16},{24,28},{28,24},{32,36},... | collective-permute-start | bytes 589832 | tf_op jit(solution)/shard_map/ppermute | solution.py:244
  92.8 1.1 collective-permute-done.19
  94.1 0.3 collective-permute-start.22
  94.4 2.6 %collective-permute-start.21 = (bf16[136,768]{1,0:T(8,128)(2,1)S(1)}, bf16[136,768]{1,0:T(8,128)(2,1)S(1)}, u32[]{:S(2)}, u32[]{:S(2)}) collective-permute-start(bf16[136,768]{1,0:T(8,128)(2,1)S(1)} %centre.3.refs_1_), channel_id=1, source_target_pairs={{0,2},{1,3},{2,0},{3,1},{4,6},{5,7},{6,4},{7,5},{8,10},{9,11},{10,... | collective-permute-start | bytes 626696 | tf_op jit(solution)/shard_map/ppermute | solution.py:42
  97.1 0.6 collective-permute-start.20
  97.7 2.9 %collective-permute-done.22.refs_4_ = bf16[136,768]{1,0:T(8,128)(2,1)S(1)} collective-permute-done((bf16[136,768]{1,0:T(8,128)(2,1)S(1)}, bf16[136,768]{1,0:T(8,128)(2,1)S(1)}, u32[]{:S(2)}, u32[]{:S(2)}) %collective-permute-start.22) | collective-permute-done | bytes 208928 | tf_op jit(solution)/shard_map/ppermute | solution.py:42
  100.6 1.5 collective-permute-done.21.refs_3_
  102.0 5.4 %collective-permute-done.20.refs_2_ = bf16[136,768]{1,0:T(8,128)(2,1)S(1)} collective-permute-done((bf16[136,768]{1,0:T(8,128)(2,1)S(1)}, bf16[136,768]{1,0:T(8,128)(2,1)S(1)}, u32[]{:S(2)}, u32[]{:S(2)}) %collective-permute-start.20) | collective-permute-done | bytes 208928 | tf_op jit(solution)/shard_map/ppermute | solution.py:42
  107.4 10.9 %block.3 = (f32[128,768]{1,0:T(8,128)S(1)}, bf16[128,768]{1,0:T(8,128)(2,1)S(1)}, bf16[128,768]{1,0:T(8,128)(2,1)S(1)}, bf16[128,768]{1,0:T(8,128)(2,1)S(1)}, f3...) custom-call(s32[8]{0:T(128)S(1)} %compare_select_fusion.4.facts.refs, ...), custom_call_target="tpu_custom_call" | custom-call | flops 4831838208 | bytes 18874368 | tf_op jit(solution)/shard_map/block/pallas_call | solution.py:182
  118.3 0.4 collective-permute-start.23
  118.7 1.3 collective-permute-start.24
  120.0 2.0 %collective-permute-start.25 = (bf16[128,768]{1,0:T(8,128)(2,1)S(1)}, bf16[128,768]{1,0:T(8,128)(2,1)S(1)}, u32[]{:S(2)}, u32[]{:S(2)}) collective-permute-start(bf16[128,768]{1,0:T(8,128)(2,1)S(1)} %get-tuple-element.67), channel_id=1, source_target_pairs={{0,3},{1,0},{2,1},{3,2},{4,7},{5,4},{6,5},{7,6},{8,11},{9,8},{10,9... | collective-permute-start | bytes 589832 | tf_op jit(solution)/shard_map/ppermute | solution.py:224
  122.0 4.8 %collective-permute-done.23 = bf16[128,768]{1,0:T(8,128)(2,1)S(1)} collective-permute-done((bf16[128,768]{1,0:T(8,128)(2,1)S(1)}, bf16[128,768]{1,0:T(8,128)(2,1)S(1)}, u32[]{:S(2)}, u32[]{:S(2)}) %collective-permute-start.23) | collective-permute-done | bytes 196640 | tf_op jit(solution)/shard_map/ppermute | solution.py:224
  126.9 1.4 collective-permute-done.24
  128.3 1.9 %collective-permute-done.25 = bf16[128,768]{1,0:T(8,128)(2,1)S(1)} collective-permute-done((bf16[128,768]{1,0:T(8,128)(2,1)S(1)}, bf16[128,768]{1,0:T(8,128)(2,1)S(1)}, u32[]{:S(2)}, u32[]{:S(2)}) %collective-permute-start.25) | collective-permute-done | bytes 196640 | tf_op jit(solution)/shard_map/ppermute | solution.py:224
  130.4 1.9 %collective-permute-start.26 = (bf16[128,768]{1,0:T(8,128)(2,1)S(1)}, bf16[128,768]{1,0:T(8,128)(2,1)S(1)}, u32[]{:S(2)}, u32[]{:S(2)}) collective-permute-start(bf16[128,768]{1,0:T(8,128)(2,1)S(1)} %subtract_convert_fusion), channel_id=1, source_target_pairs={{0,4},{4,0},{8,12},{12,8},{16,20},{20,16},{24,28},{28,24},{32,36},... | collective-permute-start | bytes 589832 | tf_op jit(solution)/shard_map/ppermute | solution.py:229
  132.2 0.9 collective-permute-start.30
  133.1 2.6 %collective-permute-start.31 = (bf16[128,768]{1,0:T(8,128)(2,1)S(1)}, bf16[128,768]{1,0:T(8,128)(2,1)S(1)}, u32[]{:S(2)}, u32[]{:S(2)}) collective-permute-start(bf16[128,768]{1,0:T(8,128)(2,1)S(1)} %get-tuple-element.75), channel_id=1, source_target_pairs={{0,2},{1,3},{2,0},{3,1},{4,6},{5,7},{6,4},{7,5},{8,10},{9,11},{10,... | collective-permute-start | bytes 589832 | tf_op jit(solution)/shard_map/ppermute | solution.py:224
  136.0 1.6 %collective-permute-start.28 = (bf16[64,768]{1,0:T(8,128)(2,1)S(1)}, bf16[64,768]{1,0:T(8,128)(2,1)S(1)}, u32[]{:S(2)}, u32[]{:S(2)}) collective-permute-start(bf16[64,768]{1,0:T(8,128)(2,1)S(1)} %fusion.8), channel_id=1, source_target_pairs={{0,16},{4,20},{8,24},{12,28},{16,0},{20,4},{24,8},{28,12},{32,48},... | collective-permute-start | bytes 294920 | tf_op jit(solution)/shard_map/ppermute | solution.py:235
  137.6 2.3 %collective-permute-done.30 = bf16[128,768]{1,0:T(8,128)(2,1)S(1)} collective-permute-done((bf16[128,768]{1,0:T(8,128)(2,1)S(1)}, bf16[128,768]{1,0:T(8,128)(2,1)S(1)}, u32[]{:S(2)}, u32[]{:S(2)}) %collective-permute-start.30) | collective-permute-done | bytes 196640 | tf_op jit(solution)/shard_map/ppermute | solution.py:224
  139.9 5.1 %collective-permute-done.31 = bf16[128,768]{1,0:T(8,128)(2,1)S(1)} collective-permute-done((bf16[128,768]{1,0:T(8,128)(2,1)S(1)}, bf16[128,768]{1,0:T(8,128)(2,1)S(1)}, u32[]{:S(2)}, u32[]{:S(2)}) %collective-permute-start.31) | collective-permute-done | bytes 196640 | tf_op jit(solution)/shard_map/ppermute | solution.py:224
  145.2 2.7 %collective-permute-start.35 = (bf16[64,768]{1,0:T(8,128)(2,1)S(1)}, bf16[64,768]{1,0:T(8,128)(2,1)S(1)}, u32[]{:S(2)}, u32[]{:S(2)}) collective-permute-start(bf16[64,768]{1,0:T(8,128)(2,1)S(1)} %fusion.7), channel_id=1, source_target_pairs={{0,96},{4,100},{8,104},{12,108},{16,112},{20,116},{24,120},{28,124... | collective-permute-start | bytes 294920 | tf_op jit(solution)/shard_map/ppermute | solution.py:241
  147.9 0.9 collective-permute-start.34
  148.9 0.8 collective-permute-done.35
  149.6 3.3 %collective-permute-done.34 = bf16[64,768]{1,0:T(8,128)(2,1)S(1)} collective-permute-done((bf16[64,768]{1,0:T(8,128)(2,1)S(1)}, bf16[64,768]{1,0:T(8,128)(2,1)S(1)}, u32[]{:S(2)}, u32[]{:S(2)}) %collective-permute-start.34) | collective-permute-done | bytes 98336 | tf_op jit(solution)/shard_map/ppermute | solution.py:241
  152.9 1.0 collective-permute-done.33
  154.0 3.0 %collective-permute-start.36 = (bf16[64,768]{1,0:T(8,128)(2,1)S(1)}, bf16[64,768]{1,0:T(8,128)(2,1)S(1)}, u32[]{:S(2)}, u32[]{:S(2)}) collective-permute-start(bf16[64,768]{1,0:T(8,128)(2,1)S(1)} %fusion.6), channel_id=1, source_target_pairs={{0,4},{4,0},{8,12},{12,8},{16,20},{20,16},{24,28},{28,24},{32,36},... | collective-permute-start | bytes 294920 | tf_op jit(solution)/shard_map/ppermute | solution.py:244
  157.0 0.9 collective-permute-done.36
  158.1 0.9 pad_maximum_fusion
  (52 shorter events, 1.9 us)
Async XLA Ops:
  1.3 1.1 copy-start
  2.6 30.9 %collective-permute-start.2 = (bf16[264,768]{1,0:T(8,128)(2,1)S(1)}, bf16[264,768]{1,0:T(8,128)(2,1)S(1)}, u32[]{:S(2)}, u32[]{:S(2)}) collective-permute-start(bf16[264,768]{1,0:T(8,128)(2,1)S(1)} %centre.2.refs_1_), channel_id=1, source_target_pairs={{0,3},{1,0},{2,1},{3,2},{4,7},{5,4},{6,5},{7,6},{8,11},{9,8},{10,9... | collective-permute-start | bytes 1216520 | tf_op jit(solution)/shard_map/ppermute | solution.py:42
  6.2 27.3 %collective-permute-start.1 = (bf16[264,768]{1,0:T(8,128)(2,1)S(1)}, bf16[264,768]{1,0:T(8,128)(2,1)S(1)}, u32[]{:S(2)}, u32[]{:S(2)}) collective-permute-start(bf16[264,768]{1,0:T(8,128)(2,1)S(1)} %centre.2.refs_1_), channel_id=1, source_target_pairs={{0,2},{1,3},{2,0},{3,1},{4,6},{5,7},{6,4},{7,5},{8,10},{9,11},{10,... | collective-permute-start | bytes 1216520 | tf_op jit(solution)/shard_map/ppermute | solution.py:42
  6.5 27.0 %collective-permute-start = (bf16[264,768]{1,0:T(8,128)(2,1)S(1)}, bf16[264,768]{1,0:T(8,128)(2,1)S(1)}, u32[]{:S(2)}, u32[]{:S(2)}) collective-permute-start(bf16[264,768]{1,0:T(8,128)(2,1)S(1)} %centre.2.refs_1_), channel_id=1, source_target_pairs={{0,1},{1,2},{2,3},{3,0},{4,5},{5,6},{6,7},{7,4},{8,9},{9,10},{10,1... | collective-permute-start | bytes 1216520 | tf_op jit(solution)/shard_map/ppermute | solution.py:42
  7.2 16.3 %all-to-all-start = ((s32[32,1,2]{2,1,0:T(1,128)}), s32[32,1,2]{2,1,0:T(1,128)S(1)}, u32[]{:S(2)}, u32[]{:S(2)}) async-start(s32[32,1,2]{2,1,0:T(1,128)} %broadcast_in_dim.53), calls=%async_computation | async-start | bytes 32768 | tf_op jit(solution)/shard_map/all_to_all | solution.py:212
  23.5 1.3 copy-start.2
  33.5 23.6 %copy-start.1 = (f32[2,128,768]{2,1,0:T(8,128)S(1)}, f32[2,128,768]{2,1,0:T(8,128)}, u32[]{:S(2)}) copy-start(f32[2,128,768]{2,1,0:T(8,128)} %param.6) | copy-start | bytes 2359300
  44.9 0.7 copy-start.3
  45.6 0.7 copy-start.4
  46.3 7.9 %collective-permute-start.3 = (bf16[128,768]{1,0:T(8,128)(2,1)}, bf16[128,768]{1,0:T(8,128)(2,1)S(1)}, u32[]{:S(2)}, u32[]{:S(2)}) collective-permute-start(bf16[128,768]{1,0:T(8,128)(2,1)} %get-tuple-element.45), channel_id=1, source_target_pairs={{0,1},{1,2},{2,3},{3,0},{4,5},{5,6},{6,7},{7,4},{8,9},{9,10},{10,1... | collective-permute-start | bytes 589832 | tf_op jit(solution)/shard_map/ppermute | solution.py:224
  46.5 8.8 %collective-permute-start.4 = (bf16[128,768]{1,0:T(8,128)(2,1)}, bf16[128,768]{1,0:T(8,128)(2,1)S(1)}, u32[]{:S(2)}, u32[]{:S(2)}) collective-permute-start(bf16[128,768]{1,0:T(8,128)(2,1)} %get-tuple-element.46), channel_id=1, source_target_pairs={{0,2},{1,3},{2,0},{3,1},{4,6},{5,7},{6,4},{7,5},{8,10},{9,11},{10,... | collective-permute-start | bytes 589832 | tf_op jit(solution)/shard_map/ppermute | solution.py:224
  48.3 8.7 %collective-permute-start.5 = (bf16[128,768]{1,0:T(8,128)(2,1)}, bf16[128,768]{1,0:T(8,128)(2,1)S(1)}, u32[]{:S(2)}, u32[]{:S(2)}) collective-permute-start(bf16[128,768]{1,0:T(8,128)(2,1)} %get-tuple-element.47), channel_id=1, source_target_pairs={{0,3},{1,0},{2,1},{3,2},{4,7},{5,4},{6,5},{7,6},{8,11},{9,8},{10,9... | collective-permute-start | bytes 589832 | tf_op jit(solution)/shard_map/ppermute | solution.py:224
  57.2 6.2 %collective-permute-start.6 = (f32[128,768]{1,0:T(8,128)S(1)}, f32[128,768]{1,0:T(8,128)S(1)}, u32[]{:S(2)}, u32[]{:S(2)}) collective-permute-start(f32[128,768]{1,0:T(8,128)S(1)} %bitcast_add_fusion), channel_id=1, source_target_pairs={{0,4},{4,0},{8,12},{12,8},{16,20},{20,16},{24,28},{28,24},{32,36},... | collective-permute-start | bytes 1179656 | tf_op jit(solution)/shard_map/ppermute | solution.py:229
  60.1 7.9 %collective-permute-start.10 = (bf16[128,768]{1,0:T(8,128)(2,1)}, bf16[128,768]{1,0:T(8,128)(2,1)S(1)}, u32[]{:S(2)}, u32[]{:S(2)}) collective-permute-start(bf16[128,768]{1,0:T(8,128)(2,1)} %copy-done.4), channel_id=1, source_target_pairs={{0,1},{1,2},{2,3},{3,0},{4,5},{5,6},{6,7},{7,4},{8,9},{9,10},{10,1... | collective-permute-start | bytes 589832 | tf_op jit(solution)/shard_map/ppermute | solution.py:224
  60.1 12.7 %collective-permute-start.11 = (bf16[128,768]{1,0:T(8,128)(2,1)}, bf16[128,768]{1,0:T(8,128)(2,1)S(1)}, u32[]{:S(2)}, u32[]{:S(2)}) collective-permute-start(bf16[128,768]{1,0:T(8,128)(2,1)} %copy-done.3), channel_id=1, source_target_pairs={{0,2},{1,3},{2,0},{3,1},{4,6},{5,7},{6,4},{7,5},{8,10},{9,11},{10,... | collective-permute-start | bytes 589832 | tf_op jit(solution)/shard_map/ppermute | solution.py:224
  63.4 9.4 %collective-permute-start.12 = (bf16[128,768]{1,0:T(8,128)(2,1)S(1)}, bf16[128,768]{1,0:T(8,128)(2,1)S(1)}, u32[]{:S(2)}, u32[]{:S(2)}) collective-permute-start(bf16[128,768]{1,0:T(8,128)(2,1)S(1)} %get-tuple-element.56), channel_id=1, source_target_pairs={{0,3},{1,0},{2,1},{3,2},{4,7},{5,4},{6,5},{7,6},{8,11},{9,8},{10,9... | collective-permute-start | bytes 589832 | tf_op jit(solution)/shard_map/ppermute | solution.py:224
  63.5 9.4 %collective-permute-start.9 = (f32[64,768]{1,0:T(8,128)S(1)}, f32[64,768]{1,0:T(8,128)S(1)}, u32[]{:S(2)}, u32[]{:S(2)}) collective-permute-start(f32[64,768]{1,0:T(8,128)S(1)} %slice_select_fusion.2), channel_id=1, source_target_pairs={{0,24},{4,28},{8,0},{12,4},{16,8},{20,12},{24,16},{28,20},{32,56},... | collective-permute-start | bytes 589832 | tf_op jit(solution)/shard_map/ppermute | solution.py:235
  64.4 8.5 %collective-permute-start.8 = (f32[64,768]{1,0:T(8,128)S(1)}, f32[64,768]{1,0:T(8,128)S(1)}, u32[]{:S(2)}, u32[]{:S(2)}) collective-permute-start(f32[64,768]{1,0:T(8,128)S(1)} %slice_select_fusion.2), channel_id=1, source_target_pairs={{0,16},{4,20},{8,24},{12,28},{16,0},{20,4},{24,8},{28,12},{32,48},... | collective-permute-start | bytes 589832 | tf_op jit(solution)/shard_map/ppermute | solution.py:235
  68.0 8.6 %collective-permute-start.7 = (f32[64,768]{1,0:T(8,128)S(1)}, f32[64,768]{1,0:T(8,128)S(1)}, u32[]{:S(2)}, u32[]{:S(2)}) collective-permute-start(f32[64,768]{1,0:T(8,128)S(1)} %slice_select_fusion.2), channel_id=1, source_target_pairs={{0,8},{4,12},{8,16},{12,20},{16,24},{20,28},{24,0},{28,4},{32,40},... | collective-permute-start | bytes 589832 | tf_op jit(solution)/shard_map/ppermute | solution.py:235
  76.6 7.8 %copy-start.5 = (f32[64,768]{1,0:T(8,128)}, f32[64,768]{1,0:T(8,128)S(1)}, u32[]{:S(2)}) copy-start(f32[64,768]{1,0:T(8,128)S(1)} %collective-permute-done.7) | copy-start | bytes 589828
  76.6 5.7 %collective-permute-start.15 = (f32[64,768]{1,0:T(8,128)S(1)}, f32[64,768]{1,0:T(8,128)S(1)}, u32[]{:S(2)}, u32[]{:S(2)}) collective-permute-start(f32[64,768]{1,0:T(8,128)S(1)} %add_add_fusion), channel_id=1, source_target_pairs={{0,96},{4,100},{8,104},{12,108},{16,112},{20,116},{24,120},{28,124... | collective-permute-start | bytes 589832 | tf_op jit(solution)/shard_map/ppermute | solution.py:241
  77.6 6.8 %collective-permute-start.14 = (f32[64,768]{1,0:T(8,128)S(1)}, f32[64,768]{1,0:T(8,128)S(1)}, u32[]{:S(2)}, u32[]{:S(2)}) collective-permute-start(f32[64,768]{1,0:T(8,128)S(1)} %add_add_fusion), channel_id=1, source_target_pairs={{0,64},{4,68},{8,72},{12,76},{16,80},{20,84},{24,88},{28,92},{32,9... | collective-permute-start | bytes 589832 | tf_op jit(solution)/shard_map/ppermute | solution.py:241
  78.8 10.9 %collective-permute-start.13 = (f32[64,768]{1,0:T(8,128)S(1)}, f32[64,768]{1,0:T(8,128)S(1)}, u32[]{:S(2)}, u32[]{:S(2)}) collective-permute-start(f32[64,768]{1,0:T(8,128)S(1)} %add_add_fusion), channel_id=1, source_target_pairs={{0,32},{4,36},{8,40},{12,44},{16,48},{20,52},{24,56},{28,60},{32,6... | collective-permute-start | bytes 589832 | tf_op jit(solution)/shard_map/ppermute | solution.py:241
  78.8 11.0 %collective-permute-start.18 = (bf16[128,768]{1,0:T(8,128)(2,1)S(1)}, bf16[128,768]{1,0:T(8,128)(2,1)S(1)}, u32[]{:S(2)}, u32[]{:S(2)}) collective-permute-start(bf16[128,768]{1,0:T(8,128)(2,1)S(1)} %convert_add_fusion.3.refs_5_), channel_id=1, source_target_pairs={{0,3},{1,0},{2,1},{3,2},{4,7},{5,4},{6,5},{7,6},{8,11},{9,8},{10,9... | collective-permute-start | bytes 589832 | tf_op jit(solution)/shard_map/ppermute | solution.py:42
  78.8 11.0 %collective-permute-start.17 = (bf16[128,768]{1,0:T(8,128)(2,1)S(1)}, bf16[128,768]{1,0:T(8,128)(2,1)S(1)}, u32[]{:S(2)}, u32[]{:S(2)}) collective-permute-start(bf16[128,768]{1,0:T(8,128)(2,1)S(1)} %convert_add_fusion.3.refs_5_), channel_id=1, source_target_pairs={{0,2},{1,3},{2,0},{3,1},{4,6},{5,7},{6,4},{7,5},{8,10},{9,11},{10,... | collective-permute-start | bytes 589832 | tf_op jit(solution)/shard_map/ppermute | solution.py:42
  82.4 8.1 %collective-permute-start.16 = (bf16[128,768]{1,0:T(8,128)(2,1)S(1)}, bf16[128,768]{1,0:T(8,128)(2,1)S(1)}, u32[]{:S(2)}, u32[]{:S(2)}) collective-permute-start(bf16[128,768]{1,0:T(8,128)(2,1)S(1)} %convert_add_fusion.3.refs_5_), channel_id=1, source_target_pairs={{0,1},{1,2},{2,3},{3,0},{4,5},{5,6},{6,7},{7,4},{8,9},{9,10},{10,1... | collective-permute-start | bytes 589832 | tf_op jit(solution)/shard_map/ppermute | solution.py:42
  90.5 3.4 %collective-permute-start.19 = (f32[64,768]{1,0:T(8,128)S(1)}, f32[64,768]{1,0:T(8,128)S(1)}, u32[]{:S(2)}, u32[]{:S(2)}) collective-permute-start(f32[64,768]{1,0:T(8,128)S(1)} %select_add_fusion), channel_id=1, source_target_pairs={{0,4},{4,0},{8,12},{12,8},{16,20},{20,16},{24,28},{28,24},{32,36},... | collective-permute-start | bytes 589832 | tf_op jit(solution)/shard_map/ppermute | solution.py:244
  94.1 6.4 %collective-permute-start.22 = (bf16[136,768]{1,0:T(8,128)(2,1)S(1)}, bf16[136,768]{1,0:T(8,128)(2,1)S(1)}, u32[]{:S(2)}, u32[]{:S(2)}) collective-permute-start(bf16[136,768]{1,0:T(8,128)(2,1)S(1)} %centre.3.refs_1_), channel_id=1, source_target_pairs={{0,3},{1,0},{2,1},{3,2},{4,7},{5,4},{6,5},{7,6},{8,11},{9,8},{10,9... | collective-permute-start | bytes 626696 | tf_op jit(solution)/shard_map/ppermute | solution.py:42
  94.4 7.6 %collective-permute-start.21 = (bf16[136,768]{1,0:T(8,128)(2,1)S(1)}, bf16[136,768]{1,0:T(8,128)(2,1)S(1)}, u32[]{:S(2)}, u32[]{:S(2)}) collective-permute-start(bf16[136,768]{1,0:T(8,128)(2,1)S(1)} %centre.3.refs_1_), channel_id=1, source_target_pairs={{0,2},{1,3},{2,0},{3,1},{4,6},{5,7},{6,4},{7,5},{8,10},{9,11},{10,... | collective-permute-start | bytes 626696 | tf_op jit(solution)/shard_map/ppermute | solution.py:42
  97.1 10.3 %collective-permute-start.20 = (bf16[136,768]{1,0:T(8,128)(2,1)S(1)}, bf16[136,768]{1,0:T(8,128)(2,1)S(1)}, u32[]{:S(2)}, u32[]{:S(2)}) collective-permute-start(bf16[136,768]{1,0:T(8,128)(2,1)S(1)} %centre.3.refs_1_), channel_id=1, source_target_pairs={{0,1},{1,2},{2,3},{3,0},{4,5},{5,6},{6,7},{7,4},{8,9},{9,10},{10,1... | collective-permute-start | bytes 626696 | tf_op jit(solution)/shard_map/ppermute | solution.py:42
  118.3 8.5 %collective-permute-start.23 = (bf16[128,768]{1,0:T(8,128)(2,1)S(1)}, bf16[128,768]{1,0:T(8,128)(2,1)S(1)}, u32[]{:S(2)}, u32[]{:S(2)}) collective-permute-start(bf16[128,768]{1,0:T(8,128)(2,1)S(1)} %get-tuple-element.65), channel_id=1, source_target_pairs={{0,1},{1,2},{2,3},{3,0},{4,5},{5,6},{6,7},{7,4},{8,9},{9,10},{10,1... | collective-permute-start | bytes 589832 | tf_op jit(solution)/shard_map/ppermute | solution.py:224
  118.7 9.6 %collective-permute-start.24 = (bf16[128,768]{1,0:T(8,128)(2,1)S(1)}, bf16[128,768]{1,0:T(8,128)(2,1)S(1)}, u32[]{:S(2)}, u32[]{:S(2)}) collective-permute-start(bf16[128,768]{1,0:T(8,128)(2,1)S(1)} %get-tuple-element.66), channel_id=1, source_target_pairs={{0,2},{1,3},{2,0},{3,1},{4,6},{5,7},{6,4},{7,5},{8,10},{9,11},{10,... | collective-permute-start | bytes 589832 | tf_op jit(solution)/shard_map/ppermute | solution.py:224
  120.0 10.2 %collective-permute-start.25 = (bf16[128,768]{1,0:T(8,128)(2,1)S(1)}, bf16[128,768]{1,0:T(8,128)(2,1)S(1)}, u32[]{:S(2)}, u32[]{:S(2)}) collective-permute-start(bf16[128,768]{1,0:T(8,128)(2,1)S(1)} %get-tuple-element.67), channel_id=1, source_target_pairs={{0,3},{1,0},{2,1},{3,2},{4,7},{5,4},{6,5},{7,6},{8,11},{9,8},{10,9... | collective-permute-start | bytes 589832 | tf_op jit(solution)/shard_map/ppermute | solution.py:224
  130.4 5.5 %collective-permute-start.26 = (bf16[128,768]{1,0:T(8,128)(2,1)S(1)}, bf16[128,768]{1,0:T(8,128)(2,1)S(1)}, u32[]{:S(2)}, u32[]{:S(2)}) collective-permute-start(bf16[128,768]{1,0:T(8,128)(2,1)S(1)} %subtract_convert_fusion), channel_id=1, source_target_pairs={{0,4},{4,0},{8,12},{12,8},{16,20},{20,16},{24,28},{28,24},{32,36},... | collective-permute-start | bytes 589832 | tf_op jit(solution)/shard_map/ppermute | solution.py:229
  132.2 7.7 %collective-permute-start.30 = (bf16[128,768]{1,0:T(8,128)(2,1)S(1)}, bf16[128,768]{1,0:T(8,128)(2,1)S(1)}, u32[]{:S(2)}, u32[]{:S(2)}) collective-permute-start(bf16[128,768]{1,0:T(8,128)(2,1)S(1)} %get-tuple-element.74), channel_id=1, source_target_pairs={{0,1},{1,2},{2,3},{3,0},{4,5},{5,6},{6,7},{7,4},{8,9},{9,10},{10,1... | collective-permute-start | bytes 589832 | tf_op jit(solution)/shard_map/ppermute | solution.py:224
  133.1 11.8 %collective-permute-start.31 = (bf16[128,768]{1,0:T(8,128)(2,1)S(1)}, bf16[128,768]{1,0:T(8,128)(2,1)S(1)}, u32[]{:S(2)}, u32[]{:S(2)}) collective-permute-start(bf16[128,768]{1,0:T(8,128)(2,1)S(1)} %get-tuple-element.75), channel_id=1, source_target_pairs={{0,2},{1,3},{2,0},{3,1},{4,6},{5,7},{6,4},{7,5},{8,10},{9,11},{10,... | collective-permute-start | bytes 589832 | tf_op jit(solution)/shard_map/ppermute | solution.py:224
  135.8 9.2 %collective-permute-start.32 = (bf16[128,768]{1,0:T(8,128)(2,1)S(1)}, bf16[128,768]{1,0:T(8,128)(2,1)S(1)}, u32[]{:S(2)}, u32[]{:S(2)}) collective-permute-start(bf16[128,768]{1,0:T(8,128)(2,1)S(1)} %get-tuple-element.76), channel_id=1, source_target_pairs={{0,3},{1,0},{2,1},{3,2},{4,7},{5,4},{6,5},{7,6},{8,11},{9,8},{10,9... | collective-permute-start | bytes 589832 | tf_op jit(solution)/shard_map/ppermute | solution.py:224
  135.9 9.1 %collective-permute-start.29 = (bf16[64,768]{1,0:T(8,128)(2,1)S(1)}, bf16[64,768]{1,0:T(8,128)(2,1)S(1)}, u32[]{:S(2)}, u32[]{:S(2)}) collective-permute-start(bf16[64,768]{1,0:T(8,128)(2,1)S(1)} %fusion.8), channel_id=1, source_target_pairs={{0,24},{4,28},{8,0},{12,4},{16,8},{20,12},{24,16},{28,20},{32,56},... | collective-permute-start | bytes 294920 | tf_op jit(solution)/shard_map/ppermute | solution.py:235
  136.0 9.1 %collective-permute-start.28 = (bf16[64,768]{1,0:T(8,128)(2,1)S(1)}, bf16[64,768]{1,0:T(8,128)(2,1)S(1)}, u32[]{:S(2)}, u32[]{:S(2)}) collective-permute-start(bf16[64,768]{1,0:T(8,128)(2,1)S(1)} %fusion.8), channel_id=1, source_target_pairs={{0,16},{4,20},{8,24},{12,28},{16,0},{20,4},{24,8},{28,12},{32,48},... | collective-permute-start | bytes 294920 | tf_op jit(solution)/shard_map/ppermute | solution.py:235
  139.9 5.2 %collective-permute-start.27 = (bf16[64,768]{1,0:T(8,128)(2,1)S(1)}, bf16[64,768]{1,0:T(8,128)(2,1)S(1)}, u32[]{:S(2)}, u32[]{:S(2)}) collective-permute-start(bf16[64,768]{1,0:T(8,128)(2,1)S(1)} %fusion.8), channel_id=1, source_target_pairs={{0,8},{4,12},{8,16},{12,20},{16,24},{20,28},{24,0},{28,4},{32,40},... | collective-permute-start | bytes 294920 | tf_op jit(solution)/shard_map/ppermute | solution.py:235
  145.2 4.5 %collective-permute-start.35 = (bf16[64,768]{1,0:T(8,128)(2,1)S(1)}, bf16[64,768]{1,0:T(8,128)(2,1)S(1)}, u32[]{:S(2)}, u32[]{:S(2)}) collective-permute-start(bf16[64,768]{1,0:T(8,128)(2,1)S(1)} %fusion.7), channel_id=1, source_target_pairs={{0,96},{4,100},{8,104},{12,108},{16,112},{20,116},{24,120},{28,124... | collective-permute-start | bytes 294920 | tf_op jit(solution)/shard_map/ppermute | solution.py:241
  147.9 5.0 %collective-permute-start.34 = (bf16[64,768]{1,0:T(8,128)(2,1)S(1)}, bf16[64,768]{1,0:T(8,128)(2,1)S(1)}, u32[]{:S(2)}, u32[]{:S(2)}) collective-permute-start(bf16[64,768]{1,0:T(8,128)(2,1)S(1)} %fusion.7), channel_id=1, source_target_pairs={{0,64},{4,68},{8,72},{12,76},{16,80},{20,84},{24,88},{28,92},{32,9... | collective-permute-start | bytes 294920 | tf_op jit(solution)/shard_map/ppermute | solution.py:241
  148.7 5.2 %collective-permute-start.33 = (bf16[64,768]{1,0:T(8,128)(2,1)S(1)}, bf16[64,768]{1,0:T(8,128)(2,1)S(1)}, u32[]{:S(2)}, u32[]{:S(2)}) collective-permute-start(bf16[64,768]{1,0:T(8,128)(2,1)S(1)} %fusion.7), channel_id=1, source_target_pairs={{0,32},{4,36},{8,40},{12,44},{16,48},{20,52},{24,56},{28,60},{32,6... | collective-permute-start | bytes 294920 | tf_op jit(solution)/shard_map/ppermute | solution.py:241
  154.0 3.9 %collective-permute-start.36 = (bf16[64,768]{1,0:T(8,128)(2,1)S(1)}, bf16[64,768]{1,0:T(8,128)(2,1)S(1)}, u32[]{:S(2)}, u32[]{:S(2)}) collective-permute-start(bf16[64,768]{1,0:T(8,128)(2,1)S(1)} %fusion.6), channel_id=1, source_target_pairs={{0,4},{4,0},{8,12},{12,8},{16,20},{20,16},{24,28},{28,24},{32,36},... | collective-permute-start | bytes 294920 | tf_op jit(solution)/shard_map/ppermute | solution.py:244

commit v3 on v2

v3 whole, which is shorter than its diff:
```python
import math

import jax
import jax.numpy as jnp
from jax import lax
from jax.experimental import pallas as pl
from jax.experimental.pallas import tpu as pltpu
from jax.sharding import PartitionSpec as P

HD = 128
FREQ = 256
EXTRA = 8
LIMIT = 48
ROOM = 28
LEVELS = 320
NX, NZ, NC, NY = 4, 4, 2, 4
BF = jnp.bfloat16
F32 = jnp.float32


def ring(k):
    return [(i, (i + k) % NY) for i in range(NY)]


def place(x, z, c):
    return (x * NZ + z) * NC + c


CHIPS = [(x, z, c) for x in range(NX) for z in range(NZ) for c in range(NC)]
SWAP = [(place(x, z, c), place(x, z, 1 - c)) for x, z, c in CHIPS]


def z_shift(k):
    return [(place(x, z, c), place(x, (z + k) % NZ, c)) for x, z, c in CHIPS]


def x_shift(k):
    return [(place(x, z, c), place((x + k) % NX, z, c)) for x, z, c in CHIPS]


def spread(array):
    return [array] + [lax.ppermute(array, "tp", ring(k)) for k in (1, 2, 3)]


def modulation_body(facts, all_gaps, mod_ref, out_ref):
    half_freq = FREQ // 2
    gaps = all_gaps[...]
    earlier = lax.broadcasted_iota(jnp.int32, gaps.shape, 0) < facts[0]
    before = jnp.sum(jnp.where(earlier, gaps, 0), 0)
    level = before[:, 0:1] + before[:, 1:2] + facts[2]
    lane = lax.broadcasted_iota(jnp.int32, (1, half_freq), 1).astype(F32)
    frequencies = jnp.exp(-math.log(10000.0) * lane / half_freq)
    rows = []
    for here in (level, level + facts[3]):
        angles = 1000.0 * (1.0 - here.astype(F32) / LEVELS) * frequencies
        rows.append(jnp.concatenate([jnp.cos(angles), jnp.sin(angles)], -1))
    index = lax.broadcasted_iota(jnp.int32, (8, FREQ), 0)
    embed_rows = jnp.where(index == 0, rows[0], jnp.where(index == 1, rows[1], 0.0)).astype(BF)
    out_ref[...] = jnp.zeros_like(out_ref)
    for p in range(3):
        made = jnp.dot(embed_rows, mod_ref[p], preferred_element_type=F32)
        for s in range(2):
            for y in range(NY):
                out_ref[y, 3 * s + p : 3 * s + p + 1, :] = made[s : s + 1]


def modulation(facts, all_gaps, mod_weight):
    vmem = pl.BlockSpec(memory_space=pltpu.VMEM)
    smem = pl.BlockSpec(memory_space=pltpu.SMEM)
    return pl.pallas_call(
        modulation_body,
        out_shape=jax.ShapeDtypeStruct((NY, 8, mod_weight.shape[-1]), F32),
        in_specs=[smem, vmem, vmem],
        out_specs=vmem,
        compiler_params=pltpu.CompilerParams(vmem_limit_bytes=8 * 2**20),
        name="modulation",
    )(facts, all_gaps, mod_weight)


def centre_body(x_ref, out_ref):
    rows, cols = x_ref.shape
    x = x_ref[...]
    mean = (jnp.sum(x, -1, keepdims=True) / cols).astype(BF).astype(F32)
    out_ref[:rows, :] = (x - mean).astype(BF)
    along = jnp.transpose(jnp.broadcast_to(mean, (rows, HD)))
    out_ref[rows : rows + EXTRA, :] = jnp.zeros((EXTRA, cols), BF)
    out_ref[rows : rows + EXTRA, :rows] = along[:EXTRA].astype(BF)


def centre(x):
    rows, cols = x.shape
    vmem = pl.BlockSpec(memory_space=pltpu.VMEM)
    return pl.pallas_call(
        centre_body,
        out_shape=jax.ShapeDtypeStruct((rows + EXTRA, cols), BF),
        in_specs=[vmem],
        out_specs=vmem,
        compiler_params=pltpu.CompilerParams(vmem_limit_bytes=8 * 2**20),
        name="centre",
    )(x)


def attend(rows_of, tok, cols, nrm, wv, qkv, att, ready):
    for p in range(3):
        ready(p)
        qkv[p] = jnp.dot(nrm[...], wv[p], preferred_element_type=F32).astype(BF)
    cells = [(pl.ds(r * tok, tok), pl.ds(h * HD, HD)) for r in range(rows_of) for h in range(cols // HD)]
    scores = [
        lax.dot_general(
            qkv[0, rows, lanes], qkv[1, rows, lanes], (((1,), (1,)), ((), ())), preferred_element_type=F32
        )
        * (1.0 / math.sqrt(HD))
        for rows, lanes in cells
    ]
    weights = [jnp.exp(x - jnp.max(x, -1, keepdims=True)) for x in scores]
    probs = [(w * (1.0 / jnp.sum(w, -1, keepdims=True))).astype(BF) for w in weights]
    for (rows, lanes), prob in zip(cells, probs, strict=True):
        att[rows, lanes] = jnp.dot(prob, qkv[2, rows, lanes], preferred_element_type=F32).astype(BF)


def normalise(parts, s, row, tok, cols, me, mods, nrm):
    width = NY * cols
    mean = sum(jnp.sum(x, -1, keepdims=True) for x in parts) / width
    var = sum(jnp.sum((x - mean) * (x - mean), -1, keepdims=True) for x in parts) / width
    inv = lax.rsqrt(var + 1e-06)
    for k in range(NY):
        src = lax.rem(me + NY - k, NY)
        shift = mods[src, 3 * s : 3 * s + 1, :]
        scale = mods[src, 3 * s + 1 : 3 * s + 2, :]
        normed = (parts[k] - mean) * inv * (1.0 + scale) + shift
        nrm[row : row + tok, pl.ds(pl.multiple_of(src * cols, cols), cols)] = normed.astype(BF)
    return mean


def both_body(tok, cols, facts, *refs):
    states, mods, qkv_hbm, out_hbm = refs[:4], refs[4], refs[5], refs[6]
    tots, ins, (start_ref, nrm, qkv, att, wv, wo, sems) = refs[7:11], refs[11:15], refs[15:]
    copies = [pltpu.make_async_copy(qkv_hbm.at[p], wv.at[p], sems.at[p]) for p in range(3)]
    copies.append(pltpu.make_async_copy(out_hbm, wo, sems.at[3]))
    for copy in copies:
        copy.start()
    me = facts[1]
    centres = [jnp.transpose(states[k][2 * tok :, : 2 * tok].astype(F32))[:, 0:1] for k in range(NY)]
    for s in range(2):
        rows = pl.ds(s * tok, tok)
        parts = [states[k][rows, :].astype(F32) + centres[k][s * tok : (s + 1) * tok] for k in range(NY)]
        mean = normalise(parts, s, s * tok, tok, cols, me, mods, nrm)
        if s == 0:
            start_ref[...] = parts[0] - mean
    attend(2, tok, cols, nrm, wv, qkv, att, lambda p: copies[p].wait())
    copies[3].wait()
    neg = [-(facts[3 + s].astype(F32) / LEVELS) for s in range(2)]
    for k in (1, 2, 3, 0):
        dst = lax.rem(me + k, NY)
        at = pl.multiple_of(dst * cols, cols)
        made = jnp.dot(att[...], wo[:, pl.ds(at, cols)], preferred_element_type=F32)
        inc0 = made[:tok] * (mods[dst, 2:3, :] * neg[0])
        inc1 = made[tok:] * (mods[dst, 5:6, :] * neg[1])
        tots[k][...] = (inc0 + inc1).astype(tots[k].dtype)
        ins[k][...] = inc0.astype(ins[k].dtype)


def one_body(s, tok, cols, facts, *refs):
    states, mods, wv, wo, refs = refs[:4], refs[4], refs[5], refs[6], refs[7:]
    if s == 1:
        earlier, refs = refs[0], refs[1:]
    else:
        kept, refs = refs[0], refs[1:]
    shares, (nrm, qkv, att) = refs[:4], refs[4:]
    me = facts[1]
    normalise([states[k][...].astype(F32) for k in range(NY)], s, 0, tok, cols, me, mods, nrm)
    attend(1, tok, cols, nrm, wv, qkv, att, lambda p: None)
    neg = -(facts[3 + s].astype(F32) / LEVELS)
    for k in (1, 2, 3, 0):
        dst = lax.rem(me + k, NY)
        at = pl.multiple_of(dst * cols, cols)
        made = jnp.dot(att[...], wo[:, pl.ds(at, cols)], preferred_element_type=F32)
        made = made * (mods[dst, 3 * s + 2 : 3 * s + 3, :] * neg)
        if s == 1:
            made = made + earlier[k]
        else:
            kept[k] = made
        shares[k][...] = made.astype(shares[k].dtype)


def specs():
    return (pl.BlockSpec(memory_space=m) for m in (pltpu.VMEM, pltpu.SMEM, pltpu.HBM))


def share_shapes(tok, cols):
    return [jax.ShapeDtypeStruct((tok, cols), F32 if k == 0 else BF) for k in range(NY)]


def rows_scratch(rows, cols):
    return [pltpu.VMEM((rows, NY * cols), BF), pltpu.VMEM((3, rows, cols), BF), pltpu.VMEM((rows, cols), BF)]


def estimate(steps, tok, cols):
    return pl.CostEstimate(
        flops=2 * steps * tok * NY * cols * 4 * cols, bytes_accessed=8 * NY * cols * cols, transcendentals=0
    )


def both(facts, states, mods, qkv_weight, out_weight):
    cols, _ = out_weight.shape
    tok = (states[0].shape[0] - EXTRA) // 2
    vmem, smem, hbm = specs()
    shares = share_shapes(tok, cols)
    made = pl.pallas_call(
        lambda *refs: both_body(tok, cols, *refs),
        out_shape=shares + shares + shares[:1],
        in_specs=[smem] + [vmem] * 5 + [hbm, hbm],
        out_specs=[vmem] * 9,
        scratch_shapes=rows_scratch(2 * tok, cols)
        + [pltpu.VMEM(qkv_weight.shape, BF), pltpu.VMEM(out_weight.shape, BF), pltpu.SemaphoreType.DMA((4,))],
        compiler_params=pltpu.CompilerParams(vmem_limit_bytes=LIMIT * 2**20),
        cost_estimate=estimate(2, tok, cols),
        name="both",
    )(facts, *states, mods, qkv_weight, out_weight)
    return made[:NY], made[NY : 2 * NY], made[2 * NY]


def one(s, facts, states, mods, weights, earlier):
    tok, cols = states[0].shape
    vmem, smem, _ = specs()
    kept = [jax.ShapeDtypeStruct((NY, tok, cols), F32)] * (s == 0)
    return pl.pallas_call(
        lambda *refs: one_body(s, tok, cols, *refs),
        out_shape=kept + share_shapes(tok, cols),
        in_specs=[smem] + [vmem] * (7 + len(earlier)),
        out_specs=[vmem] * (len(kept) + NY),
        scratch_shapes=rows_scratch(tok, cols),
        compiler_params=pltpu.CompilerParams(vmem_limit_bytes=ROOM * 2**20),
        cost_estimate=estimate(1, tok, cols),
        name="one",
    )(facts, *states, mods, *weights, *earlier)


def arrive_body(facts, after, wv, wo, out):
    for i in range(8):
        out[i] = facts[i]


def arrive(facts, after, qkv_weight, out_weight):
    vmem, smem, hbm = specs()
    return pl.pallas_call(
        arrive_body,
        out_shape=jax.ShapeDtypeStruct(facts.shape, facts.dtype),
        in_specs=[smem, hbm, vmem, vmem],
        out_specs=smem,
        compiler_params=pltpu.CompilerParams(vmem_limit_bytes=ROOM * 2**20),
        name="arrive",
    )(facts, after, qkv_weight, out_weight)


def body(trajectory, offset, step_gaps, qkv_weight, out_weight, mod_weight):
    steps_here, tok, cols = trajectory.shape
    tm, tp = lax.axis_index("tm"), lax.axis_index("tp")
    x_at, z_at, core = tm // (NZ * NC), (tm // NC) % NZ, tm % NC
    half = tok // 2

    sent = jnp.broadcast_to(step_gaps[None, None], (NX * NZ * NC, 1, steps_here))
    trajectory, sent = lax.optimization_barrier((trajectory, sent))
    all_gaps = lax.all_to_all(sent, "tm", 0, 0)
    states = spread(centre(trajectory.reshape(steps_here * tok, cols)))
    place_of = jnp.arange(8, dtype=jnp.int32)
    facts = jnp.where(place_of == 0, tm, jnp.where(place_of == 1, tp, jnp.where(place_of == 2, offset[0], 0)))
    facts = jnp.where(place_of == 3, step_gaps[0], jnp.where(place_of == 4, step_gaps[1], facts))
    weights = (jnp.transpose(qkv_weight, (1, 0, 2)), out_weight)
    made = modulation(facts, all_gaps, jnp.transpose(mod_weight, (1, 0, 2)))
    mods = lax.all_to_all(made, "tp", 0, 0)

    def deliver(own, shares):
        total = own
        for k in (1, 2, 3):
            total = total + lax.ppermute(shares[k], "tp", ring(k)).astype(F32)
        return total

    def before_me(own, sent, beside_z):
        now = []

        def send(value, pairs):
            mine, theirs = sent[len(now)] if sent else ((0.0), (0.0,) * len(pairs))
            message = (value - mine).astype(BF)
            came = [lax.ppermute(message, "tm", p).astype(F32) + t for p, t in zip(pairs, theirs, strict=True)]
            now.append((message.astype(F32) + mine, came))
            return came

        (other,) = send(own, [SWAP])
        chip = own + other
        mine = jnp.where(core == 0, chip[:half], chip[half:])
        came = send(mine, [z_shift(k) for k in (1, 2, 3)])
        plane = mine + came[0] + came[1] + came[2]
        below = sum(jnp.where(z_at >= k, c, 0.0) for k, c in zip((1, 2, 3), came, strict=True))
        plane, beside_z = lax.optimization_barrier((plane, beside_z))
        came = send(plane, [x_shift(k) for k in (1, 2, 3)])
        below = below + sum(jnp.where(x_at >= k, c, 0.0) for k, c in zip((1, 2, 3), came, strict=True))
        (rest,) = send(below, [SWAP])
        low = jnp.where(core == 0, below, rest)
        high = jnp.where(core == 0, rest, below)
        return jnp.concatenate([low, high], 0), other, now, beside_z

    tots, ins, start = both(facts, states, mods, *weights)
    start = jnp.where(tm == 0, start, 0.0)
    total = deliver(tots[0], tots)
    total, ins = lax.optimization_barrier((total, ins))
    prefix, other, sent, inc0 = before_me(total + start, (), deliver(ins[0], ins))
    entry = prefix + jnp.where(core == 0, start, other)
    first, second = spread(entry.astype(BF)), spread((entry + inc0).astype(BF))
    facts = arrive(facts, first[0], *weights)
    kept, *ins = one(0, facts, first, mods, weights, [])
    inc0 = deliver(ins[0], ins)
    tots = one(1, facts, second, mods, weights, [kept])
    start = jnp.where(tm == 0, trajectory[0], 0.0)
    total, inc0 = lax.optimization_barrier((deliver(tots[0], tots), inc0))
    prefix, other, _, _ = before_me(total + start, sent, ())
    entry = prefix + jnp.where(core == 0, start, other)
    return jnp.stack([entry + inc0, entry + total])


def solution(mesh):
    placed = (
        P("tm", None, "tp"),
        P(),
        P("tm"),
        P(None, None, "tp"),
        P("tp", None),
        P(None, None, "tp"),
    )
    return jax.shard_map(
        body, mesh=mesh, in_specs=placed, out_specs=P("tm", None, "tp"), check_vma=False
    )
```

time: 159 us -> 149 us (0.937)
  waiting for transfers between devices: 60.5 us -> 42.7 us
  local copies, waits for them, and re-layouts: 6.42 us -> 13.1 us
  starting transfers between devices: 56.6 us -> 58.8 us
    ppermute x9, waiting for transfers between devices: 10.4 us -> 0.02 us  [spread(): return [array] + [lax.ppermute(array, 'tp', ring(k)) for k in (1, 2, 3)]]
    ppermute x12, waiting for transfers between devices: 30.4 us -> 23 us  [deliver(): total = total + lax.ppermute(shares[k], 'tp', ring(k)).astype(F32)]
    unnamed x12 -> x50, local copies, waits for them, and re-layouts: 3.79 us -> 10.5 us
    ppermute x12, starting transfers between devices: 13.3 us -> 15 us  [deliver(): total = total + lax.ppermute(shares[k], 'tp', ring(k)).astype(F32)]
    pallas_call x2 -> x4, Pallas kernels: 22.2 us -> 21.2 us  [the longest x1 11.4 us: both(): pl.pallas_call(lambda *refs: both_body(tok, cols, *refs), out_shape=share...]
  transfers between devices with their start and end apart: 38 -> 38, of which waited for: 22 -> 20; matrix products, arithmetic and copies ran while one was open for 2% -> 2% of each run, Pallas kernels for 1% -> 7%
where the time goes in v3:
time: 149 us
  starting transfers between devices  58.8 us (39%)
  waiting for transfers between devices  42.7 us (29%)
  Pallas kernels  22.4 us (15%)
  local copies, waits for them, and re-layouts  13.1 us (9%)
  blocking collectives  7.02 us (5%)
  other arithmetic  3.65 us (2%)
    ppermute x12, waiting for transfers between devices, deliver(): total = total + lax.ppermute(shares[k], 'tp', ring(k)).astype(F32)  23 us
    ppermute x16, starting transfers between devices, send(): lax.ppermute(message, 'tm', p).astype(F32) + t  20.9 us
    ppermute x16, waiting for transfers between devices, send(): lax.ppermute(message, 'tm', p).astype(F32) + t  16 us
    ppermute x12, starting transfers between devices, deliver(): total = total + lax.ppermute(shares[k], 'tp', ring(k)).astype(F32)  15 us
    ppermute x9, starting transfers between devices, spread(): return [array] + [lax.ppermute(array, 'tp', ring(k)) for k in (1, 2, 3)]  13.5 us
    pallas_call x1, Pallas kernels, both(): pl.pallas_call(lambda *refs: both_body(tok, cols, *refs), out_shape=share...  11.4 us
    unnamed x50, local copies, waits for them, and re-layouts  10.5 us
    all_to_all x1, starting transfers between devices, body(): all_gaps = lax.all_to_all(sent, 'tm', 0, 0)  9.44 us
  transfers between devices with their start and end apart: 38, of which 20 were waited for; matrix products, arithmetic and copies ran while one was open for 2% of the time, Pallas kernels for 7%

profile of v3, /device:TPU:1, one launch (start us, length us, event | category | flops | bytes accessed | tf_op | source)
XLA Modules:
  0.0 148.7 jit_solution(7219945661831497040)
XLA Ops:
  0.0 1.3 broadcast_in_dim.52
  1.3 1.1 copy-done.3
  2.6 2.2 %collective-permute-start = (bf16[264,768]{1,0:T(8,128)(2,1)S(1)}, bf16[264,768]{1,0:T(8,128)(2,1)S(1)}, u32[]{:S(2)}, u32[]{:S(2)}) collective-permute-start(bf16[264,768]{1,0:T(8,128)(2,1)S(1)} %centre.1.refs_1_), channel_id=1, source_target_pairs={{0,1},{1,2},{2,3},{3,0},{4,5},{5,6},{6,7},{7,4},{8,9},{9,10},{10,1... | collective-permute-start | bytes 1216520 | tf_op jit(solution)/shard_map/ppermute | solution.py:42
  4.7 2.6 %collective-permute-start.1 = (bf16[264,768]{1,0:T(8,128)(2,1)S(1)}, bf16[264,768]{1,0:T(8,128)(2,1)S(1)}, u32[]{:S(2)}, u32[]{:S(2)}) collective-permute-start(bf16[264,768]{1,0:T(8,128)(2,1)S(1)} %centre.1.refs_1_), channel_id=1, source_target_pairs={{0,2},{1,3},{2,0},{3,1},{4,6},{5,7},{6,4},{7,5},{8,10},{9,11},{10,... | collective-permute-start | bytes 1216520 | tf_op jit(solution)/shard_map/ppermute | solution.py:42
  7.4 1.1 collective-permute-start.2
  8.4 9.4 %all-to-all-start = ((s32[32,1,2]{2,1,0:T(1,128)}), s32[32,1,2]{2,1,0:T(1,128)S(1)}, u32[]{:S(2)}, u32[]{:S(2)}) async-start(s32[32,1,2]{2,1,0:T(1,128)} %broadcast_in_dim.52), calls=%async_computation | async-start | bytes 32768 | tf_op jit(solution)/shard_map/all_to_all | solution.py:264
  18.5 1.3 fusion.21
  19.8 1.2 compare_select_fusion.4.facts.refs_0_
  21.1 3.7 %all-to-all-done.all_gaps = s32[32,1,2]{2,1,0:T(1,128)S(1)} async-done(((s32[32,1,2]{2,1,0:T(1,128)}), s32[32,1,2]{2,1,0:T(1,128)S(1)}, u32[]{:S(2)}, u32[]{:S(2)}) %all-to-all-start) | async-done | bytes 288 | tf_op jit(solution)/shard_map/all_to_all | solution.py:264
  24.8 1.3 copy-done.5
  26.0 1.0 modulation.1
  27.0 7.0 %all_to_all.10.refs_5_ = f32[4,8,768]{2,1,0:T(8,128)S(1)} all-to-all(f32[4,8,768]{2,1,0:T(8,128)S(1)} %modulation.1), channel_id=1, replica_groups=mesh['tm'=32,'tp'=4] {'tp'}, dimensions={0} | all-to-all | bytes 196608 | tf_op jit(solution)/shard_map/all_to_all | solution.py:271
  34.1 11.4 %both.1 = (f32[128,768]{1,0:T(8,128)S(1)}, bf16[128,768]{1,0:T(8,128)(2,1)}, bf16[128,768]{1,0:T(8,128)(2,1)}, bf16[128,768]{1,0:T(8,128)(2,1)}, f32[128,768]{1,...) custom-call(s32[8]{0:T(128)S(1)} %compare_select_fusion.4.facts.refs, ...), custom_call_target="tpu_custom_call" | custom-call | flops 4831838208 | bytes 18874368 | tf_op jit(solution)/shard_map/both/pallas_call | solution.py:209
  45.5 0.7 copy-done.6
  46.5 1.8 %collective-permute-start.4 = (bf16[128,768]{1,0:T(8,128)(2,1)}, bf16[128,768]{1,0:T(8,128)(2,1)S(1)}, u32[]{:S(2)}, u32[]{:S(2)}) collective-permute-start(bf16[128,768]{1,0:T(8,128)(2,1)} %get-tuple-element.38), channel_id=1, source_target_pairs={{0,2},{1,3},{2,0},{3,1},{4,6},{5,7},{6,4},{7,5},{8,10},{9,11},{10,... | collective-permute-start | bytes 589832 | tf_op jit(solution)/shard_map/ppermute | solution.py:276
  48.2 0.9 collective-permute-start.5
  49.2 4.6 %collective-permute-done.3 = bf16[128,768]{1,0:T(8,128)(2,1)S(1)} collective-permute-done((bf16[128,768]{1,0:T(8,128)(2,1)}, bf16[128,768]{1,0:T(8,128)(2,1)S(1)}, u32[]{:S(2)}, u32[]{:S(2)}) %collective-permute-start.3) | collective-permute-done | bytes 196640 | tf_op jit(solution)/shard_map/ppermute | solution.py:276
  53.8 1.7 %collective-permute-done.4 = bf16[128,768]{1,0:T(8,128)(2,1)S(1)} collective-permute-done((bf16[128,768]{1,0:T(8,128)(2,1)}, bf16[128,768]{1,0:T(8,128)(2,1)S(1)}, u32[]{:S(2)}, u32[]{:S(2)}) %collective-permute-start.4) | collective-permute-done | bytes 196640 | tf_op jit(solution)/shard_map/ppermute | solution.py:276
  55.5 2.4 %collective-permute-done.5 = bf16[128,768]{1,0:T(8,128)(2,1)S(1)} collective-permute-done((bf16[128,768]{1,0:T(8,128)(2,1)}, bf16[128,768]{1,0:T(8,128)(2,1)S(1)}, u32[]{:S(2)}, u32[]{:S(2)}) %collective-permute-start.5) | collective-permute-done | bytes 196640 | tf_op jit(solution)/shard_map/ppermute | solution.py:276
  58.0 2.0 %collective-permute-start.6 = (bf16[128,768]{1,0:T(8,128)(2,1)S(1)}, bf16[128,768]{1,0:T(8,128)(2,1)S(1)}, u32[]{:S(2)}, u32[]{:S(2)}) collective-permute-start(bf16[128,768]{1,0:T(8,128)(2,1)S(1)} %fusion.15), channel_id=1, source_target_pairs={{0,4},{4,0},{8,12},{12,8},{16,20},{20,16},{24,28},{28,24},{32,36},... | collective-permute-start | bytes 589832 | tf_op jit(solution)/shard_map/ppermute | solution.py:285
  60.3 3.3 %collective-permute-start.11 = (bf16[128,768]{1,0:T(8,128)(2,1)S(1)}, bf16[128,768]{1,0:T(8,128)(2,1)S(1)}, u32[]{:S(2)}, u32[]{:S(2)}) collective-permute-start(bf16[128,768]{1,0:T(8,128)(2,1)S(1)} %get-tuple-element.48), channel_id=1, source_target_pairs={{0,2},{1,3},{2,0},{3,1},{4,6},{5,7},{6,4},{7,5},{8,10},{9,11},{10,... | collective-permute-start | bytes 589832 | tf_op jit(solution)/shard_map/ppermute | solution.py:276
  63.6 0.4 collective-permute-start.7
  64.0 1.8 %collective-permute-start.8 = (bf16[64,768]{1,0:T(8,128)(2,1)S(1)}, bf16[64,768]{1,0:T(8,128)(2,1)S(1)}, u32[]{:S(2)}, u32[]{:S(2)}) collective-permute-start(bf16[64,768]{1,0:T(8,128)(2,1)S(1)} %fusion.16), channel_id=1, source_target_pairs={{0,16},{4,20},{8,24},{12,28},{16,0},{20,4},{24,8},{28,12},{32,48},... | collective-permute-start | bytes 294920 | tf_op jit(solution)/shard_map/ppermute | solution.py:285
  65.8 2.1 %collective-permute-done.10 = bf16[128,768]{1,0:T(8,128)(2,1)S(1)} collective-permute-done((bf16[128,768]{1,0:T(8,128)(2,1)}, bf16[128,768]{1,0:T(8,128)(2,1)S(1)}, u32[]{:S(2)}, u32[]{:S(2)}) %collective-permute-start.10) | collective-permute-done | bytes 196640 | tf_op jit(solution)/shard_map/ppermute | solution.py:276
  67.9 0.9 collective-permute-start.9
  68.8 4.2 %collective-permute-done.11 = bf16[128,768]{1,0:T(8,128)(2,1)S(1)} collective-permute-done((bf16[128,768]{1,0:T(8,128)(2,1)S(1)}, bf16[128,768]{1,0:T(8,128)(2,1)S(1)}, u32[]{:S(2)}, u32[]{:S(2)}) %collective-permute-start.11) | collective-permute-done | bytes 196640 | tf_op jit(solution)/shard_map/ppermute | solution.py:276
  73.1 0.4 collective-permute-start.13
  73.5 1.7 %collective-permute-start.14 = (bf16[64,768]{1,0:T(8,128)(2,1)S(1)}, bf16[64,768]{1,0:T(8,128)(2,1)S(1)}, u32[]{:S(2)}, u32[]{:S(2)}) collective-permute-start(bf16[64,768]{1,0:T(8,128)(2,1)S(1)} %convert_add_fusion.8), channel_id=1, source_target_pairs={{0,64},{4,68},{8,72},{12,76},{16,80},{20,84},{24,88},{28,92},{32,9... | collective-permute-start | bytes 294920 | tf_op jit(solution)/shard_map/ppermute | solution.py:285
  75.3 1.0 collective-permute-start.15
  76.2 2.6 %collective-permute-done.13 = bf16[64,768]{1,0:T(8,128)(2,1)S(1)} collective-permute-done((bf16[64,768]{1,0:T(8,128)(2,1)S(1)}, bf16[64,768]{1,0:T(8,128)(2,1)S(1)}, u32[]{:S(2)}, u32[]{:S(2)}) %collective-permute-start.13) | collective-permute-done | bytes 98336 | tf_op jit(solution)/shard_map/ppermute | solution.py:285
  78.8 0.7 collective-permute-done.14
  79.5 0.7 collective-permute-done.15
  80.4 2.2 %collective-permute-start.16 = (bf16[64,768]{1,0:T(8,128)(2,1)S(1)}, bf16[64,768]{1,0:T(8,128)(2,1)S(1)}, u32[]{:S(2)}, u32[]{:S(2)}) collective-permute-start(bf16[64,768]{1,0:T(8,128)(2,1)S(1)} %get-tuple-element.67), channel_id=1, source_target_pairs={{0,4},{4,0},{8,12},{12,8},{16,20},{20,16},{24,28},{28,24},{32,36},... | collective-permute-start | bytes 294920 | tf_op jit(solution)/shard_map/ppermute | solution.py:285
  82.5 0.9 collective-permute-done.16
  83.9 3.3 %collective-permute-start.21 = (bf16[128,768]{1,0:T(8,128)(2,1)S(1)}, bf16[128,768]{1,0:T(8,128)(2,1)S(1)}, u32[]{:S(2)}, u32[]{:S(2)}) collective-permute-start(bf16[128,768]{1,0:T(8,128)(2,1)S(1)} %get-tuple-element.70.after.refs_1_), channel_id=1, source_target_pairs={{0,2},{1,3},{2,0},{3,1},{4,6},{5,7},{6,4},{7,5},{8,10},{9,11},{10,... | collective-permute-start | bytes 589832 | tf_op jit(solution)/shard_map/ppermute | solution.py:42
  87.3 5.0 %copy-done = bf16[3072,3,768]{2,0,1:T(8,128)(2,1)S(1)} copy-done((bf16[3072,3,768]{2,0,1:T(8,128)(2,1)S(1)}, bf16[3072,3,768]{2,0,1:T(8,128)(2,1)}, u32[]{:S(2)}) %copy-start) | copy-done | bytes 14155800
  92.3 2.3 %copy-done.2 = bf16[768,3072]{1,0:T(8,128)(2,1)S(1)} copy-done((bf16[768,3072]{1,0:T(8,128)(2,1)S(1)}, bf16[768,3072]{1,0:T(8,128)(2,1)}, u32[]{:S(2)}) %copy-start.2) | copy-done | bytes 4718616
  94.7 1.1 arrive.1.refs_0_
  95.8 1.5 %collective-permute-start.17 = (bf16[128,768]{1,0:T(8,128)(2,1)S(1)}, bf16[128,768]{1,0:T(8,128)(2,1)S(1)}, u32[]{:S(2)}, u32[]{:S(2)}) collective-permute-start(bf16[128,768]{1,0:T(8,128)(2,1)S(1)} %get-tuple-element.69.refs_1_), channel_id=1, source_target_pairs={{0,1},{1,2},{2,3},{3,0},{4,5},{5,6},{6,7},{7,4},{8,9},{9,10},{10,1... | collective-permute-start | bytes 589832 | tf_op jit(solution)/shard_map/ppermute | solution.py:42
  97.5 2.3 %collective-permute-start.19 = (bf16[128,768]{1,0:T(8,128)(2,1)S(1)}, bf16[128,768]{1,0:T(8,128)(2,1)S(1)}, u32[]{:S(2)}, u32[]{:S(2)}) collective-permute-start(bf16[128,768]{1,0:T(8,128)(2,1)S(1)} %get-tuple-element.69.refs_1_), channel_id=1, source_target_pairs={{0,3},{1,0},{2,1},{3,2},{4,7},{5,4},{6,5},{7,6},{8,11},{9,8},{10,9... | collective-permute-start | bytes 589832 | tf_op jit(solution)/shard_map/ppermute | solution.py:42
  99.8 4.3 %one.2 = (f32[4,128,768]{2,1,0:T(8,128)S(1)}, f32[128,768]{1,0:T(8,128)S(1)}, bf16[128,768]{1,0:T(8,128)(2,1)S(1)}, bf16[128,768]{1,0:T(8,128)(2,1)S(1)}, bf16[128,768]{1,0:T(8,128)(2,1)S(1)}) custom-call(s32[8]{0:T(128)S(1)} %arrive.1.refs_0_, bf16[128,768]{1,0:T(8,128)(2,1)S(1)} %get-tuple-element.70.after.refs_1_, ...), custom_call_target="tpu_custom_call" | custom-call | flops 2415919104 | bytes 18874368 | tf_op jit(solution)/shard_map/one/pallas_call | solution.py:227
  104.1 1.4 collective-permute-start.26
  105.5 0.7 collective-permute-start.27
  106.1 1.8 %collective-permute-start.28 = (bf16[128,768]{1,0:T(8,128)(2,1)S(1)}, bf16[128,768]{1,0:T(8,128)(2,1)S(1)}, u32[]{:S(2)}, u32[]{:S(2)}) collective-permute-start(bf16[128,768]{1,0:T(8,128)(2,1)S(1)} %get-tuple-element.60), channel_id=1, source_target_pairs={{0,3},{1,0},{2,1},{3,2},{4,7},{5,4},{6,5},{7,6},{8,11},{9,8},{10,9... | collective-permute-start | bytes 589832 | tf_op jit(solution)/shard_map/ppermute | solution.py:276
  108.0 4.3 %one.3 = (f32[128,768]{1,0:T(8,128)S(1)}, bf16[128,768]{1,0:T(8,128)(2,1)S(1)}, bf16[128,768]{1,0:T(8,128)(2,1)S(1)}, bf16[128,768]{1,0:T(8,128)(2,1)S(1)}) custom-call(s32[8]{0:T(128)S(1)} %arrive.1.refs_0_, bf16[128,768]{1,0:T(8,128)(2,1)S(1)} %get-tuple-element.69.refs_1_, bf16[128,768]{1,0:T(8,128)(2,1)S(1)} %collective-permute-done.17.refs_2_, ...), custom_call_target="tpu_custom_call" | custom-call | flops 2415919104 | bytes 18874368 | tf_op jit(solution)/shard_map/one/pallas_call | solution.py:227
  112.4 2.1 %collective-permute-start.23 = (bf16[128,768]{1,0:T(8,128)(2,1)S(1)}, bf16[128,768]{1,0:T(8,128)(2,1)S(1)}, u32[]{:S(2)}, u32[]{:S(2)}) collective-permute-start(bf16[128,768]{1,0:T(8,128)(2,1)S(1)} %get-tuple-element.54), channel_id=1, source_target_pairs={{0,1},{1,2},{2,3},{3,0},{4,5},{5,6},{6,7},{7,4},{8,9},{9,10},{10,1... | collective-permute-start | bytes 589832 | tf_op jit(solution)/shard_map/ppermute | solution.py:276
  114.5 2.1 %collective-permute-start.24 = (bf16[128,768]{1,0:T(8,128)(2,1)S(1)}, bf16[128,768]{1,0:T(8,128)(2,1)S(1)}, u32[]{:S(2)}, u32[]{:S(2)}) collective-permute-start(bf16[128,768]{1,0:T(8,128)(2,1)S(1)} %get-tuple-element.55), channel_id=1, source_target_pairs={{0,2},{1,3},{2,0},{3,1},{4,6},{5,7},{6,4},{7,5},{8,10},{9,11},{10,... | collective-permute-start | bytes 589832 | tf_op jit(solution)/shard_map/ppermute | solution.py:276
  116.6 0.4 collective-permute-start.25
  117.1 1.4 collective-permute-done.23
  118.5 6.7 %collective-permute-done.24 = bf16[128,768]{1,0:T(8,128)(2,1)S(1)} collective-permute-done((bf16[128,768]{1,0:T(8,128)(2,1)S(1)}, bf16[128,768]{1,0:T(8,128)(2,1)S(1)}, u32[]{:S(2)}, u32[]{:S(2)}) %collective-permute-start.24) | collective-permute-done | bytes 196640 | tf_op jit(solution)/shard_map/ppermute | solution.py:276
  125.4 1.6 %collective-permute-start.29 = (bf16[128,768]{1,0:T(8,128)(2,1)S(1)}, bf16[128,768]{1,0:T(8,128)(2,1)S(1)}, u32[]{:S(2)}, u32[]{:S(2)}) collective-permute-start(bf16[128,768]{1,0:T(8,128)(2,1)S(1)} %subtract_convert_fusion), channel_id=1, source_target_pairs={{0,4},{4,0},{8,12},{12,8},{16,20},{20,16},{24,28},{28,24},{32,36},... | collective-permute-start | bytes 589832 | tf_op jit(solution)/shard_map/ppermute | solution.py:285
  126.9 1.1 collective-permute-done.29
  128.2 0.4 collective-permute-start.30
  128.5 2.5 %collective-permute-start.31 = (bf16[64,768]{1,0:T(8,128)(2,1)S(1)}, bf16[64,768]{1,0:T(8,128)(2,1)S(1)}, u32[]{:S(2)}, u32[]{:S(2)}) collective-permute-start(bf16[64,768]{1,0:T(8,128)(2,1)S(1)} %subtract_convert_fusion.3), channel_id=1, source_target_pairs={{0,16},{4,20},{8,24},{12,28},{16,0},{20,4},{24,8},{28,12},{32,48},... | collective-permute-start | bytes 294920 | tf_op jit(solution)/shard_map/ppermute | solution.py:285
  131.2 2.2 %collective-permute-done.30 = bf16[64,768]{1,0:T(8,128)(2,1)S(1)} collective-permute-done((bf16[64,768]{1,0:T(8,128)(2,1)S(1)}, bf16[64,768]{1,0:T(8,128)(2,1)S(1)}, u32[]{:S(2)}, u32[]{:S(2)}) %collective-permute-start.30) | collective-permute-done | bytes 98336 | tf_op jit(solution)/shard_map/ppermute | solution.py:285
  133.5 2.2 %collective-permute-done.31 = bf16[64,768]{1,0:T(8,128)(2,1)S(1)} collective-permute-done((bf16[64,768]{1,0:T(8,128)(2,1)S(1)}, bf16[64,768]{1,0:T(8,128)(2,1)S(1)}, u32[]{:S(2)}, u32[]{:S(2)}) %collective-permute-start.31) | collective-permute-done | bytes 98336 | tf_op jit(solution)/shard_map/ppermute | solution.py:285
  136.0 0.5 collective-permute-start.33
  136.4 3.2 %collective-permute-start.34 = (bf16[64,768]{1,0:T(8,128)(2,1)S(1)}, bf16[64,768]{1,0:T(8,128)(2,1)S(1)}, u32[]{:S(2)}, u32[]{:S(2)}) collective-permute-start(bf16[64,768]{1,0:T(8,128)(2,1)S(1)} %subtract_convert_fusion.2), channel_id=1, source_target_pairs={{0,64},{4,68},{8,72},{12,76},{16,80},{20,84},{24,88},{28,92},{32,9... | collective-permute-start | bytes 294920 | tf_op jit(solution)/shard_map/ppermute | solution.py:285
  139.6 1.1 collective-permute-done.33
  140.7 2.1 %collective-permute-done.34 = bf16[64,768]{1,0:T(8,128)(2,1)S(1)} collective-permute-done((bf16[64,768]{1,0:T(8,128)(2,1)S(1)}, bf16[64,768]{1,0:T(8,128)(2,1)S(1)}, u32[]{:S(2)}, u32[]{:S(2)}) %collective-permute-start.34) | collective-permute-done | bytes 98336 | tf_op jit(solution)/shard_map/ppermute | solution.py:285
  142.8 1.3 collective-permute-done.35
  144.3 2.4 %collective-permute-start.36 = (bf16[64,768]{1,0:T(8,128)(2,1)S(1)}, bf16[64,768]{1,0:T(8,128)(2,1)S(1)}, u32[]{:S(2)}, u32[]{:S(2)}) collective-permute-start(bf16[64,768]{1,0:T(8,128)(2,1)S(1)} %get-tuple-element.65), channel_id=1, source_target_pairs={{0,4},{4,0},{8,12},{12,8},{16,20},{20,16},{24,28},{28,24},{32,36},... | collective-permute-start | bytes 294920 | tf_op jit(solution)/shard_map/ppermute | solution.py:285
  146.6 0.9 collective-permute-done.36
  147.8 0.9 pad_maximum_fusion
  (93 shorter events, 3.3 us)
Async XLA Ops:
  1.3 1.1 copy-start.3
  2.6 31.5 %collective-permute-start = (bf16[264,768]{1,0:T(8,128)(2,1)S(1)}, bf16[264,768]{1,0:T(8,128)(2,1)S(1)}, u32[]{:S(2)}, u32[]{:S(2)}) collective-permute-start(bf16[264,768]{1,0:T(8,128)(2,1)S(1)} %centre.1.refs_1_), channel_id=1, source_target_pairs={{0,1},{1,2},{2,3},{3,0},{4,5},{5,6},{6,7},{7,4},{8,9},{9,10},{10,1... | collective-permute-start | bytes 1216520 | tf_op jit(solution)/shard_map/ppermute | solution.py:42
  4.7 29.3 %collective-permute-start.1 = (bf16[264,768]{1,0:T(8,128)(2,1)S(1)}, bf16[264,768]{1,0:T(8,128)(2,1)S(1)}, u32[]{:S(2)}, u32[]{:S(2)}) collective-permute-start(bf16[264,768]{1,0:T(8,128)(2,1)S(1)} %centre.1.refs_1_), channel_id=1, source_target_pairs={{0,2},{1,3},{2,0},{3,1},{4,6},{5,7},{6,4},{7,5},{8,10},{9,11},{10,... | collective-permute-start | bytes 1216520 | tf_op jit(solution)/shard_map/ppermute | solution.py:42
  7.4 26.7 %collective-permute-start.2 = (bf16[264,768]{1,0:T(8,128)(2,1)S(1)}, bf16[264,768]{1,0:T(8,128)(2,1)S(1)}, u32[]{:S(2)}, u32[]{:S(2)}) collective-permute-start(bf16[264,768]{1,0:T(8,128)(2,1)S(1)} %centre.1.refs_1_), channel_id=1, source_target_pairs={{0,3},{1,0},{2,1},{3,2},{4,7},{5,4},{6,5},{7,6},{8,11},{9,8},{10,9... | collective-permute-start | bytes 1216520 | tf_op jit(solution)/shard_map/ppermute | solution.py:42
  8.4 16.3 %all-to-all-start = ((s32[32,1,2]{2,1,0:T(1,128)}), s32[32,1,2]{2,1,0:T(1,128)S(1)}, u32[]{:S(2)}, u32[]{:S(2)}) async-start(s32[32,1,2]{2,1,0:T(1,128)} %broadcast_in_dim.52), calls=%async_computation | async-start | bytes 32768 | tf_op jit(solution)/shard_map/all_to_all | solution.py:264
  24.8 1.3 copy-start.5
  45.5 0.7 copy-start.6
  46.2 7.6 %collective-permute-start.3 = (bf16[128,768]{1,0:T(8,128)(2,1)}, bf16[128,768]{1,0:T(8,128)(2,1)S(1)}, u32[]{:S(2)}, u32[]{:S(2)}) collective-permute-start(bf16[128,768]{1,0:T(8,128)(2,1)} %get-tuple-element.37), channel_id=1, source_target_pairs={{0,1},{1,2},{2,3},{3,0},{4,5},{5,6},{6,7},{7,4},{8,9},{9,10},{10,1... | collective-permute-start | bytes 589832 | tf_op jit(solution)/shard_map/ppermute | solution.py:276
  46.5 9.0 %collective-permute-start.4 = (bf16[128,768]{1,0:T(8,128)(2,1)}, bf16[128,768]{1,0:T(8,128)(2,1)S(1)}, u32[]{:S(2)}, u32[]{:S(2)}) collective-permute-start(bf16[128,768]{1,0:T(8,128)(2,1)} %get-tuple-element.38), channel_id=1, source_target_pairs={{0,2},{1,3},{2,0},{3,1},{4,6},{5,7},{6,4},{7,5},{8,10},{9,11},{10,... | collective-permute-start | bytes 589832 | tf_op jit(solution)/shard_map/ppermute | solution.py:276
  48.2 9.6 %collective-permute-start.5 = (bf16[128,768]{1,0:T(8,128)(2,1)}, bf16[128,768]{1,0:T(8,128)(2,1)S(1)}, u32[]{:S(2)}, u32[]{:S(2)}) collective-permute-start(bf16[128,768]{1,0:T(8,128)(2,1)} %get-tuple-element.39), channel_id=1, source_target_pairs={{0,3},{1,0},{2,1},{3,2},{4,7},{5,4},{6,5},{7,6},{8,11},{9,8},{10,9... | collective-permute-start | bytes 589832 | tf_op jit(solution)/shard_map/ppermute | solution.py:276
  58.0 5.5 %copy-start.13 = (bf16[128,768]{1,0:T(8,128)(2,1)}, bf16[128,768]{1,0:T(8,128)(2,1)S(1)}, u32[]{:S(2)}) copy-start(bf16[128,768]{1,0:T(8,128)(2,1)S(1)} %fusion.15) | copy-start | bytes 589828
  58.0 5.5 %collective-permute-start.6 = (bf16[128,768]{1,0:T(8,128)(2,1)S(1)}, bf16[128,768]{1,0:T(8,128)(2,1)S(1)}, u32[]{:S(2)}, u32[]{:S(2)}) collective-permute-start(bf16[128,768]{1,0:T(8,128)(2,1)S(1)} %fusion.15), channel_id=1, source_target_pairs={{0,4},{4,0},{8,12},{12,8},{16,20},{20,16},{24,28},{28,24},{32,36},... | collective-permute-start | bytes 589832 | tf_op jit(solution)/shard_map/ppermute | solution.py:285
  60.0 7.9 %collective-permute-start.10 = (bf16[128,768]{1,0:T(8,128)(2,1)}, bf16[128,768]{1,0:T(8,128)(2,1)S(1)}, u32[]{:S(2)}, u32[]{:S(2)}) collective-permute-start(bf16[128,768]{1,0:T(8,128)(2,1)} %copy-done.6), channel_id=1, source_target_pairs={{0,1},{1,2},{2,3},{3,0},{4,5},{5,6},{6,7},{7,4},{8,9},{9,10},{10,1... | collective-permute-start | bytes 589832 | tf_op jit(solution)/shard_map/ppermute | solution.py:276
  60.3 12.7 %collective-permute-start.11 = (bf16[128,768]{1,0:T(8,128)(2,1)S(1)}, bf16[128,768]{1,0:T(8,128)(2,1)S(1)}, u32[]{:S(2)}, u32[]{:S(2)}) collective-permute-start(bf16[128,768]{1,0:T(8,128)(2,1)S(1)} %get-tuple-element.48), channel_id=1, source_target_pairs={{0,2},{1,3},{2,0},{3,1},{4,6},{5,7},{6,4},{7,5},{8,10},{9,11},{10,... | collective-permute-start | bytes 589832 | tf_op jit(solution)/shard_map/ppermute | solution.py:276
  63.5 9.4 %collective-permute-start.12 = (bf16[128,768]{1,0:T(8,128)(2,1)S(1)}, bf16[128,768]{1,0:T(8,128)(2,1)S(1)}, u32[]{:S(2)}, u32[]{:S(2)}) collective-permute-start(bf16[128,768]{1,0:T(8,128)(2,1)S(1)} %get-tuple-element.49), channel_id=1, source_target_pairs={{0,3},{1,0},{2,1},{3,2},{4,7},{5,4},{6,5},{7,6},{8,11},{9,8},{10,9... | collective-permute-start | bytes 589832 | tf_op jit(solution)/shard_map/ppermute | solution.py:276
  63.5 23.7 %copy-start.7 = (bf16[128,768]{1,0:T(8,128)(2,1)}, bf16[128,768]{1,0:T(8,128)(2,1)S(1)}, u32[]{:S(2)}) copy-start(bf16[128,768]{1,0:T(8,128)(2,1)S(1)} %collective-permute-done.6) | copy-start | bytes 589828
  63.6 9.4 %collective-permute-start.7 = (bf16[64,768]{1,0:T(8,128)(2,1)S(1)}, bf16[64,768]{1,0:T(8,128)(2,1)S(1)}, u32[]{:S(2)}, u32[]{:S(2)}) collective-permute-start(bf16[64,768]{1,0:T(8,128)(2,1)S(1)} %fusion.16), channel_id=1, source_target_pairs={{0,8},{4,12},{8,16},{12,20},{16,24},{20,28},{24,0},{28,4},{32,40},... | collective-permute-start | bytes 294920 | tf_op jit(solution)/shard_map/ppermute | solution.py:285
  64.0 9.0 %collective-permute-start.8 = (bf16[64,768]{1,0:T(8,128)(2,1)S(1)}, bf16[64,768]{1,0:T(8,128)(2,1)S(1)}, u32[]{:S(2)}, u32[]{:S(2)}) collective-permute-start(bf16[64,768]{1,0:T(8,128)(2,1)S(1)} %fusion.16), channel_id=1, source_target_pairs={{0,16},{4,20},{8,24},{12,28},{16,0},{20,4},{24,8},{28,12},{32,48},... | collective-permute-start | bytes 294920 | tf_op jit(solution)/shard_map/ppermute | solution.py:285
  67.9 5.2 %collective-permute-start.9 = (bf16[64,768]{1,0:T(8,128)(2,1)S(1)}, bf16[64,768]{1,0:T(8,128)(2,1)S(1)}, u32[]{:S(2)}, u32[]{:S(2)}) collective-permute-start(bf16[64,768]{1,0:T(8,128)(2,1)S(1)} %fusion.16), channel_id=1, source_target_pairs={{0,24},{4,28},{8,0},{12,4},{16,8},{20,12},{24,16},{28,20},{32,56},... | collective-permute-start | bytes 294920 | tf_op jit(solution)/shard_map/ppermute | solution.py:285
  73.0 10.5 %copy-start.9 = (bf16[64,768]{1,0:T(8,128)(2,1)}, bf16[64,768]{1,0:T(8,128)(2,1)S(1)}, u32[]{:S(2)}) copy-start(bf16[64,768]{1,0:T(8,128)(2,1)S(1)} %collective-permute-done.8) | copy-start | bytes 294916
  73.1 14.2 %copy-start.11 = (bf16[64,768]{1,0:T(8,128)(2,1)}, bf16[64,768]{1,0:T(8,128)(2,1)S(1)}, u32[]{:S(2)}) copy-start(bf16[64,768]{1,0:T(8,128)(2,1)S(1)} %collective-permute-done.9) | copy-start | bytes 294916
  73.1 10.3 %copy-start.15 = (bf16[64,768]{1,0:T(8,128)(2,1)}, bf16[64,768]{1,0:T(8,128)(2,1)S(1)}, u32[]{:S(2)}) copy-start(bf16[64,768]{1,0:T(8,128)(2,1)S(1)} %convert_add_fusion.8) | copy-start | bytes 294916
  73.1 5.7 %collective-permute-start.13 = (bf16[64,768]{1,0:T(8,128)(2,1)S(1)}, bf16[64,768]{1,0:T(8,128)(2,1)S(1)}, u32[]{:S(2)}, u32[]{:S(2)}) collective-permute-start(bf16[64,768]{1,0:T(8,128)(2,1)S(1)} %convert_add_fusion.8), channel_id=1, source_target_pairs={{0,32},{4,36},{8,40},{12,44},{16,48},{20,52},{24,56},{28,60},{32,6... | collective-permute-start | bytes 294920 | tf_op jit(solution)/shard_map/ppermute | solution.py:285
  73.5 5.9 %collective-permute-start.14 = (bf16[64,768]{1,0:T(8,128)(2,1)S(1)}, bf16[64,768]{1,0:T(8,128)(2,1)S(1)}, u32[]{:S(2)}, u32[]{:S(2)}) collective-permute-start(bf16[64,768]{1,0:T(8,128)(2,1)S(1)} %convert_add_fusion.8), channel_id=1, source_target_pairs={{0,64},{4,68},{8,72},{12,76},{16,80},{20,84},{24,88},{28,92},{32,9... | collective-permute-start | bytes 294920 | tf_op jit(solution)/shard_map/ppermute | solution.py:285
  75.3 5.0 %collective-permute-start.15 = (bf16[64,768]{1,0:T(8,128)(2,1)S(1)}, bf16[64,768]{1,0:T(8,128)(2,1)S(1)}, u32[]{:S(2)}, u32[]{:S(2)}) collective-permute-start(bf16[64,768]{1,0:T(8,128)(2,1)S(1)} %convert_add_fusion.8), channel_id=1, source_target_pairs={{0,96},{4,100},{8,104},{12,108},{16,112},{20,116},{24,120},{28,124... | collective-permute-start | bytes 294920 | tf_op jit(solution)/shard_map/ppermute | solution.py:285
  78.8 4.7 %copy-start.17 = (bf16[64,768]{1,0:T(8,128)(2,1)}, bf16[64,768]{1,0:T(8,128)(2,1)S(1)}, u32[]{:S(2)}) copy-start(bf16[64,768]{1,0:T(8,128)(2,1)S(1)} %collective-permute-done.13) | copy-start | bytes 294916
  79.5 4.0 %copy-start.19 = (bf16[64,768]{1,0:T(8,128)(2,1)}, bf16[64,768]{1,0:T(8,128)(2,1)S(1)}, u32[]{:S(2)}) copy-start(bf16[64,768]{1,0:T(8,128)(2,1)S(1)} %collective-permute-done.14) | copy-start | bytes 294916
  80.2 3.2 %copy-start.21 = (bf16[64,768]{1,0:T(8,128)(2,1)}, bf16[64,768]{1,0:T(8,128)(2,1)S(1)}, u32[]{:S(2)}) copy-start(bf16[64,768]{1,0:T(8,128)(2,1)S(1)} %collective-permute-done.15) | copy-start | bytes 294916
  80.4 6.8 %copy-start.23 = (bf16[64,768]{1,0:T(8,128)(2,1)}, bf16[64,768]{1,0:T(8,128)(2,1)S(1)}, u32[]{:S(2)}) copy-start(bf16[64,768]{1,0:T(8,128)(2,1)S(1)} %get-tuple-element.67) | copy-start | bytes 294916
  80.4 3.1 %collective-permute-start.16 = (bf16[64,768]{1,0:T(8,128)(2,1)S(1)}, bf16[64,768]{1,0:T(8,128)(2,1)S(1)}, u32[]{:S(2)}, u32[]{:S(2)}) collective-permute-start(bf16[64,768]{1,0:T(8,128)(2,1)S(1)} %get-tuple-element.67), channel_id=1, source_target_pairs={{0,4},{4,0},{8,12},{12,8},{16,20},{20,16},{24,28},{28,24},{32,36},... | collective-permute-start | bytes 294920 | tf_op jit(solution)/shard_map/ppermute | solution.py:285
  83.7 13.9 %collective-permute-start.20 = (bf16[128,768]{1,0:T(8,128)(2,1)S(1)}, bf16[128,768]{1,0:T(8,128)(2,1)S(1)}, u32[]{:S(2)}, u32[]{:S(2)}) collective-permute-start(bf16[128,768]{1,0:T(8,128)(2,1)S(1)} %get-tuple-element.70.after.refs_1_), channel_id=1, source_target_pairs={{0,1},{1,2},{2,3},{3,0},{4,5},{5,6},{6,7},{7,4},{8,9},{9,10},{10,1... | collective-permute-start | bytes 589832 | tf_op jit(solution)/shard_map/ppermute | solution.py:42
  83.9 15.9 %collective-permute-start.21 = (bf16[128,768]{1,0:T(8,128)(2,1)S(1)}, bf16[128,768]{1,0:T(8,128)(2,1)S(1)}, u32[]{:S(2)}, u32[]{:S(2)}) collective-permute-start(bf16[128,768]{1,0:T(8,128)(2,1)S(1)} %get-tuple-element.70.after.refs_1_), channel_id=1, source_target_pairs={{0,2},{1,3},{2,0},{3,1},{4,6},{5,7},{6,4},{7,5},{8,10},{9,11},{10,... | collective-permute-start | bytes 589832 | tf_op jit(solution)/shard_map/ppermute | solution.py:42
  87.2 12.6 %collective-permute-start.22 = (bf16[128,768]{1,0:T(8,128)(2,1)S(1)}, bf16[128,768]{1,0:T(8,128)(2,1)S(1)}, u32[]{:S(2)}, u32[]{:S(2)}) collective-permute-start(bf16[128,768]{1,0:T(8,128)(2,1)S(1)} %get-tuple-element.70.after.refs_1_), channel_id=1, source_target_pairs={{0,3},{1,0},{2,1},{3,2},{4,7},{5,4},{6,5},{7,6},{8,11},{9,8},{10,9... | collective-permute-start | bytes 589832 | tf_op jit(solution)/shard_map/ppermute | solution.py:42
  87.3 5.0 %copy-start = (bf16[3072,3,768]{2,0,1:T(8,128)(2,1)S(1)}, bf16[3072,3,768]{2,0,1:T(8,128)(2,1)}, u32[]{:S(2)}) copy-start(bf16[3072,3,768]{2,0,1:T(8,128)(2,1)} %param.9) | copy-start | bytes 42467332
  92.3 2.3 %copy-start.2 = (bf16[768,3072]{1,0:T(8,128)(2,1)S(1)}, bf16[768,3072]{1,0:T(8,128)(2,1)}, u32[]{:S(2)}) copy-start(bf16[768,3072]{1,0:T(8,128)(2,1)} %refs_7_.5) | copy-start | bytes 14155780
  94.7 5.2 %copy-start.1 = (bf16[3072,3,768]{2,0,1:T(8,128)(2,1)S(1)}, bf16[3072,3,768]{2,0,1:T(8,128)(2,1)}, u32[]{:S(2)}) copy-start(bf16[3072,3,768]{2,0,1:T(8,128)(2,1)} %param.9) | copy-start | bytes 42467332
  95.8 10.3 %collective-permute-start.17 = (bf16[128,768]{1,0:T(8,128)(2,1)S(1)}, bf16[128,768]{1,0:T(8,128)(2,1)S(1)}, u32[]{:S(2)}, u32[]{:S(2)}) collective-permute-start(bf16[128,768]{1,0:T(8,128)(2,1)S(1)} %get-tuple-element.69.refs_1_), channel_id=1, source_target_pairs={{0,1},{1,2},{2,3},{3,0},{4,5},{5,6},{6,7},{7,4},{8,9},{9,10},{10,1... | collective-permute-start | bytes 589832 | tf_op jit(solution)/shard_map/ppermute | solution.py:42
  97.3 10.7 %collective-permute-start.18 = (bf16[128,768]{1,0:T(8,128)(2,1)S(1)}, bf16[128,768]{1,0:T(8,128)(2,1)S(1)}, u32[]{:S(2)}, u32[]{:S(2)}) collective-permute-start(bf16[128,768]{1,0:T(8,128)(2,1)S(1)} %get-tuple-element.69.refs_1_), channel_id=1, source_target_pairs={{0,2},{1,3},{2,0},{3,1},{4,6},{5,7},{6,4},{7,5},{8,10},{9,11},{10,... | collective-permute-start | bytes 589832 | tf_op jit(solution)/shard_map/ppermute | solution.py:42
  97.5 10.5 %collective-permute-start.19 = (bf16[128,768]{1,0:T(8,128)(2,1)S(1)}, bf16[128,768]{1,0:T(8,128)(2,1)S(1)}, u32[]{:S(2)}, u32[]{:S(2)}) collective-permute-start(bf16[128,768]{1,0:T(8,128)(2,1)S(1)} %get-tuple-element.69.refs_1_), channel_id=1, source_target_pairs={{0,3},{1,0},{2,1},{3,2},{4,7},{5,4},{6,5},{7,6},{8,11},{9,8},{10,9... | collective-permute-start | bytes 589832 | tf_op jit(solution)/shard_map/ppermute | solution.py:42
  104.1 12.5 %collective-permute-start.26 = (bf16[128,768]{1,0:T(8,128)(2,1)S(1)}, bf16[128,768]{1,0:T(8,128)(2,1)S(1)}, u32[]{:S(2)}, u32[]{:S(2)}) collective-permute-start(bf16[128,768]{1,0:T(8,128)(2,1)S(1)} %get-tuple-element.58), channel_id=1, source_target_pairs={{0,1},{1,2},{2,3},{3,0},{4,5},{5,6},{6,7},{7,4},{8,9},{9,10},{10,1... | collective-permute-start | bytes 589832 | tf_op jit(solution)/shard_map/ppermute | solution.py:276
  105.5 11.5 %collective-permute-start.27 = (bf16[128,768]{1,0:T(8,128)(2,1)S(1)}, bf16[128,768]{1,0:T(8,128)(2,1)S(1)}, u32[]{:S(2)}, u32[]{:S(2)}) collective-permute-start(bf16[128,768]{1,0:T(8,128)(2,1)S(1)} %get-tuple-element.59), channel_id=1, source_target_pairs={{0,2},{1,3},{2,0},{3,1},{4,6},{5,7},{6,4},{7,5},{8,10},{9,11},{10,... | collective-permute-start | bytes 589832 | tf_op jit(solution)/shard_map/ppermute | solution.py:276
  106.1 10.9 %collective-permute-start.28 = (bf16[128,768]{1,0:T(8,128)(2,1)S(1)}, bf16[128,768]{1,0:T(8,128)(2,1)S(1)}, u32[]{:S(2)}, u32[]{:S(2)}) collective-permute-start(bf16[128,768]{1,0:T(8,128)(2,1)S(1)} %get-tuple-element.60), channel_id=1, source_target_pairs={{0,3},{1,0},{2,1},{3,2},{4,7},{5,4},{6,5},{7,6},{8,11},{9,8},{10,9... | collective-permute-start | bytes 589832 | tf_op jit(solution)/shard_map/ppermute | solution.py:276
  108.0 17.3 %copy-start.4 = (f32[2,128,768]{2,1,0:T(8,128)S(1)}, f32[2,128,768]{2,1,0:T(8,128)}, u32[]{:S(2)}) copy-start(f32[2,128,768]{2,1,0:T(8,128)} %param.6) | copy-start | bytes 2359300
  108.0 17.3 %copy-start.14 = (bf16[128,768]{1,0:T(8,128)(2,1)S(1)}, bf16[128,768]{1,0:T(8,128)(2,1)}, u32[]{:S(2)}) copy-start(bf16[128,768]{1,0:T(8,128)(2,1)} %copy-done.13) | copy-start | bytes 589828
  108.0 20.0 %copy-start.8 = (bf16[128,768]{1,0:T(8,128)(2,1)S(1)}, bf16[128,768]{1,0:T(8,128)(2,1)}, u32[]{:S(2)}) copy-start(bf16[128,768]{1,0:T(8,128)(2,1)} %copy-done.7) | copy-start | bytes 589828
  112.3 23.5 %copy-start.10 = (bf16[64,768]{1,0:T(8,128)(2,1)S(1)}, bf16[64,768]{1,0:T(8,128)(2,1)}, u32[]{:S(2)}) copy-start(bf16[64,768]{1,0:T(8,128)(2,1)} %copy-done.9) | copy-start | bytes 294916
  112.4 23.5 %copy-start.12 = (bf16[64,768]{1,0:T(8,128)(2,1)S(1)}, bf16[64,768]{1,0:T(8,128)(2,1)}, u32[]{:S(2)}) copy-start(bf16[64,768]{1,0:T(8,128)(2,1)} %copy-done.11) | copy-start | bytes 294916
  112.4 23.6 %copy-start.16 = (bf16[64,768]{1,0:T(8,128)(2,1)S(1)}, bf16[64,768]{1,0:T(8,128)(2,1)}, u32[]{:S(2)}) copy-start(bf16[64,768]{1,0:T(8,128)(2,1)} %copy-done.15) | copy-start | bytes 294916
  112.4 31.6 %copy-start.18 = (bf16[64,768]{1,0:T(8,128)(2,1)S(1)}, bf16[64,768]{1,0:T(8,128)(2,1)}, u32[]{:S(2)}) copy-start(bf16[64,768]{1,0:T(8,128)(2,1)} %copy-done.17) | copy-start | bytes 294916
  112.4 31.6 %copy-start.20 = (bf16[64,768]{1,0:T(8,128)(2,1)S(1)}, bf16[64,768]{1,0:T(8,128)(2,1)}, u32[]{:S(2)}) copy-start(bf16[64,768]{1,0:T(8,128)(2,1)} %copy-done.19) | copy-start | bytes 294916
  112.4 31.6 %copy-start.22 = (bf16[64,768]{1,0:T(8,128)(2,1)S(1)}, bf16[64,768]{1,0:T(8,128)(2,1)}, u32[]{:S(2)}) copy-start(bf16[64,768]{1,0:T(8,128)(2,1)} %copy-done.21) | copy-start | bytes 294916
  112.4 31.6 %copy-start.24 = (bf16[64,768]{1,0:T(8,128)(2,1)S(1)}, bf16[64,768]{1,0:T(8,128)(2,1)}, u32[]{:S(2)}) copy-start(bf16[64,768]{1,0:T(8,128)(2,1)} %copy-done.23) | copy-start | bytes 294916
  112.4 6.1 %collective-permute-start.23 = (bf16[128,768]{1,0:T(8,128)(2,1)S(1)}, bf16[128,768]{1,0:T(8,128)(2,1)S(1)}, u32[]{:S(2)}, u32[]{:S(2)}) collective-permute-start(bf16[128,768]{1,0:T(8,128)(2,1)S(1)} %get-tuple-element.54), channel_id=1, source_target_pairs={{0,1},{1,2},{2,3},{3,0},{4,5},{5,6},{6,7},{7,4},{8,9},{9,10},{10,1... | collective-permute-start | bytes 589832 | tf_op jit(solution)/shard_map/ppermute | solution.py:276
  114.5 10.7 %collective-permute-start.24 = (bf16[128,768]{1,0:T(8,128)(2,1)S(1)}, bf16[128,768]{1,0:T(8,128)(2,1)S(1)}, u32[]{:S(2)}, u32[]{:S(2)}) collective-permute-start(bf16[128,768]{1,0:T(8,128)(2,1)S(1)} %get-tuple-element.55), channel_id=1, source_target_pairs={{0,2},{1,3},{2,0},{3,1},{4,6},{5,7},{6,4},{7,5},{8,10},{9,11},{10,... | collective-permute-start | bytes 589832 | tf_op jit(solution)/shard_map/ppermute | solution.py:276
  116.6 8.6 %collective-permute-start.25 = (bf16[128,768]{1,0:T(8,128)(2,1)S(1)}, bf16[128,768]{1,0:T(8,128)(2,1)S(1)}, u32[]{:S(2)}, u32[]{:S(2)}) collective-permute-start(bf16[128,768]{1,0:T(8,128)(2,1)S(1)} %get-tuple-element.56), channel_id=1, source_target_pairs={{0,3},{1,0},{2,1},{3,2},{4,7},{5,4},{6,5},{7,6},{8,11},{9,8},{10,9... | collective-permute-start | bytes 589832 | tf_op jit(solution)/shard_map/ppermute | solution.py:276
  125.4 2.7 %collective-permute-start.29 = (bf16[128,768]{1,0:T(8,128)(2,1)S(1)}, bf16[128,768]{1,0:T(8,128)(2,1)S(1)}, u32[]{:S(2)}, u32[]{:S(2)}) collective-permute-start(bf16[128,768]{1,0:T(8,128)(2,1)S(1)} %subtract_convert_fusion), channel_id=1, source_target_pairs={{0,4},{4,0},{8,12},{12,8},{16,20},{20,16},{24,28},{28,24},{32,36},... | collective-permute-start | bytes 589832 | tf_op jit(solution)/shard_map/ppermute | solution.py:285
  128.2 5.3 %collective-permute-start.30 = (bf16[64,768]{1,0:T(8,128)(2,1)S(1)}, bf16[64,768]{1,0:T(8,128)(2,1)S(1)}, u32[]{:S(2)}, u32[]{:S(2)}) collective-permute-start(bf16[64,768]{1,0:T(8,128)(2,1)S(1)} %subtract_convert_fusion.3), channel_id=1, source_target_pairs={{0,8},{4,12},{8,16},{12,20},{16,24},{20,28},{24,0},{28,4},{32,40},... | collective-permute-start | bytes 294920 | tf_op jit(solution)/shard_map/ppermute | solution.py:285
  128.5 7.1 %collective-permute-start.31 = (bf16[64,768]{1,0:T(8,128)(2,1)S(1)}, bf16[64,768]{1,0:T(8,128)(2,1)S(1)}, u32[]{:S(2)}, u32[]{:S(2)}) collective-permute-start(bf16[64,768]{1,0:T(8,128)(2,1)S(1)} %subtract_convert_fusion.3), channel_id=1, source_target_pairs={{0,16},{4,20},{8,24},{12,28},{16,0},{20,4},{24,8},{28,12},{32,48},... | collective-permute-start | bytes 294920 | tf_op jit(solution)/shard_map/ppermute | solution.py:285
  131.0 4.8 %collective-permute-start.32 = (bf16[64,768]{1,0:T(8,128)(2,1)S(1)}, bf16[64,768]{1,0:T(8,128)(2,1)S(1)}, u32[]{:S(2)}, u32[]{:S(2)}) collective-permute-start(bf16[64,768]{1,0:T(8,128)(2,1)S(1)} %subtract_convert_fusion.3), channel_id=1, source_target_pairs={{0,24},{4,28},{8,0},{12,4},{16,8},{20,12},{24,16},{28,20},{32,56},... | collective-permute-start | bytes 294920 | tf_op jit(solution)/shard_map/ppermute | solution.py:285
  136.0 4.7 %collective-permute-start.33 = (bf16[64,768]{1,0:T(8,128)(2,1)S(1)}, bf16[64,768]{1,0:T(8,128)(2,1)S(1)}, u32[]{:S(2)}, u32[]{:S(2)}) collective-permute-start(bf16[64,768]{1,0:T(8,128)(2,1)S(1)} %subtract_convert_fusion.2), channel_id=1, source_target_pairs={{0,32},{4,36},{8,40},{12,44},{16,48},{20,52},{24,56},{28,60},{32,6... | collective-permute-start | bytes 294920 | tf_op jit(solution)/shard_map/ppermute | solution.py:285
  136.4 6.3 %collective-permute-start.34 = (bf16[64,768]{1,0:T(8,128)(2,1)S(1)}, bf16[64,768]{1,0:T(8,128)(2,1)S(1)}, u32[]{:S(2)}, u32[]{:S(2)}) collective-permute-start(bf16[64,768]{1,0:T(8,128)(2,1)S(1)} %subtract_convert_fusion.2), channel_id=1, source_target_pairs={{0,64},{4,68},{8,72},{12,76},{16,80},{20,84},{24,88},{28,92},{32,9... | collective-permute-start | bytes 294920 | tf_op jit(solution)/shard_map/ppermute | solution.py:285
  139.6 4.4 %collective-permute-start.35 = (bf16[64,768]{1,0:T(8,128)(2,1)S(1)}, bf16[64,768]{1,0:T(8,128)(2,1)S(1)}, u32[]{:S(2)}, u32[]{:S(2)}) collective-permute-start(bf16[64,768]{1,0:T(8,128)(2,1)S(1)} %subtract_convert_fusion.2), channel_id=1, source_target_pairs={{0,96},{4,100},{8,104},{12,108},{16,112},{20,116},{24,120},{28,124... | collective-permute-start | bytes 294920 | tf_op jit(solution)/shard_map/ppermute | solution.py:285
  144.3 3.3 %collective-permute-start.36 = (bf16[64,768]{1,0:T(8,128)(2,1)S(1)}, bf16[64,768]{1,0:T(8,128)(2,1)S(1)}, u32[]{:S(2)}, u32[]{:S(2)}) collective-permute-start(bf16[64,768]{1,0:T(8,128)(2,1)S(1)} %get-tuple-element.65), channel_id=1, source_target_pairs={{0,4},{4,0},{8,12},{12,8},{16,20},{20,16},{24,28},{28,24},{32,36},... | collective-permute-start | bytes 294920 | tf_op jit(solution)/shard_map/ppermute | solution.py:285

commit v4 on v3

--- a/solution.py
+++ b/solution.py
@@ -10,8 +10,9 @@
 HD = 128
 FREQ = 256
 EXTRA = 8
-LIMIT = 48
+LIMIT = 30
 ROOM = 28
+WAIT = 10**10
 LEVELS = 320
 NX, NZ, NC, NY = 4, 4, 2, 4
 BF = jnp.bfloat16
@@ -73,6 +74,7 @@
         in_specs=[smem, vmem, vmem],
         out_specs=vmem,
         compiler_params=pltpu.CompilerParams(vmem_limit_bytes=8 * 2**20),
+        cost_estimate=pl.CostEstimate(flops=WAIT, bytes_accessed=10**6, transcendentals=0),
         name="modulation",
     )(facts, all_gaps, mod_weight)
 
@@ -133,12 +135,8 @@
 
 
 def both_body(tok, cols, facts, *refs):
-    states, mods, qkv_hbm, out_hbm = refs[:4], refs[4], refs[5], refs[6]
-    tots, ins, (start_ref, nrm, qkv, att, wv, wo, sems) = refs[7:11], refs[11:15], refs[15:]
-    copies = [pltpu.make_async_copy(qkv_hbm.at[p], wv.at[p], sems.at[p]) for p in range(3)]
-    copies.append(pltpu.make_async_copy(out_hbm, wo, sems.at[3]))
-    for copy in copies:
-        copy.start()
+    states, mods, wv, wo = refs[:4], refs[4], refs[5], refs[6]
+    tots, ins, (start_ref, nrm, qkv, att) = refs[7:11], refs[11:15], refs[15:]
     me = facts[1]
     centres = [jnp.transpose(states[k][2 * tok :, : 2 * tok].astype(F32))[:, 0:1] for k in range(NY)]
     for s in range(2):
@@ -147,8 +145,7 @@
         mean = normalise(parts, s, s * tok, tok, cols, me, mods, nrm)
         if s == 0:
             start_ref[...] = parts[0] - mean
-    attend(2, tok, cols, nrm, wv, qkv, att, lambda p: copies[p].wait())
-    copies[3].wait()
+    attend(2, tok, cols, nrm, wv, qkv, att, lambda p: None)
     neg = [-(facts[3 + s].astype(F32) / LEVELS) for s in range(2)]
     for k in (1, 2, 3, 0):
         dst = lax.rem(me + k, NY)
@@ -204,15 +201,14 @@
 def both(facts, states, mods, qkv_weight, out_weight):
     cols, _ = out_weight.shape
     tok = (states[0].shape[0] - EXTRA) // 2
-    vmem, smem, hbm = specs()
+    vmem, smem, _ = specs()
     shares = share_shapes(tok, cols)
     made = pl.pallas_call(
         lambda *refs: both_body(tok, cols, *refs),
         out_shape=shares + shares + shares[:1],
-        in_specs=[smem] + [vmem] * 5 + [hbm, hbm],
+        in_specs=[smem] + [vmem] * 7,
         out_specs=[vmem] * 9,
-        scratch_shapes=rows_scratch(2 * tok, cols)
-        + [pltpu.VMEM(qkv_weight.shape, BF), pltpu.VMEM(out_weight.shape, BF), pltpu.SemaphoreType.DMA((4,))],
+        scratch_shapes=rows_scratch(2 * tok, cols),
         compiler_params=pltpu.CompilerParams(vmem_limit_bytes=LIMIT * 2**20),
         cost_estimate=estimate(2, tok, cols),
         name="both",
@@ -236,21 +232,22 @@
     )(facts, *states, mods, *weights, *earlier)
 
 
-def arrive_body(facts, after, wv, wo, out):
+def arrive_body(facts, after, out):
     for i in range(8):
         out[i] = facts[i]
 
 
-def arrive(facts, after, qkv_weight, out_weight):
-    vmem, smem, hbm = specs()
+def arrive(facts, after):
+    _, smem, hbm = specs()
     return pl.pallas_call(
         arrive_body,
         out_shape=jax.ShapeDtypeStruct(facts.shape, facts.dtype),
-        in_specs=[smem, hbm, vmem, vmem],
+        in_specs=[smem, hbm],
         out_specs=smem,
-        compiler_params=pltpu.CompilerParams(vmem_limit_bytes=ROOM * 2**20),
+        compiler_params=pltpu.CompilerParams(vmem_limit_bytes=2**20),
+        cost_estimate=pl.CostEstimate(flops=WAIT, bytes_accessed=1024, transcendentals=0),
         name="arrive",
-    )(facts, after, qkv_weight, out_weight)
+    )(facts, after)
 
 
 def body(trajectory, offset, step_gaps, qkv_weight, out_weight, mod_weight):
@@ -307,7 +304,7 @@
     prefix, other, sent, inc0 = before_me(total + start, (), deliver(ins[0], ins))
     entry = prefix + jnp.where(core == 0, start, other)
     first, second = spread(entry.astype(BF)), spread((entry + inc0).astype(BF))
-    facts = arrive(facts, first[0], *weights)
+    facts = arrive(facts, first[0])
     kept, *ins = one(0, facts, first, mods, weights, [])
     inc0 = deliver(ins[0], ins)
     tots = one(1, facts, second, mods, weights, [kept])

time: 149 us -> 146 us (0.980)
  local copies, waits for them, and re-layouts: 13.1 us -> 6.6 us
  waiting for transfers between devices: 42.7 us -> 47.9 us
  Pallas kernels: 22.4 us -> 19.3 us
    unnamed x50 -> x64, local copies, waits for them, and re-layouts: 10.5 us -> 3.96 us
    ppermute x9, waiting for transfers between devices: 0.02 us -> 4.75 us  [spread(): return [array] + [lax.ppermute(array, 'tp', ring(k)) for k in (1, 2, 3)]]
    pallas_call x1, Pallas kernels: 11.4 us -> 8.41 us  [both(): pl.pallas_call(lambda *refs: both_body(tok, cols, *refs), out_shape=share...]
  transfers between devices with their start and end apart: 38 -> 38, of which waited for: 20 -> 22; matrix products, arithmetic and copies ran while one was open for 2% -> 2% of each run, Pallas kernels for 7% -> 7%
where the time goes in v4:
time: 146 us; the launch traced here: 145 us
  starting transfers between devices  58.1 us (40%)
  waiting for transfers between devices  47.9 us (33%)
  Pallas kernels  19.3 us (13%)
  blocking collectives  7.55 us (5%)
  local copies, waits for them, and re-layouts  6.6 us (5%)
  other arithmetic  4.72 us (3%)
    ppermute x12, waiting for transfers between devices, deliver(): total = total + lax.ppermute(shares[k], 'tp', ring(k)).astype(F32)  23.6 us
    ppermute x16, starting transfers between devices, send(): lax.ppermute(message, 'tm', p).astype(F32) + t  20.7 us
    ppermute x16, waiting for transfers between devices, send(): lax.ppermute(message, 'tm', p).astype(F32) + t  16 us
    ppermute x12, starting transfers between devices, deliver(): total = total + lax.ppermute(shares[k], 'tp', ring(k)).astype(F32)  15.6 us
    ppermute x9, starting transfers between devices, spread(): return [array] + [lax.ppermute(array, 'tp', ring(k)) for k in (1, 2, 3)]  12.4 us
    all_to_all x1, starting transfers between devices, body(): all_gaps = lax.all_to_all(sent, 'tm', 0, 0)  9.44 us
    pallas_call x2, Pallas kernels, one(): pl.pallas_call(lambda *refs: one_body(s, tok, cols, *refs), out_shape=kep...  8.59 us
    pallas_call x1, Pallas kernels, both(): pl.pallas_call(lambda *refs: both_body(tok, cols, *refs), out_shape=share...  8.41 us
  transfers between devices with their start and end apart: 38, of which 22 were waited for; matrix products, arithmetic and copies ran while one was open for 2% of the time, Pallas kernels for 7%

profile of v4, /device:TPU:1, one launch (start us, length us, event | category | flops | bytes accessed | tf_op | source)
XLA Modules:
  0.0 145.5 jit_solution(5783131241639371864)
XLA Ops:
  0.0 1.3 broadcast_in_dim.52
  1.3 1.1 copy-done.1
  2.6 2.2 %collective-permute-start = (bf16[264,768]{1,0:T(8,128)(2,1)S(1)}, bf16[264,768]{1,0:T(8,128)(2,1)S(1)}, u32[]{:S(2)}, u32[]{:S(2)}) collective-permute-start(bf16[264,768]{1,0:T(8,128)(2,1)S(1)} %centre.1.refs_1_), channel_id=1, source_target_pairs={{0,1},{1,2},{2,3},{3,0},{4,5},{5,6},{6,7},{7,4},{8,9},{9,10},{10,1... | collective-permute-start | bytes 1216520 | tf_op jit(solution)/shard_map/ppermute | solution.py:43
  4.7 2.6 %collective-permute-start.1 = (bf16[264,768]{1,0:T(8,128)(2,1)S(1)}, bf16[264,768]{1,0:T(8,128)(2,1)S(1)}, u32[]{:S(2)}, u32[]{:S(2)}) collective-permute-start(bf16[264,768]{1,0:T(8,128)(2,1)S(1)} %centre.1.refs_1_), channel_id=1, source_target_pairs={{0,2},{1,3},{2,0},{3,1},{4,6},{5,7},{6,4},{7,5},{8,10},{9,11},{10,... | collective-permute-start | bytes 1216520 | tf_op jit(solution)/shard_map/ppermute | solution.py:43
  7.4 1.1 collective-permute-start.2
  8.4 9.4 %all-to-all-start = ((s32[32,1,2]{2,1,0:T(1,128)}), s32[32,1,2]{2,1,0:T(1,128)S(1)}, u32[]{:S(2)}, u32[]{:S(2)}) async-start(s32[32,1,2]{2,1,0:T(1,128)} %broadcast_in_dim.52), calls=%async_computation | async-start | bytes 32768 | tf_op jit(solution)/shard_map/all_to_all | solution.py:261
  17.9 1.4 fusion.21
  19.9 1.2 compare_select_fusion.4.facts.refs_0_
  21.2 3.6 %all-to-all-done.all_gaps = s32[32,1,2]{2,1,0:T(1,128)S(1)} async-done(((s32[32,1,2]{2,1,0:T(1,128)}), s32[32,1,2]{2,1,0:T(1,128)S(1)}, u32[]{:S(2)}, u32[]{:S(2)}) %all-to-all-start) | async-done | bytes 288 | tf_op jit(solution)/shard_map/all_to_all | solution.py:261
  24.8 1.3 copy-done.4
  26.0 1.0 modulation.1
  27.0 7.5 %all_to_all.10.refs_5_ = f32[4,8,768]{2,1,0:T(8,128)S(1)} all-to-all(f32[4,8,768]{2,1,0:T(8,128)S(1)} %modulation.1), channel_id=1, replica_groups=mesh['tm'=32,'tp'=4] {'tp'}, dimensions={0} | all-to-all | bytes 196608 | tf_op jit(solution)/shard_map/all_to_all | solution.py:268
  34.6 8.4 %both.1 = (f32[128,768]{1,0:T(8,128)S(1)}, bf16[128,768]{1,0:T(8,128)(2,1)}, bf16[128,768]{1,0:T(8,128)(2,1)}, bf16[128,768]{1,0:T(8,128)(2,1)}, f32[128,768]{1,...) custom-call(s32[8]{0:T(128)S(1)} %compare_select_fusion.4.facts.refs, ...), custom_call_target="tpu_custom_call" | custom-call | flops 4831838208 | bytes 18874368 | tf_op jit(solution)/shard_map/both/pallas_call | solution.py:206
  43.0 0.7 copy-done.3
  43.8 0.7 copy-done.5
  44.8 1.8 %collective-permute-start.4 = (bf16[128,768]{1,0:T(8,128)(2,1)}, bf16[128,768]{1,0:T(8,128)(2,1)S(1)}, u32[]{:S(2)}, u32[]{:S(2)}) collective-permute-start(bf16[128,768]{1,0:T(8,128)(2,1)} %get-tuple-element.38), channel_id=1, source_target_pairs={{0,2},{1,3},{2,0},{3,1},{4,6},{5,7},{6,4},{7,5},{8,10},{9,11},{10,... | collective-permute-start | bytes 589832 | tf_op jit(solution)/shard_map/ppermute | solution.py:273
  46.6 0.9 collective-permute-start.5
  47.5 4.5 %collective-permute-done.3 = bf16[128,768]{1,0:T(8,128)(2,1)S(1)} collective-permute-done((bf16[128,768]{1,0:T(8,128)(2,1)}, bf16[128,768]{1,0:T(8,128)(2,1)S(1)}, u32[]{:S(2)}, u32[]{:S(2)}) %collective-permute-start.3) | collective-permute-done | bytes 196640 | tf_op jit(solution)/shard_map/ppermute | solution.py:273
  52.0 1.8 %collective-permute-done.4 = bf16[128,768]{1,0:T(8,128)(2,1)S(1)} collective-permute-done((bf16[128,768]{1,0:T(8,128)(2,1)}, bf16[128,768]{1,0:T(8,128)(2,1)S(1)}, u32[]{:S(2)}, u32[]{:S(2)}) %collective-permute-start.4) | collective-permute-done | bytes 196640 | tf_op jit(solution)/shard_map/ppermute | solution.py:273
  53.8 2.3 %collective-permute-done.5 = bf16[128,768]{1,0:T(8,128)(2,1)S(1)} collective-permute-done((bf16[128,768]{1,0:T(8,128)(2,1)}, bf16[128,768]{1,0:T(8,128)(2,1)S(1)}, u32[]{:S(2)}, u32[]{:S(2)}) %collective-permute-start.5) | collective-permute-done | bytes 196640 | tf_op jit(solution)/shard_map/ppermute | solution.py:273
  56.2 1.1 convert_add_fusion.5
  57.3 2.0 %collective-permute-start.6 = (bf16[128,768]{1,0:T(8,128)(2,1)S(1)}, bf16[128,768]{1,0:T(8,128)(2,1)S(1)}, u32[]{:S(2)}, u32[]{:S(2)}) collective-permute-start(bf16[128,768]{1,0:T(8,128)(2,1)S(1)} %fusion.15), channel_id=1, source_target_pairs={{0,4},{4,0},{8,12},{12,8},{16,20},{20,16},{24,28},{28,24},{32,36},... | collective-permute-start | bytes 589832 | tf_op jit(solution)/shard_map/ppermute | solution.py:282
  59.6 3.3 %collective-permute-start.11 = (bf16[128,768]{1,0:T(8,128)(2,1)S(1)}, bf16[128,768]{1,0:T(8,128)(2,1)S(1)}, u32[]{:S(2)}, u32[]{:S(2)}) collective-permute-start(bf16[128,768]{1,0:T(8,128)(2,1)S(1)} %get-tuple-element.48), channel_id=1, source_target_pairs={{0,2},{1,3},{2,0},{3,1},{4,6},{5,7},{6,4},{7,5},{8,10},{9,11},{10,... | collective-permute-start | bytes 589832 | tf_op jit(solution)/shard_map/ppermute | solution.py:273
  63.3 1.8 %collective-permute-start.8 = (bf16[64,768]{1,0:T(8,128)(2,1)S(1)}, bf16[64,768]{1,0:T(8,128)(2,1)S(1)}, u32[]{:S(2)}, u32[]{:S(2)}) collective-permute-start(bf16[64,768]{1,0:T(8,128)(2,1)S(1)} %fusion.16), channel_id=1, source_target_pairs={{0,16},{4,20},{8,24},{12,28},{16,0},{20,4},{24,8},{28,12},{32,48},... | collective-permute-start | bytes 294920 | tf_op jit(solution)/shard_map/ppermute | solution.py:282
  65.1 2.0 %collective-permute-done.10 = bf16[128,768]{1,0:T(8,128)(2,1)S(1)} collective-permute-done((bf16[128,768]{1,0:T(8,128)(2,1)}, bf16[128,768]{1,0:T(8,128)(2,1)S(1)}, u32[]{:S(2)}, u32[]{:S(2)}) %collective-permute-start.10) | collective-permute-done | bytes 196640 | tf_op jit(solution)/shard_map/ppermute | solution.py:273
  67.2 0.9 collective-permute-start.9
  68.1 4.2 %collective-permute-done.11 = bf16[128,768]{1,0:T(8,128)(2,1)S(1)} collective-permute-done((bf16[128,768]{1,0:T(8,128)(2,1)S(1)}, bf16[128,768]{1,0:T(8,128)(2,1)S(1)}, u32[]{:S(2)}, u32[]{:S(2)}) %collective-permute-start.11) | collective-permute-done | bytes 196640 | tf_op jit(solution)/shard_map/ppermute | solution.py:273
  72.8 1.7 %collective-permute-start.14 = (bf16[64,768]{1,0:T(8,128)(2,1)S(1)}, bf16[64,768]{1,0:T(8,128)(2,1)S(1)}, u32[]{:S(2)}, u32[]{:S(2)}) collective-permute-start(bf16[64,768]{1,0:T(8,128)(2,1)S(1)} %convert_add_fusion.8), channel_id=1, source_target_pairs={{0,64},{4,68},{8,72},{12,76},{16,80},{20,84},{24,88},{28,92},{32,9... | collective-permute-start | bytes 294920 | tf_op jit(solution)/shard_map/ppermute | solution.py:282
  74.6 1.0 collective-permute-start.15
  75.5 2.5 %collective-permute-done.13 = bf16[64,768]{1,0:T(8,128)(2,1)S(1)} collective-permute-done((bf16[64,768]{1,0:T(8,128)(2,1)S(1)}, bf16[64,768]{1,0:T(8,128)(2,1)S(1)}, u32[]{:S(2)}, u32[]{:S(2)}) %collective-permute-start.13) | collective-permute-done | bytes 98336 | tf_op jit(solution)/shard_map/ppermute | solution.py:282
  78.1 0.7 collective-permute-done.14
  78.8 0.7 collective-permute-done.15
  79.7 2.2 %collective-permute-start.16 = (bf16[64,768]{1,0:T(8,128)(2,1)S(1)}, bf16[64,768]{1,0:T(8,128)(2,1)S(1)}, u32[]{:S(2)}, u32[]{:S(2)}) collective-permute-start(bf16[64,768]{1,0:T(8,128)(2,1)S(1)} %get-tuple-element.67), channel_id=1, source_target_pairs={{0,4},{4,0},{8,12},{12,8},{16,20},{20,16},{24,28},{28,24},{32,36},... | collective-permute-start | bytes 294920 | tf_op jit(solution)/shard_map/ppermute | solution.py:282
  81.8 0.9 collective-permute-done.16
  83.2 3.3 %collective-permute-start.21 = (bf16[128,768]{1,0:T(8,128)(2,1)S(1)}, bf16[128,768]{1,0:T(8,128)(2,1)S(1)}, u32[]{:S(2)}, u32[]{:S(2)}) collective-permute-start(bf16[128,768]{1,0:T(8,128)(2,1)S(1)} %get-tuple-element.70.after.refs_1_), channel_id=1, source_target_pairs={{0,2},{1,3},{2,0},{3,1},{4,6},{5,7},{6,4},{7,5},{8,10},{9,11},{10,... | collective-permute-start | bytes 589832 | tf_op jit(solution)/shard_map/ppermute | solution.py:43
  86.6 1.1 arrive.1.refs_0_
  87.7 1.5 %collective-permute-start.17 = (bf16[128,768]{1,0:T(8,128)(2,1)S(1)}, bf16[128,768]{1,0:T(8,128)(2,1)S(1)}, u32[]{:S(2)}, u32[]{:S(2)}) collective-permute-start(bf16[128,768]{1,0:T(8,128)(2,1)S(1)} %get-tuple-element.69.refs_1_), channel_id=1, source_target_pairs={{0,1},{1,2},{2,3},{3,0},{4,5},{5,6},{6,7},{7,4},{8,9},{9,10},{10,1... | collective-permute-start | bytes 589832 | tf_op jit(solution)/shard_map/ppermute | solution.py:43
  89.4 1.0 collective-permute-done.20.refs_2_
  90.4 1.3 collective-permute-start.19
  91.7 3.7 %collective-permute-done.21.refs_3_ = bf16[128,768]{1,0:T(8,128)(2,1)S(1)} collective-permute-done((bf16[128,768]{1,0:T(8,128)(2,1)S(1)}, bf16[128,768]{1,0:T(8,128)(2,1)S(1)}, u32[]{:S(2)}, u32[]{:S(2)}) %collective-permute-start.21) | collective-permute-done | bytes 196640 | tf_op jit(solution)/shard_map/ppermute | solution.py:43
  95.6 4.3 %one.2 = (f32[4,128,768]{2,1,0:T(8,128)S(1)}, f32[128,768]{1,0:T(8,128)S(1)}, bf16[128,768]{1,0:T(8,128)(2,1)S(1)}, bf16[128,768]{1,0:T(8,128)(2,1)S(1)}, bf16[128,768]{1,0:T(8,128)(2,1)S(1)}) custom-call(s32[8]{0:T(128)S(1)} %arrive.1.refs_0_, bf16[128,768]{1,0:T(8,128)(2,1)S(1)} %get-tuple-element.70.after.refs_1_, ...), custom_call_target="tpu_custom_call" | custom-call | flops 2415919104 | bytes 18874368 | tf_op jit(solution)/shard_map/one/pallas_call | solution.py:223
  99.9 1.1 collective-permute-start.26
  101.0 3.9 %collective-permute-start.27 = (bf16[128,768]{1,0:T(8,128)(2,1)S(1)}, bf16[128,768]{1,0:T(8,128)(2,1)S(1)}, u32[]{:S(2)}, u32[]{:S(2)}) collective-permute-start(bf16[128,768]{1,0:T(8,128)(2,1)S(1)} %get-tuple-element.59), channel_id=1, source_target_pairs={{0,2},{1,3},{2,0},{3,1},{4,6},{5,7},{6,4},{7,5},{8,10},{9,11},{10,... | collective-permute-start | bytes 589832 | tf_op jit(solution)/shard_map/ppermute | solution.py:273
  104.9 4.3 %one.3 = (f32[128,768]{1,0:T(8,128)S(1)}, bf16[128,768]{1,0:T(8,128)(2,1)S(1)}, bf16[128,768]{1,0:T(8,128)(2,1)S(1)}, bf16[128,768]{1,0:T(8,128)(2,1)S(1)}) custom-call(s32[8]{0:T(128)S(1)} %arrive.1.refs_0_, bf16[128,768]{1,0:T(8,128)(2,1)S(1)} %get-tuple-element.69.refs_1_, bf16[128,768]{1,0:T(8,128)(2,1)S(1)} %collective-permute-done.17.refs_2_, ...), custom_call_target="tpu_custom_call" | custom-call | flops 2415919104 | bytes 18874368 | tf_op jit(solution)/shard_map/one/pallas_call | solution.py:223
  109.3 1.5 %collective-permute-start.23 = (bf16[128,768]{1,0:T(8,128)(2,1)S(1)}, bf16[128,768]{1,0:T(8,128)(2,1)S(1)}, u32[]{:S(2)}, u32[]{:S(2)}) collective-permute-start(bf16[128,768]{1,0:T(8,128)(2,1)S(1)} %get-tuple-element.54), channel_id=1, source_target_pairs={{0,1},{1,2},{2,3},{3,0},{4,5},{5,6},{6,7},{7,4},{8,9},{9,10},{10,1... | collective-permute-start | bytes 589832 | tf_op jit(solution)/shard_map/ppermute | solution.py:273
  110.8 1.5 %collective-permute-start.24 = (bf16[128,768]{1,0:T(8,128)(2,1)S(1)}, bf16[128,768]{1,0:T(8,128)(2,1)S(1)}, u32[]{:S(2)}, u32[]{:S(2)}) collective-permute-start(bf16[128,768]{1,0:T(8,128)(2,1)S(1)} %get-tuple-element.55), channel_id=1, source_target_pairs={{0,2},{1,3},{2,0},{3,1},{4,6},{5,7},{6,4},{7,5},{8,10},{9,11},{10,... | collective-permute-start | bytes 589832 | tf_op jit(solution)/shard_map/ppermute | solution.py:273
  112.4 0.9 collective-permute-start.25
  113.4 4.7 %collective-permute-done.23 = bf16[128,768]{1,0:T(8,128)(2,1)S(1)} collective-permute-done((bf16[128,768]{1,0:T(8,128)(2,1)S(1)}, bf16[128,768]{1,0:T(8,128)(2,1)S(1)}, u32[]{:S(2)}, u32[]{:S(2)}) %collective-permute-start.23) | collective-permute-done | bytes 196640 | tf_op jit(solution)/shard_map/ppermute | solution.py:273
  118.1 4.0 %collective-permute-done.24 = bf16[128,768]{1,0:T(8,128)(2,1)S(1)} collective-permute-done((bf16[128,768]{1,0:T(8,128)(2,1)S(1)}, bf16[128,768]{1,0:T(8,128)(2,1)S(1)}, u32[]{:S(2)}, u32[]{:S(2)}) %collective-permute-start.24) | collective-permute-done | bytes 196640 | tf_op jit(solution)/shard_map/ppermute | solution.py:273
  122.3 1.3 collective-permute-start.29
  123.7 1.1 collective-permute-done.29
  125.3 2.0 %collective-permute-start.31 = (bf16[64,768]{1,0:T(8,128)(2,1)S(1)}, bf16[64,768]{1,0:T(8,128)(2,1)S(1)}, u32[]{:S(2)}, u32[]{:S(2)}) collective-permute-start(bf16[64,768]{1,0:T(8,128)(2,1)S(1)} %subtract_convert_fusion.3), channel_id=1, source_target_pairs={{0,16},{4,20},{8,24},{12,28},{16,0},{20,4},{24,8},{28,12},{32,48},... | collective-permute-start | bytes 294920 | tf_op jit(solution)/shard_map/ppermute | solution.py:282
  127.3 0.7 collective-permute-start.32
  128.0 2.6 %collective-permute-done.30 = bf16[64,768]{1,0:T(8,128)(2,1)S(1)} collective-permute-done((bf16[64,768]{1,0:T(8,128)(2,1)S(1)}, bf16[64,768]{1,0:T(8,128)(2,1)S(1)}, u32[]{:S(2)}, u32[]{:S(2)}) %collective-permute-start.30) | collective-permute-done | bytes 98336 | tf_op jit(solution)/shard_map/ppermute | solution.py:282
  130.6 1.4 collective-permute-done.31
  131.9 0.6 collective-permute-done.32
  132.7 0.5 collective-permute-start.33
  133.2 3.2 %collective-permute-start.34 = (bf16[64,768]{1,0:T(8,128)(2,1)S(1)}, bf16[64,768]{1,0:T(8,128)(2,1)S(1)}, u32[]{:S(2)}, u32[]{:S(2)}) collective-permute-start(bf16[64,768]{1,0:T(8,128)(2,1)S(1)} %subtract_convert_fusion.2), channel_id=1, source_target_pairs={{0,64},{4,68},{8,72},{12,76},{16,80},{20,84},{24,88},{28,92},{32,9... | collective-permute-start | bytes 294920 | tf_op jit(solution)/shard_map/ppermute | solution.py:282
  136.4 1.1 collective-permute-done.33
  137.5 2.1 %collective-permute-done.34 = bf16[64,768]{1,0:T(8,128)(2,1)S(1)} collective-permute-done((bf16[64,768]{1,0:T(8,128)(2,1)S(1)}, bf16[64,768]{1,0:T(8,128)(2,1)S(1)}, u32[]{:S(2)}, u32[]{:S(2)}) %collective-permute-start.34) | collective-permute-done | bytes 98336 | tf_op jit(solution)/shard_map/ppermute | solution.py:282
  139.5 1.3 collective-permute-done.35
  141.0 2.4 %collective-permute-start.36 = (bf16[64,768]{1,0:T(8,128)(2,1)S(1)}, bf16[64,768]{1,0:T(8,128)(2,1)S(1)}, u32[]{:S(2)}, u32[]{:S(2)}) collective-permute-start(bf16[64,768]{1,0:T(8,128)(2,1)S(1)} %get-tuple-element.65), channel_id=1, source_target_pairs={{0,4},{4,0},{8,12},{12,8},{16,20},{20,16},{24,28},{28,24},{32,36},... | collective-permute-start | bytes 294920 | tf_op jit(solution)/shard_map/ppermute | solution.py:282
  143.4 0.9 collective-permute-done.36
  144.5 0.9 pad_maximum_fusion
  (110 shorter events, 4.0 us)
Async XLA Ops:
  2.4 32.2 %slice-start.4 = ((s8[4718592]{0:T(1024)(128)(4,1)}), s8[524288]{0:T(1024)(128)(4,1)S(1)}, s32[]{:S(2)}) async-start(s8[4718592]{0:T(1024)(128)(4,1)} %bitcast.26), calls=%async_computation.6 | async-start | bytes 1048576
  2.6 32.0 %collective-permute-start = (bf16[264,768]{1,0:T(8,128)(2,1)S(1)}, bf16[264,768]{1,0:T(8,128)(2,1)S(1)}, u32[]{:S(2)}, u32[]{:S(2)}) collective-permute-start(bf16[264,768]{1,0:T(8,128)(2,1)S(1)} %centre.1.refs_1_), channel_id=1, source_target_pairs={{0,1},{1,2},{2,3},{3,0},{4,5},{5,6},{6,7},{7,4},{8,9},{9,10},{10,1... | collective-permute-start | bytes 1216520 | tf_op jit(solution)/shard_map/ppermute | solution.py:43
  4.7 29.8 %collective-permute-start.1 = (bf16[264,768]{1,0:T(8,128)(2,1)S(1)}, bf16[264,768]{1,0:T(8,128)(2,1)S(1)}, u32[]{:S(2)}, u32[]{:S(2)}) collective-permute-start(bf16[264,768]{1,0:T(8,128)(2,1)S(1)} %centre.1.refs_1_), channel_id=1, source_target_pairs={{0,2},{1,3},{2,0},{3,1},{4,6},{5,7},{6,4},{7,5},{8,10},{9,11},{10,... | collective-permute-start | bytes 1216520 | tf_op jit(solution)/shard_map/ppermute | solution.py:43
  7.4 27.2 %collective-permute-start.2 = (bf16[264,768]{1,0:T(8,128)(2,1)S(1)}, bf16[264,768]{1,0:T(8,128)(2,1)S(1)}, u32[]{:S(2)}, u32[]{:S(2)}) collective-permute-start(bf16[264,768]{1,0:T(8,128)(2,1)S(1)} %centre.1.refs_1_), channel_id=1, source_target_pairs={{0,3},{1,0},{2,1},{3,2},{4,7},{5,4},{6,5},{7,6},{8,11},{9,8},{10,9... | collective-permute-start | bytes 1216520 | tf_op jit(solution)/shard_map/ppermute | solution.py:43
  8.4 16.3 %all-to-all-start = ((s32[32,1,2]{2,1,0:T(1,128)}), s32[32,1,2]{2,1,0:T(1,128)S(1)}, u32[]{:S(2)}, u32[]{:S(2)}) async-start(s32[32,1,2]{2,1,0:T(1,128)} %broadcast_in_dim.52), calls=%async_computation | async-start | bytes 32768 | tf_op jit(solution)/shard_map/all_to_all | solution.py:261
  26.0 8.6 %copy-start = (bf16[3072,3,768]{2,0,1:T(8,128)(2,1)S(1)}, bf16[3072,3,768]{2,0,1:T(8,128)(2,1)}, u32[]{:S(2)}) copy-start(bf16[3072,3,768]{2,0,1:T(8,128)(2,1)} %param.9) | copy-start | bytes 42467332
  26.0 8.6 %slice-start.5 = ((s8[4718592]{0:T(1024)(128)(4,1)}), s8[4194304]{0:T(1024)(128)(4,1)S(1)}, s32[]{:S(2)}) async-start(s8[4718592]{0:T(1024)(128)(4,1)} %bitcast.26), calls=%async_computation.7 | async-start | bytes 8388608
  44.5 7.5 %collective-permute-start.3 = (bf16[128,768]{1,0:T(8,128)(2,1)}, bf16[128,768]{1,0:T(8,128)(2,1)S(1)}, u32[]{:S(2)}, u32[]{:S(2)}) collective-permute-start(bf16[128,768]{1,0:T(8,128)(2,1)} %get-tuple-element.37), channel_id=1, source_target_pairs={{0,1},{1,2},{2,3},{3,0},{4,5},{5,6},{6,7},{7,4},{8,9},{9,10},{10,1... | collective-permute-start | bytes 589832 | tf_op jit(solution)/shard_map/ppermute | solution.py:273
  44.8 9.1 %collective-permute-start.4 = (bf16[128,768]{1,0:T(8,128)(2,1)}, bf16[128,768]{1,0:T(8,128)(2,1)S(1)}, u32[]{:S(2)}, u32[]{:S(2)}) collective-permute-start(bf16[128,768]{1,0:T(8,128)(2,1)} %get-tuple-element.38), channel_id=1, source_target_pairs={{0,2},{1,3},{2,0},{3,1},{4,6},{5,7},{6,4},{7,5},{8,10},{9,11},{10,... | collective-permute-start | bytes 589832 | tf_op jit(solution)/shard_map/ppermute | solution.py:273
  46.6 9.6 %collective-permute-start.5 = (bf16[128,768]{1,0:T(8,128)(2,1)}, bf16[128,768]{1,0:T(8,128)(2,1)S(1)}, u32[]{:S(2)}, u32[]{:S(2)}) collective-permute-start(bf16[128,768]{1,0:T(8,128)(2,1)} %get-tuple-element.39), channel_id=1, source_target_pairs={{0,3},{1,0},{2,1},{3,2},{4,7},{5,4},{6,5},{7,6},{8,11},{9,8},{10,9... | collective-permute-start | bytes 589832 | tf_op jit(solution)/shard_map/ppermute | solution.py:273
  57.3 5.6 %copy-start.14 = (bf16[128,768]{1,0:T(8,128)(2,1)}, bf16[128,768]{1,0:T(8,128)(2,1)S(1)}, u32[]{:S(2)}) copy-start(bf16[128,768]{1,0:T(8,128)(2,1)S(1)} %fusion.15) | copy-start | bytes 589828
  57.3 5.5 %collective-permute-start.6 = (bf16[128,768]{1,0:T(8,128)(2,1)S(1)}, bf16[128,768]{1,0:T(8,128)(2,1)S(1)}, u32[]{:S(2)}, u32[]{:S(2)}) collective-permute-start(bf16[128,768]{1,0:T(8,128)(2,1)S(1)} %fusion.15), channel_id=1, source_target_pairs={{0,4},{4,0},{8,12},{12,8},{16,20},{20,16},{24,28},{28,24},{32,36},... | collective-permute-start | bytes 589832 | tf_op jit(solution)/shard_map/ppermute | solution.py:282
  59.3 7.9 %collective-permute-start.10 = (bf16[128,768]{1,0:T(8,128)(2,1)}, bf16[128,768]{1,0:T(8,128)(2,1)S(1)}, u32[]{:S(2)}, u32[]{:S(2)}) collective-permute-start(bf16[128,768]{1,0:T(8,128)(2,1)} %copy-done.5), channel_id=1, source_target_pairs={{0,1},{1,2},{2,3},{3,0},{4,5},{5,6},{6,7},{7,4},{8,9},{9,10},{10,1... | collective-permute-start | bytes 589832 | tf_op jit(solution)/shard_map/ppermute | solution.py:273
  59.6 12.7 %collective-permute-start.11 = (bf16[128,768]{1,0:T(8,128)(2,1)S(1)}, bf16[128,768]{1,0:T(8,128)(2,1)S(1)}, u32[]{:S(2)}, u32[]{:S(2)}) collective-permute-start(bf16[128,768]{1,0:T(8,128)(2,1)S(1)} %get-tuple-element.48), channel_id=1, source_target_pairs={{0,2},{1,3},{2,0},{3,1},{4,6},{5,7},{6,4},{7,5},{8,10},{9,11},{10,... | collective-permute-start | bytes 589832 | tf_op jit(solution)/shard_map/ppermute | solution.py:273
  62.8 9.4 %collective-permute-start.12 = (bf16[128,768]{1,0:T(8,128)(2,1)S(1)}, bf16[128,768]{1,0:T(8,128)(2,1)S(1)}, u32[]{:S(2)}, u32[]{:S(2)}) collective-permute-start(bf16[128,768]{1,0:T(8,128)(2,1)S(1)} %get-tuple-element.49), channel_id=1, source_target_pairs={{0,3},{1,0},{2,1},{3,2},{4,7},{5,4},{6,5},{7,6},{8,11},{9,8},{10,9... | collective-permute-start | bytes 589832 | tf_op jit(solution)/shard_map/ppermute | solution.py:273
  62.8 20.1 %copy-start.8 = (bf16[128,768]{1,0:T(8,128)(2,1)}, bf16[128,768]{1,0:T(8,128)(2,1)S(1)}, u32[]{:S(2)}) copy-start(bf16[128,768]{1,0:T(8,128)(2,1)S(1)} %collective-permute-done.6) | copy-start | bytes 589828
  62.9 20.0 %copy-start.6 = (f32[128,768]{1,0:T(8,128)}, f32[128,768]{1,0:T(8,128)S(1)}, u32[]{:S(2)}) copy-start(f32[128,768]{1,0:T(8,128)S(1)} %convert_add_fusion.1) | copy-start | bytes 1179652
  63.0 9.4 %collective-permute-start.7 = (bf16[64,768]{1,0:T(8,128)(2,1)S(1)}, bf16[64,768]{1,0:T(8,128)(2,1)S(1)}, u32[]{:S(2)}, u32[]{:S(2)}) collective-permute-start(bf16[64,768]{1,0:T(8,128)(2,1)S(1)} %fusion.16), channel_id=1, source_target_pairs={{0,8},{4,12},{8,16},{12,20},{16,24},{20,28},{24,0},{28,4},{32,40},... | collective-permute-start | bytes 294920 | tf_op jit(solution)/shard_map/ppermute | solution.py:282
  63.3 9.0 %collective-permute-start.8 = (bf16[64,768]{1,0:T(8,128)(2,1)S(1)}, bf16[64,768]{1,0:T(8,128)(2,1)S(1)}, u32[]{:S(2)}, u32[]{:S(2)}) collective-permute-start(bf16[64,768]{1,0:T(8,128)(2,1)S(1)} %fusion.16), channel_id=1, source_target_pairs={{0,16},{4,20},{8,24},{12,28},{16,0},{20,4},{24,8},{28,12},{32,48},... | collective-permute-start | bytes 294920 | tf_op jit(solution)/shard_map/ppermute | solution.py:282
  67.2 5.2 %collective-permute-start.9 = (bf16[64,768]{1,0:T(8,128)(2,1)S(1)}, bf16[64,768]{1,0:T(8,128)(2,1)S(1)}, u32[]{:S(2)}, u32[]{:S(2)}) collective-permute-start(bf16[64,768]{1,0:T(8,128)(2,1)S(1)} %fusion.16), channel_id=1, source_target_pairs={{0,24},{4,28},{8,0},{12,4},{16,8},{20,12},{24,16},{28,20},{32,56},... | collective-permute-start | bytes 294920 | tf_op jit(solution)/shard_map/ppermute | solution.py:282
  72.3 10.6 %copy-start.10 = (bf16[64,768]{1,0:T(8,128)(2,1)}, bf16[64,768]{1,0:T(8,128)(2,1)S(1)}, u32[]{:S(2)}) copy-start(bf16[64,768]{1,0:T(8,128)(2,1)S(1)} %collective-permute-done.8) | copy-start | bytes 294916
  72.3 10.6 %copy-start.12 = (bf16[64,768]{1,0:T(8,128)(2,1)}, bf16[64,768]{1,0:T(8,128)(2,1)S(1)}, u32[]{:S(2)}) copy-start(bf16[64,768]{1,0:T(8,128)(2,1)S(1)} %collective-permute-done.9) | copy-start | bytes 294916
  72.4 10.5 %copy-start.16 = (bf16[64,768]{1,0:T(8,128)(2,1)}, bf16[64,768]{1,0:T(8,128)(2,1)S(1)}, u32[]{:S(2)}) copy-start(bf16[64,768]{1,0:T(8,128)(2,1)S(1)} %convert_add_fusion.8) | copy-start | bytes 294916
  72.4 5.7 %collective-permute-start.13 = (bf16[64,768]{1,0:T(8,128)(2,1)S(1)}, bf16[64,768]{1,0:T(8,128)(2,1)S(1)}, u32[]{:S(2)}, u32[]{:S(2)}) collective-permute-start(bf16[64,768]{1,0:T(8,128)(2,1)S(1)} %convert_add_fusion.8), channel_id=1, source_target_pairs={{0,32},{4,36},{8,40},{12,44},{16,48},{20,52},{24,56},{28,60},{32,6... | collective-permute-start | bytes 294920 | tf_op jit(solution)/shard_map/ppermute | solution.py:282
  72.8 6.0 %collective-permute-start.14 = (bf16[64,768]{1,0:T(8,128)(2,1)S(1)}, bf16[64,768]{1,0:T(8,128)(2,1)S(1)}, u32[]{:S(2)}, u32[]{:S(2)}) collective-permute-start(bf16[64,768]{1,0:T(8,128)(2,1)S(1)} %convert_add_fusion.8), channel_id=1, source_target_pairs={{0,64},{4,68},{8,72},{12,76},{16,80},{20,84},{24,88},{28,92},{32,9... | collective-permute-start | bytes 294920 | tf_op jit(solution)/shard_map/ppermute | solution.py:282
  74.6 5.0 %collective-permute-start.15 = (bf16[64,768]{1,0:T(8,128)(2,1)S(1)}, bf16[64,768]{1,0:T(8,128)(2,1)S(1)}, u32[]{:S(2)}, u32[]{:S(2)}) collective-permute-start(bf16[64,768]{1,0:T(8,128)(2,1)S(1)} %convert_add_fusion.8), channel_id=1, source_target_pairs={{0,96},{4,100},{8,104},{12,108},{16,112},{20,116},{24,120},{28,124... | collective-permute-start | bytes 294920 | tf_op jit(solution)/shard_map/ppermute | solution.py:282
  78.1 4.7 %copy-start.18 = (bf16[64,768]{1,0:T(8,128)(2,1)}, bf16[64,768]{1,0:T(8,128)(2,1)S(1)}, u32[]{:S(2)}) copy-start(bf16[64,768]{1,0:T(8,128)(2,1)S(1)} %collective-permute-done.13) | copy-start | bytes 294916
  79.7 3.1 %collective-permute-start.16 = (bf16[64,768]{1,0:T(8,128)(2,1)S(1)}, bf16[64,768]{1,0:T(8,128)(2,1)S(1)}, u32[]{:S(2)}, u32[]{:S(2)}) collective-permute-start(bf16[64,768]{1,0:T(8,128)(2,1)S(1)} %get-tuple-element.67), channel_id=1, source_target_pairs={{0,4},{4,0},{8,12},{12,8},{16,20},{20,16},{24,28},{28,24},{32,36},... | collective-permute-start | bytes 294920 | tf_op jit(solution)/shard_map/ppermute | solution.py:282
  83.0 12.5 %slice-start = ((s8[14155776]{0:T(1024)(128)(4,1)}), s8[4194304]{0:T(1024)(128)(4,1)S(1)}, s32[]{:S(2)}) async-start(s8[14155776]{0:T(1024)(128)(4,1)} %bitcast.22), calls=%async_computation.2 | async-start | bytes 8388608
  83.0 12.5 %slice-start.6 = ((s8[4718592]{0:T(1024)(128)(4,1)}), s8[4194304]{0:T(1024)(128)(4,1)S(1)}, s32[]{:S(2)}) async-start(s8[4718592]{0:T(1024)(128)(4,1)} %bitcast.28), calls=%async_computation.8 | async-start | bytes 8388608
  83.0 12.5 %slice-start.1 = ((s8[14155776]{0:T(1024)(128)(4,1)}), s8[4194304]{0:T(1024)(128)(4,1)S(1)}, s32[]{:S(2)}) async-start(s8[14155776]{0:T(1024)(128)(4,1)} %bitcast.22), calls=%async_computation.3 | async-start | bytes 8388608
  83.0 12.5 %slice-start.2 = ((s8[14155776]{0:T(1024)(128)(4,1)}), s8[4194304]{0:T(1024)(128)(4,1)S(1)}, s32[]{:S(2)}) async-start(s8[14155776]{0:T(1024)(128)(4,1)} %bitcast.22), calls=%async_computation.4 | async-start | bytes 8388608
  83.0 12.5 %slice-start.3 = ((s8[14155776]{0:T(1024)(128)(4,1)}), s8[1572864]{0:T(1024)(128)(4,1)S(1)}, s32[]{:S(2)}) async-start(s8[14155776]{0:T(1024)(128)(4,1)} %bitcast.22), calls=%async_computation.5 | async-start | bytes 3145728
  83.0 12.5 %slice-start.7 = ((s8[4718592]{0:T(1024)(128)(4,1)}), s8[524288]{0:T(1024)(128)(4,1)S(1)}, s32[]{:S(2)}) async-start(s8[4718592]{0:T(1024)(128)(4,1)} %bitcast.28), calls=%async_computation.9 | async-start | bytes 1048576
  83.0 7.4 %collective-permute-start.20 = (bf16[128,768]{1,0:T(8,128)(2,1)S(1)}, bf16[128,768]{1,0:T(8,128)(2,1)S(1)}, u32[]{:S(2)}, u32[]{:S(2)}) collective-permute-start(bf16[128,768]{1,0:T(8,128)(2,1)S(1)} %get-tuple-element.70.after.refs_1_), channel_id=1, source_target_pairs={{0,1},{1,2},{2,3},{3,0},{4,5},{5,6},{6,7},{7,4},{8,9},{9,10},{10,1... | collective-permute-start | bytes 589832 | tf_op jit(solution)/shard_map/ppermute | solution.py:43
  83.2 12.2 %collective-permute-start.21 = (bf16[128,768]{1,0:T(8,128)(2,1)S(1)}, bf16[128,768]{1,0:T(8,128)(2,1)S(1)}, u32[]{:S(2)}, u32[]{:S(2)}) collective-permute-start(bf16[128,768]{1,0:T(8,128)(2,1)S(1)} %get-tuple-element.70.after.refs_1_), channel_id=1, source_target_pairs={{0,2},{1,3},{2,0},{3,1},{4,6},{5,7},{6,4},{7,5},{8,10},{9,11},{10,... | collective-permute-start | bytes 589832 | tf_op jit(solution)/shard_map/ppermute | solution.py:43
  86.6 8.9 %collective-permute-start.22 = (bf16[128,768]{1,0:T(8,128)(2,1)S(1)}, bf16[128,768]{1,0:T(8,128)(2,1)S(1)}, u32[]{:S(2)}, u32[]{:S(2)}) collective-permute-start(bf16[128,768]{1,0:T(8,128)(2,1)S(1)} %get-tuple-element.70.after.refs_1_), channel_id=1, source_target_pairs={{0,3},{1,0},{2,1},{3,2},{4,7},{5,4},{6,5},{7,6},{8,11},{9,8},{10,9... | collective-permute-start | bytes 589832 | tf_op jit(solution)/shard_map/ppermute | solution.py:43
  87.7 17.2 %collective-permute-start.17 = (bf16[128,768]{1,0:T(8,128)(2,1)S(1)}, bf16[128,768]{1,0:T(8,128)(2,1)S(1)}, u32[]{:S(2)}, u32[]{:S(2)}) collective-permute-start(bf16[128,768]{1,0:T(8,128)(2,1)S(1)} %get-tuple-element.69.refs_1_), channel_id=1, source_target_pairs={{0,1},{1,2},{2,3},{3,0},{4,5},{5,6},{6,7},{7,4},{8,9},{9,10},{10,1... | collective-permute-start | bytes 589832 | tf_op jit(solution)/shard_map/ppermute | solution.py:43
  89.3 15.6 %collective-permute-start.18 = (bf16[128,768]{1,0:T(8,128)(2,1)S(1)}, bf16[128,768]{1,0:T(8,128)(2,1)S(1)}, u32[]{:S(2)}, u32[]{:S(2)}) collective-permute-start(bf16[128,768]{1,0:T(8,128)(2,1)S(1)} %get-tuple-element.69.refs_1_), channel_id=1, source_target_pairs={{0,2},{1,3},{2,0},{3,1},{4,6},{5,7},{6,4},{7,5},{8,10},{9,11},{10,... | collective-permute-start | bytes 589832 | tf_op jit(solution)/shard_map/ppermute | solution.py:43
  90.4 14.5 %collective-permute-start.19 = (bf16[128,768]{1,0:T(8,128)(2,1)S(1)}, bf16[128,768]{1,0:T(8,128)(2,1)S(1)}, u32[]{:S(2)}, u32[]{:S(2)}) collective-permute-start(bf16[128,768]{1,0:T(8,128)(2,1)S(1)} %get-tuple-element.69.refs_1_), channel_id=1, source_target_pairs={{0,3},{1,0},{2,1},{3,2},{4,7},{5,4},{6,5},{7,6},{8,11},{9,8},{10,9... | collective-permute-start | bytes 589832 | tf_op jit(solution)/shard_map/ppermute | solution.py:43
  99.9 12.6 %collective-permute-start.26 = (bf16[128,768]{1,0:T(8,128)(2,1)S(1)}, bf16[128,768]{1,0:T(8,128)(2,1)S(1)}, u32[]{:S(2)}, u32[]{:S(2)}) collective-permute-start(bf16[128,768]{1,0:T(8,128)(2,1)S(1)} %get-tuple-element.58), channel_id=1, source_target_pairs={{0,1},{1,2},{2,3},{3,0},{4,5},{5,6},{6,7},{7,4},{8,9},{9,10},{10,1... | collective-permute-start | bytes 589832 | tf_op jit(solution)/shard_map/ppermute | solution.py:273
  101.0 12.4 %collective-permute-start.27 = (bf16[128,768]{1,0:T(8,128)(2,1)S(1)}, bf16[128,768]{1,0:T(8,128)(2,1)S(1)}, u32[]{:S(2)}, u32[]{:S(2)}) collective-permute-start(bf16[128,768]{1,0:T(8,128)(2,1)S(1)} %get-tuple-element.59), channel_id=1, source_target_pairs={{0,2},{1,3},{2,0},{3,1},{4,6},{5,7},{6,4},{7,5},{8,10},{9,11},{10,... | collective-permute-start | bytes 589832 | tf_op jit(solution)/shard_map/ppermute | solution.py:273
  104.9 8.4 %collective-permute-start.28 = (bf16[128,768]{1,0:T(8,128)(2,1)S(1)}, bf16[128,768]{1,0:T(8,128)(2,1)S(1)}, u32[]{:S(2)}, u32[]{:S(2)}) collective-permute-start(bf16[128,768]{1,0:T(8,128)(2,1)S(1)} %get-tuple-element.60), channel_id=1, source_target_pairs={{0,3},{1,0},{2,1},{3,2},{4,7},{5,4},{6,5},{7,6},{8,11},{9,8},{10,9... | collective-permute-start | bytes 589832 | tf_op jit(solution)/shard_map/ppermute | solution.py:273
  104.9 17.3 %copy-start.2 = (f32[2,128,768]{2,1,0:T(8,128)S(1)}, f32[2,128,768]{2,1,0:T(8,128)}, u32[]{:S(2)}) copy-start(f32[2,128,768]{2,1,0:T(8,128)} %param.6) | copy-start | bytes 2359300
  104.9 17.3 %copy-start.15 = (bf16[128,768]{1,0:T(8,128)(2,1)S(1)}, bf16[128,768]{1,0:T(8,128)(2,1)}, u32[]{:S(2)}) copy-start(bf16[128,768]{1,0:T(8,128)(2,1)} %copy-done.14) | copy-start | bytes 589828
  104.9 19.8 %copy-start.9 = (bf16[128,768]{1,0:T(8,128)(2,1)S(1)}, bf16[128,768]{1,0:T(8,128)(2,1)}, u32[]{:S(2)}) copy-start(bf16[128,768]{1,0:T(8,128)(2,1)} %copy-done.8) | copy-start | bytes 589828
  109.3 15.6 %copy-start.7 = (f32[128,768]{1,0:T(8,128)S(1)}, f32[128,768]{1,0:T(8,128)}, u32[]{:S(2)}) copy-start(f32[128,768]{1,0:T(8,128)} %copy-done.6) | copy-start | bytes 1179652
  109.3 23.3 %copy-start.11 = (bf16[64,768]{1,0:T(8,128)(2,1)S(1)}, bf16[64,768]{1,0:T(8,128)(2,1)}, u32[]{:S(2)}) copy-start(bf16[64,768]{1,0:T(8,128)(2,1)} %copy-done.10) | copy-start | bytes 294916
  109.3 23.3 %copy-start.13 = (bf16[64,768]{1,0:T(8,128)(2,1)S(1)}, bf16[64,768]{1,0:T(8,128)(2,1)}, u32[]{:S(2)}) copy-start(bf16[64,768]{1,0:T(8,128)(2,1)} %copy-done.12) | copy-start | bytes 294916
  109.3 23.4 %copy-start.17 = (bf16[64,768]{1,0:T(8,128)(2,1)S(1)}, bf16[64,768]{1,0:T(8,128)(2,1)}, u32[]{:S(2)}) copy-start(bf16[64,768]{1,0:T(8,128)(2,1)} %copy-done.16) | copy-start | bytes 294916
  109.3 31.5 %copy-start.19 = (bf16[64,768]{1,0:T(8,128)(2,1)S(1)}, bf16[64,768]{1,0:T(8,128)(2,1)}, u32[]{:S(2)}) copy-start(bf16[64,768]{1,0:T(8,128)(2,1)} %copy-done.18) | copy-start | bytes 294916
  109.3 31.5 %copy-start.21 = (bf16[64,768]{1,0:T(8,128)(2,1)S(1)}, bf16[64,768]{1,0:T(8,128)(2,1)}, u32[]{:S(2)}) copy-start(bf16[64,768]{1,0:T(8,128)(2,1)} %copy-done.20) | copy-start | bytes 294916
  109.3 31.5 %copy-start.23 = (bf16[64,768]{1,0:T(8,128)(2,1)S(1)}, bf16[64,768]{1,0:T(8,128)(2,1)}, u32[]{:S(2)}) copy-start(bf16[64,768]{1,0:T(8,128)(2,1)} %copy-done.22) | copy-start | bytes 294916
  109.3 8.8 %collective-permute-start.23 = (bf16[128,768]{1,0:T(8,128)(2,1)S(1)}, bf16[128,768]{1,0:T(8,128)(2,1)S(1)}, u32[]{:S(2)}, u32[]{:S(2)}) collective-permute-start(bf16[128,768]{1,0:T(8,128)(2,1)S(1)} %get-tuple-element.54), channel_id=1, source_target_pairs={{0,1},{1,2},{2,3},{3,0},{4,5},{5,6},{6,7},{7,4},{8,9},{9,10},{10,1... | collective-permute-start | bytes 589832 | tf_op jit(solution)/shard_map/ppermute | solution.py:273
  110.8 11.3 %collective-permute-start.24 = (bf16[128,768]{1,0:T(8,128)(2,1)S(1)}, bf16[128,768]{1,0:T(8,128)(2,1)S(1)}, u32[]{:S(2)}, u32[]{:S(2)}) collective-permute-start(bf16[128,768]{1,0:T(8,128)(2,1)S(1)} %get-tuple-element.55), channel_id=1, source_target_pairs={{0,2},{1,3},{2,0},{3,1},{4,6},{5,7},{6,4},{7,5},{8,10},{9,11},{10,... | collective-permute-start | bytes 589832 | tf_op jit(solution)/shard_map/ppermute | solution.py:273
  112.4 9.7 %collective-permute-start.25 = (bf16[128,768]{1,0:T(8,128)(2,1)S(1)}, bf16[128,768]{1,0:T(8,128)(2,1)S(1)}, u32[]{:S(2)}, u32[]{:S(2)}) collective-permute-start(bf16[128,768]{1,0:T(8,128)(2,1)S(1)} %get-tuple-element.56), channel_id=1, source_target_pairs={{0,3},{1,0},{2,1},{3,2},{4,7},{5,4},{6,5},{7,6},{8,11},{9,8},{10,9... | collective-permute-start | bytes 589832 | tf_op jit(solution)/shard_map/ppermute | solution.py:273
  122.3 2.4 %collective-permute-start.29 = (bf16[128,768]{1,0:T(8,128)(2,1)S(1)}, bf16[128,768]{1,0:T(8,128)(2,1)S(1)}, u32[]{:S(2)}, u32[]{:S(2)}) collective-permute-start(bf16[128,768]{1,0:T(8,128)(2,1)S(1)} %subtract_convert_fusion), channel_id=1, source_target_pairs={{0,4},{4,0},{8,12},{12,8},{16,20},{20,16},{24,28},{28,24},{32,36},... | collective-permute-start | bytes 589832 | tf_op jit(solution)/shard_map/ppermute | solution.py:282
  124.9 5.7 %collective-permute-start.30 = (bf16[64,768]{1,0:T(8,128)(2,1)S(1)}, bf16[64,768]{1,0:T(8,128)(2,1)S(1)}, u32[]{:S(2)}, u32[]{:S(2)}) collective-permute-start(bf16[64,768]{1,0:T(8,128)(2,1)S(1)} %subtract_convert_fusion.3), channel_id=1, source_target_pairs={{0,8},{4,12},{8,16},{12,20},{16,24},{20,28},{24,0},{28,4},{32,40},... | collective-permute-start | bytes 294920 | tf_op jit(solution)/shard_map/ppermute | solution.py:282
  125.3 6.7 %collective-permute-start.31 = (bf16[64,768]{1,0:T(8,128)(2,1)S(1)}, bf16[64,768]{1,0:T(8,128)(2,1)S(1)}, u32[]{:S(2)}, u32[]{:S(2)}) collective-permute-start(bf16[64,768]{1,0:T(8,128)(2,1)S(1)} %subtract_convert_fusion.3), channel_id=1, source_target_pairs={{0,16},{4,20},{8,24},{12,28},{16,0},{20,4},{24,8},{28,12},{32,48},... | collective-permute-start | bytes 294920 | tf_op jit(solution)/shard_map/ppermute | solution.py:282
  127.3 5.3 %collective-permute-start.32 = (bf16[64,768]{1,0:T(8,128)(2,1)S(1)}, bf16[64,768]{1,0:T(8,128)(2,1)S(1)}, u32[]{:S(2)}, u32[]{:S(2)}) collective-permute-start(bf16[64,768]{1,0:T(8,128)(2,1)S(1)} %subtract_convert_fusion.3), channel_id=1, source_target_pairs={{0,24},{4,28},{8,0},{12,4},{16,8},{20,12},{24,16},{28,20},{32,56},... | collective-permute-start | bytes 294920 | tf_op jit(solution)/shard_map/ppermute | solution.py:282
  132.7 4.7 %collective-permute-start.33 = (bf16[64,768]{1,0:T(8,128)(2,1)S(1)}, bf16[64,768]{1,0:T(8,128)(2,1)S(1)}, u32[]{:S(2)}, u32[]{:S(2)}) collective-permute-start(bf16[64,768]{1,0:T(8,128)(2,1)S(1)} %subtract_convert_fusion.2), channel_id=1, source_target_pairs={{0,32},{4,36},{8,40},{12,44},{16,48},{20,52},{24,56},{28,60},{32,6... | collective-permute-start | bytes 294920 | tf_op jit(solution)/shard_map/ppermute | solution.py:282
  133.2 6.3 %collective-permute-start.34 = (bf16[64,768]{1,0:T(8,128)(2,1)S(1)}, bf16[64,768]{1,0:T(8,128)(2,1)S(1)}, u32[]{:S(2)}, u32[]{:S(2)}) collective-permute-start(bf16[64,768]{1,0:T(8,128)(2,1)S(1)} %subtract_convert_fusion.2), channel_id=1, source_target_pairs={{0,64},{4,68},{8,72},{12,76},{16,80},{20,84},{24,88},{28,92},{32,9... | collective-permute-start | bytes 294920 | tf_op jit(solution)/shard_map/ppermute | solution.py:282
  136.4 4.4 %collective-permute-start.35 = (bf16[64,768]{1,0:T(8,128)(2,1)S(1)}, bf16[64,768]{1,0:T(8,128)(2,1)S(1)}, u32[]{:S(2)}, u32[]{:S(2)}) collective-permute-start(bf16[64,768]{1,0:T(8,128)(2,1)S(1)} %subtract_convert_fusion.2), channel_id=1, source_target_pairs={{0,96},{4,100},{8,104},{12,108},{16,112},{20,116},{24,120},{28,124... | collective-permute-start | bytes 294920 | tf_op jit(solution)/shard_map/ppermute | solution.py:282
  141.0 3.3 %collective-permute-start.36 = (bf16[64,768]{1,0:T(8,128)(2,1)S(1)}, bf16[64,768]{1,0:T(8,128)(2,1)S(1)}, u32[]{:S(2)}, u32[]{:S(2)}) collective-permute-start(bf16[64,768]{1,0:T(8,128)(2,1)S(1)} %get-tuple-element.65), channel_id=1, source_target_pairs={{0,4},{4,0},{8,12},{12,8},{16,20},{20,16},{24,28},{28,24},{32,36},... | collective-permute-start | bytes 294920 | tf_op jit(solution)/shard_map/ppermute | solution.py:282
  (6 other events, 11.0 us)

commit v5 on v4

--- a/solution.py
+++ b/solution.py
@@ -40,7 +40,8 @@
 
 
 def spread(array):
-    return [array] + [lax.ppermute(array, "tp", ring(k)) for k in (1, 2, 3)]
+    far = lax.ppermute(array, "tp", ring(2))
+    return [array, lax.ppermute(array, "tp", ring(1)), far, lax.ppermute(array, "tp", ring(3))]
 
 
 def modulation_body(facts, all_gaps, mod_ref, out_ref):
@@ -269,7 +270,7 @@
 
     def deliver(own, shares):
         total = own
-        for k in (1, 2, 3):
+        for k in (2, 1, 3):
             total = total + lax.ppermute(shares[k], "tp", ring(k)).astype(F32)
         return total
 

time: 146 us -> 145 us (level)
  transfers between devices with their start and end apart: 38 -> 38, of which waited for: 22 -> 23; matrix products, arithmetic and copies ran while one was open for 2% -> 2% of each run, Pallas kernels for 7% -> 7%
where the time goes in v5:
time: 145 us
  starting transfers between devices  57.4 us (40%)
  waiting for transfers between devices  47.7 us (33%)
  Pallas kernels  19.3 us (13%)
  blocking collectives  7.55 us (5%)
  local copies, waits for them, and re-layouts  6.6 us (5%)
  other arithmetic  4.72 us (3%)
    ppermute x12, waiting for transfers between devices, deliver(): total = total + lax.ppermute(shares[k], 'tp', ring(k)).astype(F32)  22.8 us
    ppermute x16, starting transfers between devices, send(): lax.ppermute(message, 'tm', p).astype(F32) + t  19.9 us
    ppermute x12, starting transfers between devices, deliver(): total = total + lax.ppermute(shares[k], 'tp', ring(k)).astype(F32)  16.3 us
    ppermute x16, waiting for transfers between devices, send(): lax.ppermute(message, 'tm', p).astype(F32) + t  16.1 us
    all_to_all x1, starting transfers between devices, body(): all_gaps = lax.all_to_all(sent, 'tm', 0, 0)  9.44 us
    pallas_call x2, Pallas kernels, one(): pl.pallas_call(lambda *refs: one_body(s, tok, cols, *refs), out_shape=kep...  8.59 us
    pallas_call x1, Pallas kernels, both(): pl.pallas_call(lambda *refs: both_body(tok, cols, *refs), out_shape=share...  8.41 us
    all_to_all x1, blocking collectives, body(): mods = lax.all_to_all(made, 'tp', 0, 0)  7.55 us
  transfers between devices with their start and end apart: 38, of which 23 were waited for; matrix products, arithmetic and copies ran while one was open for 2% of the time, Pallas kernels for 7%

profile of v5, /device:TPU:1, one launch (start us, length us, event | category | flops | bytes accessed | tf_op | source)
XLA Modules:
  0.0 144.5 jit_solution(16601748379536146565)
XLA Ops:
  0.0 1.3 broadcast_in_dim.52
  1.3 1.1 copy-done.1
  2.6 2.2 %collective-permute-start = (bf16[264,768]{1,0:T(8,128)(2,1)S(1)}, bf16[264,768]{1,0:T(8,128)(2,1)S(1)}, u32[]{:S(2)}, u32[]{:S(2)}) collective-permute-start(bf16[264,768]{1,0:T(8,128)(2,1)S(1)} %centre.1.refs_1_), channel_id=1, source_target_pairs={{0,1},{1,2},{2,3},{3,0},{4,5},{5,6},{6,7},{7,4},{8,9},{9,10},{10,1... | collective-permute-start | bytes 1216520 | tf_op jit(solution)/shard_map/ppermute | solution.py:44
  4.7 2.6 %collective-permute-start.1 = (bf16[264,768]{1,0:T(8,128)(2,1)S(1)}, bf16[264,768]{1,0:T(8,128)(2,1)S(1)}, u32[]{:S(2)}, u32[]{:S(2)}) collective-permute-start(bf16[264,768]{1,0:T(8,128)(2,1)S(1)} %centre.1.refs_1_), channel_id=1, source_target_pairs={{0,2},{1,3},{2,0},{3,1},{4,6},{5,7},{6,4},{7,5},{8,10},{9,11},{10,... | collective-permute-start | bytes 1216520 | tf_op jit(solution)/shard_map/ppermute | solution.py:43
  7.4 1.1 collective-permute-start.2
  8.4 9.4 %all-to-all-start = ((s32[32,1,2]{2,1,0:T(1,128)}), s32[32,1,2]{2,1,0:T(1,128)S(1)}, u32[]{:S(2)}, u32[]{:S(2)}) async-start(s32[32,1,2]{2,1,0:T(1,128)} %broadcast_in_dim.52), calls=%async_computation | async-start | bytes 32768 | tf_op jit(solution)/shard_map/all_to_all | solution.py:262
  17.9 1.4 fusion.21
  19.9 1.2 compare_select_fusion.4.facts.refs_0_
  21.2 3.6 %all-to-all-done.all_gaps = s32[32,1,2]{2,1,0:T(1,128)S(1)} async-done(((s32[32,1,2]{2,1,0:T(1,128)}), s32[32,1,2]{2,1,0:T(1,128)S(1)}, u32[]{:S(2)}, u32[]{:S(2)}) %all-to-all-start) | async-done | bytes 288 | tf_op jit(solution)/shard_map/all_to_all | solution.py:262
  24.8 1.3 copy-done.4
  26.0 1.0 modulation.1
  27.0 7.5 %all_to_all.10.refs_5_ = f32[4,8,768]{2,1,0:T(8,128)S(1)} all-to-all(f32[4,8,768]{2,1,0:T(8,128)S(1)} %modulation.1), channel_id=1, replica_groups=mesh['tm'=32,'tp'=4] {'tp'}, dimensions={0} | all-to-all | bytes 196608 | tf_op jit(solution)/shard_map/all_to_all | solution.py:269
  34.6 8.4 %both.1 = (f32[128,768]{1,0:T(8,128)S(1)}, bf16[128,768]{1,0:T(8,128)(2,1)}, bf16[128,768]{1,0:T(8,128)(2,1)}, bf16[128,768]{1,0:T(8,128)(2,1)}, f32[128,768]{1,...) custom-call(s32[8]{0:T(128)S(1)} %compare_select_fusion.4.facts.refs, ...), custom_call_target="tpu_custom_call" | custom-call | flops 4831838208 | bytes 18874368 | tf_op jit(solution)/shard_map/both/pallas_call | solution.py:207
  43.0 0.7 copy-done.3
  43.8 0.7 copy-done.5
  44.5 0.9 collective-permute-start.3
  46.0 2.1 %collective-permute-start.5 = (bf16[128,768]{1,0:T(8,128)(2,1)}, bf16[128,768]{1,0:T(8,128)(2,1)S(1)}, u32[]{:S(2)}, u32[]{:S(2)}) collective-permute-start(bf16[128,768]{1,0:T(8,128)(2,1)} %get-tuple-element.39), channel_id=1, source_target_pairs={{0,3},{1,0},{2,1},{3,2},{4,7},{5,4},{6,5},{7,6},{8,11},{9,8},{10,9... | collective-permute-start | bytes 589832 | tf_op jit(solution)/shard_map/ppermute | solution.py:274
  48.1 2.7 %collective-permute-done.3 = bf16[128,768]{1,0:T(8,128)(2,1)S(1)} collective-permute-done((bf16[128,768]{1,0:T(8,128)(2,1)}, bf16[128,768]{1,0:T(8,128)(2,1)S(1)}, u32[]{:S(2)}, u32[]{:S(2)}) %collective-permute-start.3) | collective-permute-done | bytes 196640 | tf_op jit(solution)/shard_map/ppermute | solution.py:274
  50.8 5.9 %collective-permute-done.4 = bf16[128,768]{1,0:T(8,128)(2,1)S(1)} collective-permute-done((bf16[128,768]{1,0:T(8,128)(2,1)}, bf16[128,768]{1,0:T(8,128)(2,1)S(1)}, u32[]{:S(2)}, u32[]{:S(2)}) %collective-permute-start.4) | collective-permute-done | bytes 196640 | tf_op jit(solution)/shard_map/ppermute | solution.py:274
  56.8 1.1 convert_add_fusion.5
  57.9 1.0 collective-permute-start.6
  58.9 0.9 collective-permute-start.10
  59.9 0.8 collective-permute-start.11
  60.7 1.9 %collective-permute-start.12 = (bf16[128,768]{1,0:T(8,128)(2,1)S(1)}, bf16[128,768]{1,0:T(8,128)(2,1)S(1)}, u32[]{:S(2)}, u32[]{:S(2)}) collective-permute-start(bf16[128,768]{1,0:T(8,128)(2,1)S(1)} %get-tuple-element.49), channel_id=1, source_target_pairs={{0,3},{1,0},{2,1},{3,2},{4,7},{5,4},{6,5},{7,6},{8,11},{9,8},{10,9... | collective-permute-start | bytes 589832 | tf_op jit(solution)/shard_map/ppermute | solution.py:274
  63.1 1.8 %collective-permute-start.8 = (bf16[64,768]{1,0:T(8,128)(2,1)S(1)}, bf16[64,768]{1,0:T(8,128)(2,1)S(1)}, u32[]{:S(2)}, u32[]{:S(2)}) collective-permute-start(bf16[64,768]{1,0:T(8,128)(2,1)S(1)} %fusion.16), channel_id=1, source_target_pairs={{0,16},{4,20},{8,24},{12,28},{16,0},{20,4},{24,8},{28,12},{32,48},... | collective-permute-start | bytes 294920 | tf_op jit(solution)/shard_map/ppermute | solution.py:283
  64.8 2.3 %collective-permute-done.10 = bf16[128,768]{1,0:T(8,128)(2,1)S(1)} collective-permute-done((bf16[128,768]{1,0:T(8,128)(2,1)}, bf16[128,768]{1,0:T(8,128)(2,1)S(1)}, u32[]{:S(2)}, u32[]{:S(2)}) %collective-permute-start.10) | collective-permute-done | bytes 196640 | tf_op jit(solution)/shard_map/ppermute | solution.py:274
  67.2 0.9 collective-permute-start.9
  68.1 3.7 %collective-permute-done.11 = bf16[128,768]{1,0:T(8,128)(2,1)S(1)} collective-permute-done((bf16[128,768]{1,0:T(8,128)(2,1)S(1)}, bf16[128,768]{1,0:T(8,128)(2,1)S(1)}, u32[]{:S(2)}, u32[]{:S(2)}) %collective-permute-start.11) | collective-permute-done | bytes 196640 | tf_op jit(solution)/shard_map/ppermute | solution.py:274
  72.4 1.7 %collective-permute-start.14 = (bf16[64,768]{1,0:T(8,128)(2,1)S(1)}, bf16[64,768]{1,0:T(8,128)(2,1)S(1)}, u32[]{:S(2)}, u32[]{:S(2)}) collective-permute-start(bf16[64,768]{1,0:T(8,128)(2,1)S(1)} %convert_add_fusion.8), channel_id=1, source_target_pairs={{0,64},{4,68},{8,72},{12,76},{16,80},{20,84},{24,88},{28,92},{32,9... | collective-permute-start | bytes 294920 | tf_op jit(solution)/shard_map/ppermute | solution.py:283
  74.1 1.0 collective-permute-start.15
  75.1 2.4 %collective-permute-done.13 = bf16[64,768]{1,0:T(8,128)(2,1)S(1)} collective-permute-done((bf16[64,768]{1,0:T(8,128)(2,1)S(1)}, bf16[64,768]{1,0:T(8,128)(2,1)S(1)}, u32[]{:S(2)}, u32[]{:S(2)}) %collective-permute-start.13) | collective-permute-done | bytes 98336 | tf_op jit(solution)/shard_map/ppermute | solution.py:283
  78.8 2.5 %collective-permute-start.16 = (bf16[64,768]{1,0:T(8,128)(2,1)S(1)}, bf16[64,768]{1,0:T(8,128)(2,1)S(1)}, u32[]{:S(2)}, u32[]{:S(2)}) collective-permute-start(bf16[64,768]{1,0:T(8,128)(2,1)S(1)} %get-tuple-element.67), channel_id=1, source_target_pairs={{0,4},{4,0},{8,12},{12,8},{16,20},{20,16},{24,28},{28,24},{32,36},... | collective-permute-start | bytes 294920 | tf_op jit(solution)/shard_map/ppermute | solution.py:283
  81.3 0.9 collective-permute-done.16
  82.9 2.1 %collective-permute-start.21 = (bf16[128,768]{1,0:T(8,128)(2,1)S(1)}, bf16[128,768]{1,0:T(8,128)(2,1)S(1)}, u32[]{:S(2)}, u32[]{:S(2)}) collective-permute-start(bf16[128,768]{1,0:T(8,128)(2,1)S(1)} %get-tuple-element.70.after.refs_1_), channel_id=1, source_target_pairs={{0,2},{1,3},{2,0},{3,1},{4,6},{5,7},{6,4},{7,5},{8,10},{9,11},{10,... | collective-permute-start | bytes 589832 | tf_op jit(solution)/shard_map/ppermute | solution.py:43
  84.9 0.7 collective-permute-start.22
  85.6 1.1 arrive.1.refs_0_
  86.8 0.9 collective-permute-start.17
  87.6 1.3 collective-permute-start.18
  89.0 1.3 collective-permute-done.20.refs_2_
  90.9 2.9 %collective-permute-done.21.refs_3_ = bf16[128,768]{1,0:T(8,128)(2,1)S(1)} collective-permute-done((bf16[128,768]{1,0:T(8,128)(2,1)S(1)}, bf16[128,768]{1,0:T(8,128)(2,1)S(1)}, u32[]{:S(2)}, u32[]{:S(2)}) %collective-permute-start.21) | collective-permute-done | bytes 196640 | tf_op jit(solution)/shard_map/ppermute | solution.py:43
  93.9 1.0 collective-permute-done.22.refs_4_
  94.9 4.3 %one.2 = (f32[4,128,768]{2,1,0:T(8,128)S(1)}, f32[128,768]{1,0:T(8,128)S(1)}, bf16[128,768]{1,0:T(8,128)(2,1)S(1)}, bf16[128,768]{1,0:T(8,128)(2,1)S(1)}, bf16[128,768]{1,0:T(8,128)(2,1)S(1)}) custom-call(s32[8]{0:T(128)S(1)} %arrive.1.refs_0_, bf16[128,768]{1,0:T(8,128)(2,1)S(1)} %get-tuple-element.70.after.refs_1_, ...), custom_call_target="tpu_custom_call" | custom-call | flops 2415919104 | bytes 18874368 | tf_op jit(solution)/shard_map/one/pallas_call | solution.py:224
  99.2 1.0 collective-permute-start.26
  100.2 3.6 %collective-permute-start.27 = (bf16[128,768]{1,0:T(8,128)(2,1)S(1)}, bf16[128,768]{1,0:T(8,128)(2,1)S(1)}, u32[]{:S(2)}, u32[]{:S(2)}) collective-permute-start(bf16[128,768]{1,0:T(8,128)(2,1)S(1)} %get-tuple-element.59), channel_id=1, source_target_pairs={{0,1},{1,2},{2,3},{3,0},{4,5},{5,6},{6,7},{7,4},{8,9},{9,10},{10,1... | collective-permute-start | bytes 589832 | tf_op jit(solution)/shard_map/ppermute | solution.py:274
  103.9 4.3 %one.3 = (f32[128,768]{1,0:T(8,128)S(1)}, bf16[128,768]{1,0:T(8,128)(2,1)S(1)}, bf16[128,768]{1,0:T(8,128)(2,1)S(1)}, bf16[128,768]{1,0:T(8,128)(2,1)S(1)}) custom-call(s32[8]{0:T(128)S(1)} %arrive.1.refs_0_, bf16[128,768]{1,0:T(8,128)(2,1)S(1)} %get-tuple-element.69.refs_1_, bf16[128,768]{1,0:T(8,128)(2,1)S(1)} %collective-permute-done.17.refs_2_, ...), custom_call_target="tpu_custom_call" | custom-call | flops 2415919104 | bytes 18874368 | tf_op jit(solution)/shard_map/one/pallas_call | solution.py:224
  108.3 1.9 %collective-permute-start.23 = (bf16[128,768]{1,0:T(8,128)(2,1)S(1)}, bf16[128,768]{1,0:T(8,128)(2,1)S(1)}, u32[]{:S(2)}, u32[]{:S(2)}) collective-permute-start(bf16[128,768]{1,0:T(8,128)(2,1)S(1)} %get-tuple-element.54), channel_id=1, source_target_pairs={{0,2},{1,3},{2,0},{3,1},{4,6},{5,7},{6,4},{7,5},{8,10},{9,11},{10,... | collective-permute-start | bytes 589832 | tf_op jit(solution)/shard_map/ppermute | solution.py:274
  110.1 1.1 collective-permute-start.24
  111.2 1.6 %collective-permute-start.25 = (bf16[128,768]{1,0:T(8,128)(2,1)S(1)}, bf16[128,768]{1,0:T(8,128)(2,1)S(1)}, u32[]{:S(2)}, u32[]{:S(2)}) collective-permute-start(bf16[128,768]{1,0:T(8,128)(2,1)S(1)} %get-tuple-element.56), channel_id=1, source_target_pairs={{0,3},{1,0},{2,1},{3,2},{4,7},{5,4},{6,5},{7,6},{8,11},{9,8},{10,9... | collective-permute-start | bytes 589832 | tf_op jit(solution)/shard_map/ppermute | solution.py:274
  112.9 1.5 %collective-permute-done.23 = bf16[128,768]{1,0:T(8,128)(2,1)S(1)} collective-permute-done((bf16[128,768]{1,0:T(8,128)(2,1)S(1)}, bf16[128,768]{1,0:T(8,128)(2,1)S(1)}, u32[]{:S(2)}, u32[]{:S(2)}) %collective-permute-start.23) | collective-permute-done | bytes 196640 | tf_op jit(solution)/shard_map/ppermute | solution.py:274
  114.4 5.5 %collective-permute-done.24 = bf16[128,768]{1,0:T(8,128)(2,1)S(1)} collective-permute-done((bf16[128,768]{1,0:T(8,128)(2,1)S(1)}, bf16[128,768]{1,0:T(8,128)(2,1)S(1)}, u32[]{:S(2)}, u32[]{:S(2)}) %collective-permute-start.24) | collective-permute-done | bytes 196640 | tf_op jit(solution)/shard_map/ppermute | solution.py:274
  119.9 1.1 collective-permute-done.25
  121.2 1.5 %collective-permute-start.29 = (bf16[128,768]{1,0:T(8,128)(2,1)S(1)}, bf16[128,768]{1,0:T(8,128)(2,1)S(1)}, u32[]{:S(2)}, u32[]{:S(2)}) collective-permute-start(bf16[128,768]{1,0:T(8,128)(2,1)S(1)} %subtract_convert_fusion), channel_id=1, source_target_pairs={{0,4},{4,0},{8,12},{12,8},{16,20},{20,16},{24,28},{28,24},{32,36},... | collective-permute-start | bytes 589832 | tf_op jit(solution)/shard_map/ppermute | solution.py:283
  122.7 1.1 collective-permute-done.29
  124.3 2.9 %collective-permute-start.31 = (bf16[64,768]{1,0:T(8,128)(2,1)S(1)}, bf16[64,768]{1,0:T(8,128)(2,1)S(1)}, u32[]{:S(2)}, u32[]{:S(2)}) collective-permute-start(bf16[64,768]{1,0:T(8,128)(2,1)S(1)} %subtract_convert_fusion.3), channel_id=1, source_target_pairs={{0,16},{4,20},{8,24},{12,28},{16,0},{20,4},{24,8},{28,12},{32,48},... | collective-permute-start | bytes 294920 | tf_op jit(solution)/shard_map/ppermute | solution.py:283
  127.2 2.0 %collective-permute-done.30 = bf16[64,768]{1,0:T(8,128)(2,1)S(1)} collective-permute-done((bf16[64,768]{1,0:T(8,128)(2,1)S(1)}, bf16[64,768]{1,0:T(8,128)(2,1)S(1)}, u32[]{:S(2)}, u32[]{:S(2)}) %collective-permute-start.30) | collective-permute-done | bytes 98336 | tf_op jit(solution)/shard_map/ppermute | solution.py:283
  129.2 2.6 %collective-permute-done.31 = bf16[64,768]{1,0:T(8,128)(2,1)S(1)} collective-permute-done((bf16[64,768]{1,0:T(8,128)(2,1)S(1)}, bf16[64,768]{1,0:T(8,128)(2,1)S(1)}, u32[]{:S(2)}, u32[]{:S(2)}) %collective-permute-start.31) | collective-permute-done | bytes 98336 | tf_op jit(solution)/shard_map/ppermute | solution.py:283
  132.1 0.7 collective-permute-start.33
  132.8 3.0 %collective-permute-start.34 = (bf16[64,768]{1,0:T(8,128)(2,1)S(1)}, bf16[64,768]{1,0:T(8,128)(2,1)S(1)}, u32[]{:S(2)}, u32[]{:S(2)}) collective-permute-start(bf16[64,768]{1,0:T(8,128)(2,1)S(1)} %subtract_convert_fusion.2), channel_id=1, source_target_pairs={{0,64},{4,68},{8,72},{12,76},{16,80},{20,84},{24,88},{28,92},{32,9... | collective-permute-start | bytes 294920 | tf_op jit(solution)/shard_map/ppermute | solution.py:283
  135.8 1.1 collective-permute-done.33
  136.9 2.4 %collective-permute-done.34 = bf16[64,768]{1,0:T(8,128)(2,1)S(1)} collective-permute-done((bf16[64,768]{1,0:T(8,128)(2,1)S(1)}, bf16[64,768]{1,0:T(8,128)(2,1)S(1)}, u32[]{:S(2)}, u32[]{:S(2)}) %collective-permute-start.34) | collective-permute-done | bytes 98336 | tf_op jit(solution)/shard_map/ppermute | solution.py:283
  139.2 1.2 collective-permute-done.35
  140.7 1.7 %collective-permute-start.36 = (bf16[64,768]{1,0:T(8,128)(2,1)S(1)}, bf16[64,768]{1,0:T(8,128)(2,1)S(1)}, u32[]{:S(2)}, u32[]{:S(2)}) collective-permute-start(bf16[64,768]{1,0:T(8,128)(2,1)S(1)} %get-tuple-element.65), channel_id=1, source_target_pairs={{0,4},{4,0},{8,12},{12,8},{16,20},{20,16},{24,28},{28,24},{32,36},... | collective-permute-start | bytes 294920 | tf_op jit(solution)/shard_map/ppermute | solution.py:283
  142.4 0.9 collective-permute-done.36
  143.6 0.9 pad_maximum_fusion
  (110 shorter events, 5.8 us)
Async XLA Ops:
  2.4 32.2 %slice-start.4 = ((s8[4718592]{0:T(1024)(128)(4,1)}), s8[524288]{0:T(1024)(128)(4,1)S(1)}, s32[]{:S(2)}) async-start(s8[4718592]{0:T(1024)(128)(4,1)} %bitcast.26), calls=%async_computation.6 | async-start | bytes 1048576
  2.6 32.0 %collective-permute-start = (bf16[264,768]{1,0:T(8,128)(2,1)S(1)}, bf16[264,768]{1,0:T(8,128)(2,1)S(1)}, u32[]{:S(2)}, u32[]{:S(2)}) collective-permute-start(bf16[264,768]{1,0:T(8,128)(2,1)S(1)} %centre.1.refs_1_), channel_id=1, source_target_pairs={{0,1},{1,2},{2,3},{3,0},{4,5},{5,6},{6,7},{7,4},{8,9},{9,10},{10,1... | collective-permute-start | bytes 1216520 | tf_op jit(solution)/shard_map/ppermute | solution.py:44
  4.7 29.8 %collective-permute-start.1 = (bf16[264,768]{1,0:T(8,128)(2,1)S(1)}, bf16[264,768]{1,0:T(8,128)(2,1)S(1)}, u32[]{:S(2)}, u32[]{:S(2)}) collective-permute-start(bf16[264,768]{1,0:T(8,128)(2,1)S(1)} %centre.1.refs_1_), channel_id=1, source_target_pairs={{0,2},{1,3},{2,0},{3,1},{4,6},{5,7},{6,4},{7,5},{8,10},{9,11},{10,... | collective-permute-start | bytes 1216520 | tf_op jit(solution)/shard_map/ppermute | solution.py:43
  7.4 27.2 %collective-permute-start.2 = (bf16[264,768]{1,0:T(8,128)(2,1)S(1)}, bf16[264,768]{1,0:T(8,128)(2,1)S(1)}, u32[]{:S(2)}, u32[]{:S(2)}) collective-permute-start(bf16[264,768]{1,0:T(8,128)(2,1)S(1)} %centre.1.refs_1_), channel_id=1, source_target_pairs={{0,3},{1,0},{2,1},{3,2},{4,7},{5,4},{6,5},{7,6},{8,11},{9,8},{10,9... | collective-permute-start | bytes 1216520 | tf_op jit(solution)/shard_map/ppermute | solution.py:44
  8.4 16.3 %all-to-all-start = ((s32[32,1,2]{2,1,0:T(1,128)}), s32[32,1,2]{2,1,0:T(1,128)S(1)}, u32[]{:S(2)}, u32[]{:S(2)}) async-start(s32[32,1,2]{2,1,0:T(1,128)} %broadcast_in_dim.52), calls=%async_computation | async-start | bytes 32768 | tf_op jit(solution)/shard_map/all_to_all | solution.py:262
  26.0 8.6 %copy-start = (bf16[3072,3,768]{2,0,1:T(8,128)(2,1)S(1)}, bf16[3072,3,768]{2,0,1:T(8,128)(2,1)}, u32[]{:S(2)}) copy-start(bf16[3072,3,768]{2,0,1:T(8,128)(2,1)} %param.9) | copy-start | bytes 42467332
  26.0 8.6 %slice-start.5 = ((s8[4718592]{0:T(1024)(128)(4,1)}), s8[4194304]{0:T(1024)(128)(4,1)S(1)}, s32[]{:S(2)}) async-start(s8[4718592]{0:T(1024)(128)(4,1)} %bitcast.26), calls=%async_computation.7 | async-start | bytes 8388608
  44.5 6.3 %collective-permute-start.3 = (bf16[128,768]{1,0:T(8,128)(2,1)}, bf16[128,768]{1,0:T(8,128)(2,1)S(1)}, u32[]{:S(2)}, u32[]{:S(2)}) collective-permute-start(bf16[128,768]{1,0:T(8,128)(2,1)} %get-tuple-element.37), channel_id=1, source_target_pairs={{0,2},{1,3},{2,0},{3,1},{4,6},{5,7},{6,4},{7,5},{8,10},{9,11},{10,... | collective-permute-start | bytes 589832 | tf_op jit(solution)/shard_map/ppermute | solution.py:274
  45.4 11.4 %collective-permute-start.4 = (bf16[128,768]{1,0:T(8,128)(2,1)}, bf16[128,768]{1,0:T(8,128)(2,1)S(1)}, u32[]{:S(2)}, u32[]{:S(2)}) collective-permute-start(bf16[128,768]{1,0:T(8,128)(2,1)} %get-tuple-element.38), channel_id=1, source_target_pairs={{0,1},{1,2},{2,3},{3,0},{4,5},{5,6},{6,7},{7,4},{8,9},{9,10},{10,1... | collective-permute-start | bytes 589832 | tf_op jit(solution)/shard_map/ppermute | solution.py:274
  46.0 10.8 %collective-permute-start.5 = (bf16[128,768]{1,0:T(8,128)(2,1)}, bf16[128,768]{1,0:T(8,128)(2,1)S(1)}, u32[]{:S(2)}, u32[]{:S(2)}) collective-permute-start(bf16[128,768]{1,0:T(8,128)(2,1)} %get-tuple-element.39), channel_id=1, source_target_pairs={{0,3},{1,0},{2,1},{3,2},{4,7},{5,4},{6,5},{7,6},{8,11},{9,8},{10,9... | collective-permute-start | bytes 589832 | tf_op jit(solution)/shard_map/ppermute | solution.py:274
  57.9 4.8 %copy-start.14 = (bf16[128,768]{1,0:T(8,128)(2,1)}, bf16[128,768]{1,0:T(8,128)(2,1)S(1)}, u32[]{:S(2)}) copy-start(bf16[128,768]{1,0:T(8,128)(2,1)S(1)} %fusion.15) | copy-start | bytes 589828
  57.9 4.7 %collective-permute-start.6 = (bf16[128,768]{1,0:T(8,128)(2,1)S(1)}, bf16[128,768]{1,0:T(8,128)(2,1)S(1)}, u32[]{:S(2)}, u32[]{:S(2)}) collective-permute-start(bf16[128,768]{1,0:T(8,128)(2,1)S(1)} %fusion.15), channel_id=1, source_target_pairs={{0,4},{4,0},{8,12},{12,8},{16,20},{20,16},{24,28},{28,24},{32,36},... | collective-permute-start | bytes 589832 | tf_op jit(solution)/shard_map/ppermute | solution.py:283
  58.9 8.2 %collective-permute-start.10 = (bf16[128,768]{1,0:T(8,128)(2,1)}, bf16[128,768]{1,0:T(8,128)(2,1)S(1)}, u32[]{:S(2)}, u32[]{:S(2)}) collective-permute-start(bf16[128,768]{1,0:T(8,128)(2,1)} %copy-done.5), channel_id=1, source_target_pairs={{0,2},{1,3},{2,0},{3,1},{4,6},{5,7},{6,4},{7,5},{8,10},{9,11},{10,... | collective-permute-start | bytes 589832 | tf_op jit(solution)/shard_map/ppermute | solution.py:274
  59.9 11.9 %collective-permute-start.11 = (bf16[128,768]{1,0:T(8,128)(2,1)S(1)}, bf16[128,768]{1,0:T(8,128)(2,1)S(1)}, u32[]{:S(2)}, u32[]{:S(2)}) collective-permute-start(bf16[128,768]{1,0:T(8,128)(2,1)S(1)} %get-tuple-element.48), channel_id=1, source_target_pairs={{0,1},{1,2},{2,3},{3,0},{4,5},{5,6},{6,7},{7,4},{8,9},{9,10},{10,1... | collective-permute-start | bytes 589832 | tf_op jit(solution)/shard_map/ppermute | solution.py:274
  60.7 11.0 %collective-permute-start.12 = (bf16[128,768]{1,0:T(8,128)(2,1)S(1)}, bf16[128,768]{1,0:T(8,128)(2,1)S(1)}, u32[]{:S(2)}, u32[]{:S(2)}) collective-permute-start(bf16[128,768]{1,0:T(8,128)(2,1)S(1)} %get-tuple-element.49), channel_id=1, source_target_pairs={{0,3},{1,0},{2,1},{3,2},{4,7},{5,4},{6,5},{7,6},{8,11},{9,8},{10,9... | collective-permute-start | bytes 589832 | tf_op jit(solution)/shard_map/ppermute | solution.py:274
  62.6 19.9 %copy-start.8 = (bf16[128,768]{1,0:T(8,128)(2,1)}, bf16[128,768]{1,0:T(8,128)(2,1)S(1)}, u32[]{:S(2)}) copy-start(bf16[128,768]{1,0:T(8,128)(2,1)S(1)} %collective-permute-done.6) | copy-start | bytes 589828
  62.6 19.8 %copy-start.6 = (f32[128,768]{1,0:T(8,128)}, f32[128,768]{1,0:T(8,128)S(1)}, u32[]{:S(2)}) copy-start(f32[128,768]{1,0:T(8,128)S(1)} %convert_add_fusion.1) | copy-start | bytes 1179652
  62.7 9.1 %collective-permute-start.7 = (bf16[64,768]{1,0:T(8,128)(2,1)S(1)}, bf16[64,768]{1,0:T(8,128)(2,1)S(1)}, u32[]{:S(2)}, u32[]{:S(2)}) collective-permute-start(bf16[64,768]{1,0:T(8,128)(2,1)S(1)} %fusion.16), channel_id=1, source_target_pairs={{0,8},{4,12},{8,16},{12,20},{16,24},{20,28},{24,0},{28,4},{32,40},... | collective-permute-start | bytes 294920 | tf_op jit(solution)/shard_map/ppermute | solution.py:283
  63.1 8.8 %collective-permute-start.8 = (bf16[64,768]{1,0:T(8,128)(2,1)S(1)}, bf16[64,768]{1,0:T(8,128)(2,1)S(1)}, u32[]{:S(2)}, u32[]{:S(2)}) collective-permute-start(bf16[64,768]{1,0:T(8,128)(2,1)S(1)} %fusion.16), channel_id=1, source_target_pairs={{0,16},{4,20},{8,24},{12,28},{16,0},{20,4},{24,8},{28,12},{32,48},... | collective-permute-start | bytes 294920 | tf_op jit(solution)/shard_map/ppermute | solution.py:283
  67.2 4.7 %collective-permute-start.9 = (bf16[64,768]{1,0:T(8,128)(2,1)S(1)}, bf16[64,768]{1,0:T(8,128)(2,1)S(1)}, u32[]{:S(2)}, u32[]{:S(2)}) collective-permute-start(bf16[64,768]{1,0:T(8,128)(2,1)S(1)} %fusion.16), channel_id=1, source_target_pairs={{0,24},{4,28},{8,0},{12,4},{16,8},{20,12},{24,16},{28,20},{32,56},... | collective-permute-start | bytes 294920 | tf_op jit(solution)/shard_map/ppermute | solution.py:283
  71.9 10.6 %copy-start.10 = (bf16[64,768]{1,0:T(8,128)(2,1)}, bf16[64,768]{1,0:T(8,128)(2,1)S(1)}, u32[]{:S(2)}) copy-start(bf16[64,768]{1,0:T(8,128)(2,1)S(1)} %collective-permute-done.8) | copy-start | bytes 294916
  71.9 10.6 %copy-start.12 = (bf16[64,768]{1,0:T(8,128)(2,1)}, bf16[64,768]{1,0:T(8,128)(2,1)S(1)}, u32[]{:S(2)}) copy-start(bf16[64,768]{1,0:T(8,128)(2,1)S(1)} %collective-permute-done.9) | copy-start | bytes 294916
  71.9 10.5 %copy-start.16 = (bf16[64,768]{1,0:T(8,128)(2,1)}, bf16[64,768]{1,0:T(8,128)(2,1)S(1)}, u32[]{:S(2)}) copy-start(bf16[64,768]{1,0:T(8,128)(2,1)S(1)} %convert_add_fusion.8) | copy-start | bytes 294916
  72.0 5.5 %collective-permute-start.13 = (bf16[64,768]{1,0:T(8,128)(2,1)S(1)}, bf16[64,768]{1,0:T(8,128)(2,1)S(1)}, u32[]{:S(2)}, u32[]{:S(2)}) collective-permute-start(bf16[64,768]{1,0:T(8,128)(2,1)S(1)} %convert_add_fusion.8), channel_id=1, source_target_pairs={{0,32},{4,36},{8,40},{12,44},{16,48},{20,52},{24,56},{28,60},{32,6... | collective-permute-start | bytes 294920 | tf_op jit(solution)/shard_map/ppermute | solution.py:283
  72.4 5.6 %collective-permute-start.14 = (bf16[64,768]{1,0:T(8,128)(2,1)S(1)}, bf16[64,768]{1,0:T(8,128)(2,1)S(1)}, u32[]{:S(2)}, u32[]{:S(2)}) collective-permute-start(bf16[64,768]{1,0:T(8,128)(2,1)S(1)} %convert_add_fusion.8), channel_id=1, source_target_pairs={{0,64},{4,68},{8,72},{12,76},{16,80},{20,84},{24,88},{28,92},{32,9... | collective-permute-start | bytes 294920 | tf_op jit(solution)/shard_map/ppermute | solution.py:283
  74.1 4.6 %collective-permute-start.15 = (bf16[64,768]{1,0:T(8,128)(2,1)S(1)}, bf16[64,768]{1,0:T(8,128)(2,1)S(1)}, u32[]{:S(2)}, u32[]{:S(2)}) collective-permute-start(bf16[64,768]{1,0:T(8,128)(2,1)S(1)} %convert_add_fusion.8), channel_id=1, source_target_pairs={{0,96},{4,100},{8,104},{12,108},{16,112},{20,116},{24,120},{28,124... | collective-permute-start | bytes 294920 | tf_op jit(solution)/shard_map/ppermute | solution.py:283
  77.5 4.8 %copy-start.18 = (bf16[64,768]{1,0:T(8,128)(2,1)}, bf16[64,768]{1,0:T(8,128)(2,1)S(1)}, u32[]{:S(2)}) copy-start(bf16[64,768]{1,0:T(8,128)(2,1)S(1)} %collective-permute-done.13) | copy-start | bytes 294916
  78.8 3.5 %collective-permute-start.16 = (bf16[64,768]{1,0:T(8,128)(2,1)S(1)}, bf16[64,768]{1,0:T(8,128)(2,1)S(1)}, u32[]{:S(2)}, u32[]{:S(2)}) collective-permute-start(bf16[64,768]{1,0:T(8,128)(2,1)S(1)} %get-tuple-element.67), channel_id=1, source_target_pairs={{0,4},{4,0},{8,12},{12,8},{16,20},{20,16},{24,28},{28,24},{32,36},... | collective-permute-start | bytes 294920 | tf_op jit(solution)/shard_map/ppermute | solution.py:283
  82.5 12.4 %slice-start = ((s8[14155776]{0:T(1024)(128)(4,1)}), s8[4194304]{0:T(1024)(128)(4,1)S(1)}, s32[]{:S(2)}) async-start(s8[14155776]{0:T(1024)(128)(4,1)} %bitcast.22), calls=%async_computation.2 | async-start | bytes 8388608
  82.5 12.4 %slice-start.6 = ((s8[4718592]{0:T(1024)(128)(4,1)}), s8[4194304]{0:T(1024)(128)(4,1)S(1)}, s32[]{:S(2)}) async-start(s8[4718592]{0:T(1024)(128)(4,1)} %bitcast.28), calls=%async_computation.8 | async-start | bytes 8388608
  82.5 12.4 %slice-start.1 = ((s8[14155776]{0:T(1024)(128)(4,1)}), s8[4194304]{0:T(1024)(128)(4,1)S(1)}, s32[]{:S(2)}) async-start(s8[14155776]{0:T(1024)(128)(4,1)} %bitcast.22), calls=%async_computation.3 | async-start | bytes 8388608
  82.5 12.4 %slice-start.2 = ((s8[14155776]{0:T(1024)(128)(4,1)}), s8[4194304]{0:T(1024)(128)(4,1)S(1)}, s32[]{:S(2)}) async-start(s8[14155776]{0:T(1024)(128)(4,1)} %bitcast.22), calls=%async_computation.4 | async-start | bytes 8388608
  82.5 12.4 %slice-start.3 = ((s8[14155776]{0:T(1024)(128)(4,1)}), s8[1572864]{0:T(1024)(128)(4,1)S(1)}, s32[]{:S(2)}) async-start(s8[14155776]{0:T(1024)(128)(4,1)} %bitcast.22), calls=%async_computation.5 | async-start | bytes 3145728
  82.5 12.4 %slice-start.7 = ((s8[4718592]{0:T(1024)(128)(4,1)}), s8[524288]{0:T(1024)(128)(4,1)S(1)}, s32[]{:S(2)}) async-start(s8[4718592]{0:T(1024)(128)(4,1)} %bitcast.28), calls=%async_computation.9 | async-start | bytes 1048576
  82.5 7.8 %collective-permute-start.20 = (bf16[128,768]{1,0:T(8,128)(2,1)S(1)}, bf16[128,768]{1,0:T(8,128)(2,1)S(1)}, u32[]{:S(2)}, u32[]{:S(2)}) collective-permute-start(bf16[128,768]{1,0:T(8,128)(2,1)S(1)} %get-tuple-element.70.after.refs_1_), channel_id=1, source_target_pairs={{0,1},{1,2},{2,3},{3,0},{4,5},{5,6},{6,7},{7,4},{8,9},{9,10},{10,1... | collective-permute-start | bytes 589832 | tf_op jit(solution)/shard_map/ppermute | solution.py:44
  82.9 11.0 %collective-permute-start.21 = (bf16[128,768]{1,0:T(8,128)(2,1)S(1)}, bf16[128,768]{1,0:T(8,128)(2,1)S(1)}, u32[]{:S(2)}, u32[]{:S(2)}) collective-permute-start(bf16[128,768]{1,0:T(8,128)(2,1)S(1)} %get-tuple-element.70.after.refs_1_), channel_id=1, source_target_pairs={{0,2},{1,3},{2,0},{3,1},{4,6},{5,7},{6,4},{7,5},{8,10},{9,11},{10,... | collective-permute-start | bytes 589832 | tf_op jit(solution)/shard_map/ppermute | solution.py:43
  84.9 10.0 %collective-permute-start.22 = (bf16[128,768]{1,0:T(8,128)(2,1)S(1)}, bf16[128,768]{1,0:T(8,128)(2,1)S(1)}, u32[]{:S(2)}, u32[]{:S(2)}) collective-permute-start(bf16[128,768]{1,0:T(8,128)(2,1)S(1)} %get-tuple-element.70.after.refs_1_), channel_id=1, source_target_pairs={{0,3},{1,0},{2,1},{3,2},{4,7},{5,4},{6,5},{7,6},{8,11},{9,8},{10,9... | collective-permute-start | bytes 589832 | tf_op jit(solution)/shard_map/ppermute | solution.py:44
  86.8 17.1 %collective-permute-start.17 = (bf16[128,768]{1,0:T(8,128)(2,1)S(1)}, bf16[128,768]{1,0:T(8,128)(2,1)S(1)}, u32[]{:S(2)}, u32[]{:S(2)}) collective-permute-start(bf16[128,768]{1,0:T(8,128)(2,1)S(1)} %get-tuple-element.69.refs_1_), channel_id=1, source_target_pairs={{0,1},{1,2},{2,3},{3,0},{4,5},{5,6},{6,7},{7,4},{8,9},{9,10},{10,1... | collective-permute-start | bytes 589832 | tf_op jit(solution)/shard_map/ppermute | solution.py:44
  87.6 16.2 %collective-permute-start.18 = (bf16[128,768]{1,0:T(8,128)(2,1)S(1)}, bf16[128,768]{1,0:T(8,128)(2,1)S(1)}, u32[]{:S(2)}, u32[]{:S(2)}) collective-permute-start(bf16[128,768]{1,0:T(8,128)(2,1)S(1)} %get-tuple-element.69.refs_1_), channel_id=1, source_target_pairs={{0,2},{1,3},{2,0},{3,1},{4,6},{5,7},{6,4},{7,5},{8,10},{9,11},{10,... | collective-permute-start | bytes 589832 | tf_op jit(solution)/shard_map/ppermute | solution.py:43
  90.3 13.5 %collective-permute-start.19 = (bf16[128,768]{1,0:T(8,128)(2,1)S(1)}, bf16[128,768]{1,0:T(8,128)(2,1)S(1)}, u32[]{:S(2)}, u32[]{:S(2)}) collective-permute-start(bf16[128,768]{1,0:T(8,128)(2,1)S(1)} %get-tuple-element.69.refs_1_), channel_id=1, source_target_pairs={{0,3},{1,0},{2,1},{3,2},{4,7},{5,4},{6,5},{7,6},{8,11},{9,8},{10,9... | collective-permute-start | bytes 589832 | tf_op jit(solution)/shard_map/ppermute | solution.py:44
  99.2 12.0 %collective-permute-start.26 = (bf16[128,768]{1,0:T(8,128)(2,1)S(1)}, bf16[128,768]{1,0:T(8,128)(2,1)S(1)}, u32[]{:S(2)}, u32[]{:S(2)}) collective-permute-start(bf16[128,768]{1,0:T(8,128)(2,1)S(1)} %get-tuple-element.58), channel_id=1, source_target_pairs={{0,2},{1,3},{2,0},{3,1},{4,6},{5,7},{6,4},{7,5},{8,10},{9,11},{10,... | collective-permute-start | bytes 589832 | tf_op jit(solution)/shard_map/ppermute | solution.py:274
  100.2 12.6 %collective-permute-start.27 = (bf16[128,768]{1,0:T(8,128)(2,1)S(1)}, bf16[128,768]{1,0:T(8,128)(2,1)S(1)}, u32[]{:S(2)}, u32[]{:S(2)}) collective-permute-start(bf16[128,768]{1,0:T(8,128)(2,1)S(1)} %get-tuple-element.59), channel_id=1, source_target_pairs={{0,1},{1,2},{2,3},{3,0},{4,5},{5,6},{6,7},{7,4},{8,9},{9,10},{10,1... | collective-permute-start | bytes 589832 | tf_op jit(solution)/shard_map/ppermute | solution.py:274
  103.8 9.0 %collective-permute-start.28 = (bf16[128,768]{1,0:T(8,128)(2,1)S(1)}, bf16[128,768]{1,0:T(8,128)(2,1)S(1)}, u32[]{:S(2)}, u32[]{:S(2)}) collective-permute-start(bf16[128,768]{1,0:T(8,128)(2,1)S(1)} %get-tuple-element.60), channel_id=1, source_target_pairs={{0,3},{1,0},{2,1},{3,2},{4,7},{5,4},{6,5},{7,6},{8,11},{9,8},{10,9... | collective-permute-start | bytes 589832 | tf_op jit(solution)/shard_map/ppermute | solution.py:274
  103.8 17.3 %copy-start.2 = (f32[2,128,768]{2,1,0:T(8,128)S(1)}, f32[2,128,768]{2,1,0:T(8,128)}, u32[]{:S(2)}) copy-start(f32[2,128,768]{2,1,0:T(8,128)} %param.6) | copy-start | bytes 2359300
  103.9 17.3 %copy-start.15 = (bf16[128,768]{1,0:T(8,128)(2,1)S(1)}, bf16[128,768]{1,0:T(8,128)(2,1)}, u32[]{:S(2)}) copy-start(bf16[128,768]{1,0:T(8,128)(2,1)} %copy-done.14) | copy-start | bytes 589828
  103.9 19.9 %copy-start.9 = (bf16[128,768]{1,0:T(8,128)(2,1)S(1)}, bf16[128,768]{1,0:T(8,128)(2,1)}, u32[]{:S(2)}) copy-start(bf16[128,768]{1,0:T(8,128)(2,1)} %copy-done.8) | copy-start | bytes 589828
  108.2 15.7 %copy-start.7 = (f32[128,768]{1,0:T(8,128)S(1)}, f32[128,768]{1,0:T(8,128)}, u32[]{:S(2)}) copy-start(f32[128,768]{1,0:T(8,128)} %copy-done.6) | copy-start | bytes 1179652
  108.2 23.8 %copy-start.11 = (bf16[64,768]{1,0:T(8,128)(2,1)S(1)}, bf16[64,768]{1,0:T(8,128)(2,1)}, u32[]{:S(2)}) copy-start(bf16[64,768]{1,0:T(8,128)(2,1)} %copy-done.10) | copy-start | bytes 294916
  108.2 23.8 %copy-start.13 = (bf16[64,768]{1,0:T(8,128)(2,1)S(1)}, bf16[64,768]{1,0:T(8,128)(2,1)}, u32[]{:S(2)}) copy-start(bf16[64,768]{1,0:T(8,128)(2,1)} %copy-done.12) | copy-start | bytes 294916
  108.2 23.9 %copy-start.17 = (bf16[64,768]{1,0:T(8,128)(2,1)S(1)}, bf16[64,768]{1,0:T(8,128)(2,1)}, u32[]{:S(2)}) copy-start(bf16[64,768]{1,0:T(8,128)(2,1)} %copy-done.16) | copy-start | bytes 294916
  108.2 32.2 %copy-start.19 = (bf16[64,768]{1,0:T(8,128)(2,1)S(1)}, bf16[64,768]{1,0:T(8,128)(2,1)}, u32[]{:S(2)}) copy-start(bf16[64,768]{1,0:T(8,128)(2,1)} %copy-done.18) | copy-start | bytes 294916
  108.2 32.2 %copy-start.21 = (bf16[64,768]{1,0:T(8,128)(2,1)S(1)}, bf16[64,768]{1,0:T(8,128)(2,1)}, u32[]{:S(2)}) copy-start(bf16[64,768]{1,0:T(8,128)(2,1)} %copy-done.20) | copy-start | bytes 294916
  108.3 32.2 %copy-start.23 = (bf16[64,768]{1,0:T(8,128)(2,1)S(1)}, bf16[64,768]{1,0:T(8,128)(2,1)}, u32[]{:S(2)}) copy-start(bf16[64,768]{1,0:T(8,128)(2,1)} %copy-done.22) | copy-start | bytes 294916
  108.3 6.2 %collective-permute-start.23 = (bf16[128,768]{1,0:T(8,128)(2,1)S(1)}, bf16[128,768]{1,0:T(8,128)(2,1)S(1)}, u32[]{:S(2)}, u32[]{:S(2)}) collective-permute-start(bf16[128,768]{1,0:T(8,128)(2,1)S(1)} %get-tuple-element.54), channel_id=1, source_target_pairs={{0,2},{1,3},{2,0},{3,1},{4,6},{5,7},{6,4},{7,5},{8,10},{9,11},{10,... | collective-permute-start | bytes 589832 | tf_op jit(solution)/shard_map/ppermute | solution.py:274
  110.1 9.8 %collective-permute-start.24 = (bf16[128,768]{1,0:T(8,128)(2,1)S(1)}, bf16[128,768]{1,0:T(8,128)(2,1)S(1)}, u32[]{:S(2)}, u32[]{:S(2)}) collective-permute-start(bf16[128,768]{1,0:T(8,128)(2,1)S(1)} %get-tuple-element.55), channel_id=1, source_target_pairs={{0,1},{1,2},{2,3},{3,0},{4,5},{5,6},{6,7},{7,4},{8,9},{9,10},{10,1... | collective-permute-start | bytes 589832 | tf_op jit(solution)/shard_map/ppermute | solution.py:274
  111.2 9.8 %collective-permute-start.25 = (bf16[128,768]{1,0:T(8,128)(2,1)S(1)}, bf16[128,768]{1,0:T(8,128)(2,1)S(1)}, u32[]{:S(2)}, u32[]{:S(2)}) collective-permute-start(bf16[128,768]{1,0:T(8,128)(2,1)S(1)} %get-tuple-element.56), channel_id=1, source_target_pairs={{0,3},{1,0},{2,1},{3,2},{4,7},{5,4},{6,5},{7,6},{8,11},{9,8},{10,9... | collective-permute-start | bytes 589832 | tf_op jit(solution)/shard_map/ppermute | solution.py:274
  121.2 2.6 %collective-permute-start.29 = (bf16[128,768]{1,0:T(8,128)(2,1)S(1)}, bf16[128,768]{1,0:T(8,128)(2,1)S(1)}, u32[]{:S(2)}, u32[]{:S(2)}) collective-permute-start(bf16[128,768]{1,0:T(8,128)(2,1)S(1)} %subtract_convert_fusion), channel_id=1, source_target_pairs={{0,4},{4,0},{8,12},{12,8},{16,20},{20,16},{24,28},{28,24},{32,36},... | collective-permute-start | bytes 589832 | tf_op jit(solution)/shard_map/ppermute | solution.py:283
  123.9 5.3 %collective-permute-start.30 = (bf16[64,768]{1,0:T(8,128)(2,1)S(1)}, bf16[64,768]{1,0:T(8,128)(2,1)S(1)}, u32[]{:S(2)}, u32[]{:S(2)}) collective-permute-start(bf16[64,768]{1,0:T(8,128)(2,1)S(1)} %subtract_convert_fusion.3), channel_id=1, source_target_pairs={{0,8},{4,12},{8,16},{12,20},{16,24},{20,28},{24,0},{28,4},{32,40},... | collective-permute-start | bytes 294920 | tf_op jit(solution)/shard_map/ppermute | solution.py:283
  124.3 7.5 %collective-permute-start.31 = (bf16[64,768]{1,0:T(8,128)(2,1)S(1)}, bf16[64,768]{1,0:T(8,128)(2,1)S(1)}, u32[]{:S(2)}, u32[]{:S(2)}) collective-permute-start(bf16[64,768]{1,0:T(8,128)(2,1)S(1)} %subtract_convert_fusion.3), channel_id=1, source_target_pairs={{0,16},{4,20},{8,24},{12,28},{16,0},{20,4},{24,8},{28,12},{32,48},... | collective-permute-start | bytes 294920 | tf_op jit(solution)/shard_map/ppermute | solution.py:283
  127.2 4.8 %collective-permute-start.32 = (bf16[64,768]{1,0:T(8,128)(2,1)S(1)}, bf16[64,768]{1,0:T(8,128)(2,1)S(1)}, u32[]{:S(2)}, u32[]{:S(2)}) collective-permute-start(bf16[64,768]{1,0:T(8,128)(2,1)S(1)} %subtract_convert_fusion.3), channel_id=1, source_target_pairs={{0,24},{4,28},{8,0},{12,4},{16,8},{20,12},{24,16},{28,20},{32,56},... | collective-permute-start | bytes 294920 | tf_op jit(solution)/shard_map/ppermute | solution.py:283
  132.1 4.7 %collective-permute-start.33 = (bf16[64,768]{1,0:T(8,128)(2,1)S(1)}, bf16[64,768]{1,0:T(8,128)(2,1)S(1)}, u32[]{:S(2)}, u32[]{:S(2)}) collective-permute-start(bf16[64,768]{1,0:T(8,128)(2,1)S(1)} %subtract_convert_fusion.2), channel_id=1, source_target_pairs={{0,32},{4,36},{8,40},{12,44},{16,48},{20,52},{24,56},{28,60},{32,6... | collective-permute-start | bytes 294920 | tf_op jit(solution)/shard_map/ppermute | solution.py:283
  132.8 6.4 %collective-permute-start.34 = (bf16[64,768]{1,0:T(8,128)(2,1)S(1)}, bf16[64,768]{1,0:T(8,128)(2,1)S(1)}, u32[]{:S(2)}, u32[]{:S(2)}) collective-permute-start(bf16[64,768]{1,0:T(8,128)(2,1)S(1)} %subtract_convert_fusion.2), channel_id=1, source_target_pairs={{0,64},{4,68},{8,72},{12,76},{16,80},{20,84},{24,88},{28,92},{32,9... | collective-permute-start | bytes 294920 | tf_op jit(solution)/shard_map/ppermute | solution.py:283
  135.8 4.7 %collective-permute-start.35 = (bf16[64,768]{1,0:T(8,128)(2,1)S(1)}, bf16[64,768]{1,0:T(8,128)(2,1)S(1)}, u32[]{:S(2)}, u32[]{:S(2)}) collective-permute-start(bf16[64,768]{1,0:T(8,128)(2,1)S(1)} %subtract_convert_fusion.2), channel_id=1, source_target_pairs={{0,96},{4,100},{8,104},{12,108},{16,112},{20,116},{24,120},{28,124... | collective-permute-start | bytes 294920 | tf_op jit(solution)/shard_map/ppermute | solution.py:283
  140.7 2.7 %collective-permute-start.36 = (bf16[64,768]{1,0:T(8,128)(2,1)S(1)}, bf16[64,768]{1,0:T(8,128)(2,1)S(1)}, u32[]{:S(2)}, u32[]{:S(2)}) collective-permute-start(bf16[64,768]{1,0:T(8,128)(2,1)S(1)} %get-tuple-element.65), channel_id=1, source_target_pairs={{0,4},{4,0},{8,12},{12,8},{16,20},{20,16},{24,28},{28,24},{32,36},... | collective-permute-start | bytes 294920 | tf_op jit(solution)/shard_map/ppermute | solution.py:283
  (6 other events, 11.7 us)

commit v6 on v5

--- a/solution.py
+++ b/solution.py
@@ -288,7 +288,7 @@
         chip = own + other
         mine = jnp.where(core == 0, chip[:half], chip[half:])
         came = send(mine, [z_shift(k) for k in (1, 2, 3)])
-        plane = mine + came[0] + came[1] + came[2]
+        plane = mine + came[1] + came[0] + came[2]
         below = sum(jnp.where(z_at >= k, c, 0.0) for k, c in zip((1, 2, 3), came, strict=True))
         plane, beside_z = lax.optimization_barrier((plane, beside_z))
         came = send(plane, [x_shift(k) for k in (1, 2, 3)])

time: 145 us -> 145 us (level)
  no operation moved by 1% of the time
where the time goes in v6:
time: 145 us
  starting transfers between devices  57.4 us (40%)
  waiting for transfers between devices  47.8 us (33%)
  Pallas kernels  19.3 us (13%)
  blocking collectives  7.55 us (5%)
  local copies, waits for them, and re-layouts  6.6 us (5%)
  other arithmetic  4.72 us (3%)
    ppermute x12, waiting for transfers between devices, deliver(): total = total + lax.ppermute(shares[k], 'tp', ring(k)).astype(F32)  22.8 us
    ppermute x16, starting transfers between devices, send(): lax.ppermute(message, 'tm', p).astype(F32) + t  19.9 us
    ppermute x12, starting transfers between devices, deliver(): total = total + lax.ppermute(shares[k], 'tp', ring(k)).astype(F32)  16.3 us
    ppermute x16, waiting for transfers between devices, send(): lax.ppermute(message, 'tm', p).astype(F32) + t  16.1 us
    all_to_all x1, starting transfers between devices, body(): all_gaps = lax.all_to_all(sent, 'tm', 0, 0)  9.44 us
    pallas_call x2, Pallas kernels, one(): pl.pallas_call(lambda *refs: one_body(s, tok, cols, *refs), out_shape=kep...  8.59 us
    pallas_call x1, Pallas kernels, both(): pl.pallas_call(lambda *refs: both_body(tok, cols, *refs), out_shape=share...  8.41 us
    all_to_all x1, blocking collectives, body(): mods = lax.all_to_all(made, 'tp', 0, 0)  7.55 us
  transfers between devices with their start and end apart: 38, of which 23 were waited for; matrix products, arithmetic and copies ran while one was open for 2% of the time, Pallas kernels for 7%

profile of v6, /device:TPU:1, one launch (start us, length us, event | category | flops | bytes accessed | tf_op | source)
XLA Modules:
  0.0 144.5 jit_solution(16465118181120169830)
XLA Ops:
  0.0 1.3 broadcast_in_dim.52
  1.3 1.1 copy-done.1
  2.6 2.2 %collective-permute-start = (bf16[264,768]{1,0:T(8,128)(2,1)S(1)}, bf16[264,768]{1,0:T(8,128)(2,1)S(1)}, u32[]{:S(2)}, u32[]{:S(2)}) collective-permute-start(bf16[264,768]{1,0:T(8,128)(2,1)S(1)} %centre.1.refs_1_), channel_id=1, source_target_pairs={{0,1},{1,2},{2,3},{3,0},{4,5},{5,6},{6,7},{7,4},{8,9},{9,10},{10,1... | collective-permute-start | bytes 1216520 | tf_op jit(solution)/shard_map/ppermute | solution.py:44
  4.7 2.6 %collective-permute-start.1 = (bf16[264,768]{1,0:T(8,128)(2,1)S(1)}, bf16[264,768]{1,0:T(8,128)(2,1)S(1)}, u32[]{:S(2)}, u32[]{:S(2)}) collective-permute-start(bf16[264,768]{1,0:T(8,128)(2,1)S(1)} %centre.1.refs_1_), channel_id=1, source_target_pairs={{0,2},{1,3},{2,0},{3,1},{4,6},{5,7},{6,4},{7,5},{8,10},{9,11},{10,... | collective-permute-start | bytes 1216520 | tf_op jit(solution)/shard_map/ppermute | solution.py:43
  7.4 1.1 collective-permute-start.2
  8.4 9.4 %all-to-all-start = ((s32[32,1,2]{2,1,0:T(1,128)}), s32[32,1,2]{2,1,0:T(1,128)S(1)}, u32[]{:S(2)}, u32[]{:S(2)}) async-start(s32[32,1,2]{2,1,0:T(1,128)} %broadcast_in_dim.52), calls=%async_computation | async-start | bytes 32768 | tf_op jit(solution)/shard_map/all_to_all | solution.py:262
  17.9 1.4 fusion.21
  19.9 1.2 compare_select_fusion.4.facts.refs_0_
  21.2 3.6 %all-to-all-done.all_gaps = s32[32,1,2]{2,1,0:T(1,128)S(1)} async-done(((s32[32,1,2]{2,1,0:T(1,128)}), s32[32,1,2]{2,1,0:T(1,128)S(1)}, u32[]{:S(2)}, u32[]{:S(2)}) %all-to-all-start) | async-done | bytes 288 | tf_op jit(solution)/shard_map/all_to_all | solution.py:262
  24.8 1.3 copy-done.4
  26.0 1.0 modulation.1
  27.0 7.5 %all_to_all.10.refs_5_ = f32[4,8,768]{2,1,0:T(8,128)S(1)} all-to-all(f32[4,8,768]{2,1,0:T(8,128)S(1)} %modulation.1), channel_id=1, replica_groups=mesh['tm'=32,'tp'=4] {'tp'}, dimensions={0} | all-to-all | bytes 196608 | tf_op jit(solution)/shard_map/all_to_all | solution.py:269
  34.6 8.4 %both.1 = (f32[128,768]{1,0:T(8,128)S(1)}, bf16[128,768]{1,0:T(8,128)(2,1)}, bf16[128,768]{1,0:T(8,128)(2,1)}, bf16[128,768]{1,0:T(8,128)(2,1)}, f32[128,768]{1,...) custom-call(s32[8]{0:T(128)S(1)} %compare_select_fusion.4.facts.refs, ...), custom_call_target="tpu_custom_call" | custom-call | flops 4831838208 | bytes 18874368 | tf_op jit(solution)/shard_map/both/pallas_call | solution.py:207
  43.0 0.7 copy-done.3
  43.8 0.7 copy-done.5
  44.5 0.9 collective-permute-start.3
  46.0 2.1 %collective-permute-start.5 = (bf16[128,768]{1,0:T(8,128)(2,1)}, bf16[128,768]{1,0:T(8,128)(2,1)S(1)}, u32[]{:S(2)}, u32[]{:S(2)}) collective-permute-start(bf16[128,768]{1,0:T(8,128)(2,1)} %get-tuple-element.39), channel_id=1, source_target_pairs={{0,3},{1,0},{2,1},{3,2},{4,7},{5,4},{6,5},{7,6},{8,11},{9,8},{10,9... | collective-permute-start | bytes 589832 | tf_op jit(solution)/shard_map/ppermute | solution.py:274
  48.1 2.7 %collective-permute-done.3 = bf16[128,768]{1,0:T(8,128)(2,1)S(1)} collective-permute-done((bf16[128,768]{1,0:T(8,128)(2,1)}, bf16[128,768]{1,0:T(8,128)(2,1)S(1)}, u32[]{:S(2)}, u32[]{:S(2)}) %collective-permute-start.3) | collective-permute-done | bytes 196640 | tf_op jit(solution)/shard_map/ppermute | solution.py:274
  50.8 5.9 %collective-permute-done.4 = bf16[128,768]{1,0:T(8,128)(2,1)S(1)} collective-permute-done((bf16[128,768]{1,0:T(8,128)(2,1)}, bf16[128,768]{1,0:T(8,128)(2,1)S(1)}, u32[]{:S(2)}, u32[]{:S(2)}) %collective-permute-start.4) | collective-permute-done | bytes 196640 | tf_op jit(solution)/shard_map/ppermute | solution.py:274
  56.8 1.1 convert_add_fusion.5
  57.9 1.0 collective-permute-start.6
  58.9 0.9 collective-permute-start.10
  59.9 0.8 collective-permute-start.11
  60.7 1.9 %collective-permute-start.12 = (bf16[128,768]{1,0:T(8,128)(2,1)S(1)}, bf16[128,768]{1,0:T(8,128)(2,1)S(1)}, u32[]{:S(2)}, u32[]{:S(2)}) collective-permute-start(bf16[128,768]{1,0:T(8,128)(2,1)S(1)} %get-tuple-element.49), channel_id=1, source_target_pairs={{0,3},{1,0},{2,1},{3,2},{4,7},{5,4},{6,5},{7,6},{8,11},{9,8},{10,9... | collective-permute-start | bytes 589832 | tf_op jit(solution)/shard_map/ppermute | solution.py:274
  63.1 1.8 %collective-permute-start.8 = (bf16[64,768]{1,0:T(8,128)(2,1)S(1)}, bf16[64,768]{1,0:T(8,128)(2,1)S(1)}, u32[]{:S(2)}, u32[]{:S(2)}) collective-permute-start(bf16[64,768]{1,0:T(8,128)(2,1)S(1)} %fusion.16), channel_id=1, source_target_pairs={{0,16},{4,20},{8,24},{12,28},{16,0},{20,4},{24,8},{28,12},{32,48},... | collective-permute-start | bytes 294920 | tf_op jit(solution)/shard_map/ppermute | solution.py:283
  64.8 2.3 %collective-permute-done.10 = bf16[128,768]{1,0:T(8,128)(2,1)S(1)} collective-permute-done((bf16[128,768]{1,0:T(8,128)(2,1)}, bf16[128,768]{1,0:T(8,128)(2,1)S(1)}, u32[]{:S(2)}, u32[]{:S(2)}) %collective-permute-start.10) | collective-permute-done | bytes 196640 | tf_op jit(solution)/shard_map/ppermute | solution.py:274
  67.2 0.9 collective-permute-start.9
  68.1 3.7 %collective-permute-done.11 = bf16[128,768]{1,0:T(8,128)(2,1)S(1)} collective-permute-done((bf16[128,768]{1,0:T(8,128)(2,1)S(1)}, bf16[128,768]{1,0:T(8,128)(2,1)S(1)}, u32[]{:S(2)}, u32[]{:S(2)}) %collective-permute-start.11) | collective-permute-done | bytes 196640 | tf_op jit(solution)/shard_map/ppermute | solution.py:274
  72.4 1.7 %collective-permute-start.14 = (bf16[64,768]{1,0:T(8,128)(2,1)S(1)}, bf16[64,768]{1,0:T(8,128)(2,1)S(1)}, u32[]{:S(2)}, u32[]{:S(2)}) collective-permute-start(bf16[64,768]{1,0:T(8,128)(2,1)S(1)} %convert_add_fusion.8), channel_id=1, source_target_pairs={{0,64},{4,68},{8,72},{12,76},{16,80},{20,84},{24,88},{28,92},{32,9... | collective-permute-start | bytes 294920 | tf_op jit(solution)/shard_map/ppermute | solution.py:283
  74.1 1.0 collective-permute-start.15
  75.1 2.4 %collective-permute-done.13 = bf16[64,768]{1,0:T(8,128)(2,1)S(1)} collective-permute-done((bf16[64,768]{1,0:T(8,128)(2,1)S(1)}, bf16[64,768]{1,0:T(8,128)(2,1)S(1)}, u32[]{:S(2)}, u32[]{:S(2)}) %collective-permute-start.13) | collective-permute-done | bytes 98336 | tf_op jit(solution)/shard_map/ppermute | solution.py:283
  78.8 2.5 %collective-permute-start.16 = (bf16[64,768]{1,0:T(8,128)(2,1)S(1)}, bf16[64,768]{1,0:T(8,128)(2,1)S(1)}, u32[]{:S(2)}, u32[]{:S(2)}) collective-permute-start(bf16[64,768]{1,0:T(8,128)(2,1)S(1)} %get-tuple-element.67), channel_id=1, source_target_pairs={{0,4},{4,0},{8,12},{12,8},{16,20},{20,16},{24,28},{28,24},{32,36},... | collective-permute-start | bytes 294920 | tf_op jit(solution)/shard_map/ppermute | solution.py:283
  81.3 0.9 collective-permute-done.16
  82.9 2.1 %collective-permute-start.21 = (bf16[128,768]{1,0:T(8,128)(2,1)S(1)}, bf16[128,768]{1,0:T(8,128)(2,1)S(1)}, u32[]{:S(2)}, u32[]{:S(2)}) collective-permute-start(bf16[128,768]{1,0:T(8,128)(2,1)S(1)} %get-tuple-element.70.after.refs_1_), channel_id=1, source_target_pairs={{0,2},{1,3},{2,0},{3,1},{4,6},{5,7},{6,4},{7,5},{8,10},{9,11},{10,... | collective-permute-start | bytes 589832 | tf_op jit(solution)/shard_map/ppermute | solution.py:43
  84.9 0.7 collective-permute-start.22
  85.6 1.1 arrive.1.refs_0_
  86.8 0.9 collective-permute-start.17
  87.6 1.3 collective-permute-start.18
  89.0 1.3 collective-permute-done.20.refs_2_
  90.9 2.9 %collective-permute-done.21.refs_3_ = bf16[128,768]{1,0:T(8,128)(2,1)S(1)} collective-permute-done((bf16[128,768]{1,0:T(8,128)(2,1)S(1)}, bf16[128,768]{1,0:T(8,128)(2,1)S(1)}, u32[]{:S(2)}, u32[]{:S(2)}) %collective-permute-start.21) | collective-permute-done | bytes 196640 | tf_op jit(solution)/shard_map/ppermute | solution.py:43
  93.9 1.0 collective-permute-done.22.refs_4_
  94.9 4.3 %one.2 = (f32[4,128,768]{2,1,0:T(8,128)S(1)}, f32[128,768]{1,0:T(8,128)S(1)}, bf16[128,768]{1,0:T(8,128)(2,1)S(1)}, bf16[128,768]{1,0:T(8,128)(2,1)S(1)}, bf16[128,768]{1,0:T(8,128)(2,1)S(1)}) custom-call(s32[8]{0:T(128)S(1)} %arrive.1.refs_0_, bf16[128,768]{1,0:T(8,128)(2,1)S(1)} %get-tuple-element.70.after.refs_1_, ...), custom_call_target="tpu_custom_call" | custom-call | flops 2415919104 | bytes 18874368 | tf_op jit(solution)/shard_map/one/pallas_call | solution.py:224
  99.2 1.0 collective-permute-start.26
  100.2 3.6 %collective-permute-start.27 = (bf16[128,768]{1,0:T(8,128)(2,1)S(1)}, bf16[128,768]{1,0:T(8,128)(2,1)S(1)}, u32[]{:S(2)}, u32[]{:S(2)}) collective-permute-start(bf16[128,768]{1,0:T(8,128)(2,1)S(1)} %get-tuple-element.59), channel_id=1, source_target_pairs={{0,1},{1,2},{2,3},{3,0},{4,5},{5,6},{6,7},{7,4},{8,9},{9,10},{10,1... | collective-permute-start | bytes 589832 | tf_op jit(solution)/shard_map/ppermute | solution.py:274
  103.9 4.3 %one.3 = (f32[128,768]{1,0:T(8,128)S(1)}, bf16[128,768]{1,0:T(8,128)(2,1)S(1)}, bf16[128,768]{1,0:T(8,128)(2,1)S(1)}, bf16[128,768]{1,0:T(8,128)(2,1)S(1)}) custom-call(s32[8]{0:T(128)S(1)} %arrive.1.refs_0_, bf16[128,768]{1,0:T(8,128)(2,1)S(1)} %get-tuple-element.69.refs_1_, bf16[128,768]{1,0:T(8,128)(2,1)S(1)} %collective-permute-done.17.refs_2_, ...), custom_call_target="tpu_custom_call" | custom-call | flops 2415919104 | bytes 18874368 | tf_op jit(solution)/shard_map/one/pallas_call | solution.py:224
  108.3 1.9 %collective-permute-start.23 = (bf16[128,768]{1,0:T(8,128)(2,1)S(1)}, bf16[128,768]{1,0:T(8,128)(2,1)S(1)}, u32[]{:S(2)}, u32[]{:S(2)}) collective-permute-start(bf16[128,768]{1,0:T(8,128)(2,1)S(1)} %get-tuple-element.54), channel_id=1, source_target_pairs={{0,2},{1,3},{2,0},{3,1},{4,6},{5,7},{6,4},{7,5},{8,10},{9,11},{10,... | collective-permute-start | bytes 589832 | tf_op jit(solution)/shard_map/ppermute | solution.py:274
  110.1 1.1 collective-permute-start.24
  111.2 1.6 %collective-permute-start.25 = (bf16[128,768]{1,0:T(8,128)(2,1)S(1)}, bf16[128,768]{1,0:T(8,128)(2,1)S(1)}, u32[]{:S(2)}, u32[]{:S(2)}) collective-permute-start(bf16[128,768]{1,0:T(8,128)(2,1)S(1)} %get-tuple-element.56), channel_id=1, source_target_pairs={{0,3},{1,0},{2,1},{3,2},{4,7},{5,4},{6,5},{7,6},{8,11},{9,8},{10,9... | collective-permute-start | bytes 589832 | tf_op jit(solution)/shard_map/ppermute | solution.py:274
  112.9 1.5 %collective-permute-done.23 = bf16[128,768]{1,0:T(8,128)(2,1)S(1)} collective-permute-done((bf16[128,768]{1,0:T(8,128)(2,1)S(1)}, bf16[128,768]{1,0:T(8,128)(2,1)S(1)}, u32[]{:S(2)}, u32[]{:S(2)}) %collective-permute-start.23) | collective-permute-done | bytes 196640 | tf_op jit(solution)/shard_map/ppermute | solution.py:274
  114.4 5.5 %collective-permute-done.24 = bf16[128,768]{1,0:T(8,128)(2,1)S(1)} collective-permute-done((bf16[128,768]{1,0:T(8,128)(2,1)S(1)}, bf16[128,768]{1,0:T(8,128)(2,1)S(1)}, u32[]{:S(2)}, u32[]{:S(2)}) %collective-permute-start.24) | collective-permute-done | bytes 196640 | tf_op jit(solution)/shard_map/ppermute | solution.py:274
  119.9 1.1 collective-permute-done.25
  121.2 1.5 %collective-permute-start.29 = (bf16[128,768]{1,0:T(8,128)(2,1)S(1)}, bf16[128,768]{1,0:T(8,128)(2,1)S(1)}, u32[]{:S(2)}, u32[]{:S(2)}) collective-permute-start(bf16[128,768]{1,0:T(8,128)(2,1)S(1)} %subtract_convert_fusion), channel_id=1, source_target_pairs={{0,4},{4,0},{8,12},{12,8},{16,20},{20,16},{24,28},{28,24},{32,36},... | collective-permute-start | bytes 589832 | tf_op jit(solution)/shard_map/ppermute | solution.py:283
  122.7 1.1 collective-permute-done.29
  124.3 2.9 %collective-permute-start.31 = (bf16[64,768]{1,0:T(8,128)(2,1)S(1)}, bf16[64,768]{1,0:T(8,128)(2,1)S(1)}, u32[]{:S(2)}, u32[]{:S(2)}) collective-permute-start(bf16[64,768]{1,0:T(8,128)(2,1)S(1)} %subtract_convert_fusion.3), channel_id=1, source_target_pairs={{0,16},{4,20},{8,24},{12,28},{16,0},{20,4},{24,8},{28,12},{32,48},... | collective-permute-start | bytes 294920 | tf_op jit(solution)/shard_map/ppermute | solution.py:283
  127.2 2.0 %collective-permute-done.30 = bf16[64,768]{1,0:T(8,128)(2,1)S(1)} collective-permute-done((bf16[64,768]{1,0:T(8,128)(2,1)S(1)}, bf16[64,768]{1,0:T(8,128)(2,1)S(1)}, u32[]{:S(2)}, u32[]{:S(2)}) %collective-permute-start.30) | collective-permute-done | bytes 98336 | tf_op jit(solution)/shard_map/ppermute | solution.py:283
  129.2 2.6 %collective-permute-done.31 = bf16[64,768]{1,0:T(8,128)(2,1)S(1)} collective-permute-done((bf16[64,768]{1,0:T(8,128)(2,1)S(1)}, bf16[64,768]{1,0:T(8,128)(2,1)S(1)}, u32[]{:S(2)}, u32[]{:S(2)}) %collective-permute-start.31) | collective-permute-done | bytes 98336 | tf_op jit(solution)/shard_map/ppermute | solution.py:283
  132.1 0.7 collective-permute-start.33
  132.8 3.0 %collective-permute-start.34 = (bf16[64,768]{1,0:T(8,128)(2,1)S(1)}, bf16[64,768]{1,0:T(8,128)(2,1)S(1)}, u32[]{:S(2)}, u32[]{:S(2)}) collective-permute-start(bf16[64,768]{1,0:T(8,128)(2,1)S(1)} %subtract_convert_fusion.2), channel_id=1, source_target_pairs={{0,64},{4,68},{8,72},{12,76},{16,80},{20,84},{24,88},{28,92},{32,9... | collective-permute-start | bytes 294920 | tf_op jit(solution)/shard_map/ppermute | solution.py:283
  135.8 1.1 collective-permute-done.33
  136.9 2.4 %collective-permute-done.34 = bf16[64,768]{1,0:T(8,128)(2,1)S(1)} collective-permute-done((bf16[64,768]{1,0:T(8,128)(2,1)S(1)}, bf16[64,768]{1,0:T(8,128)(2,1)S(1)}, u32[]{:S(2)}, u32[]{:S(2)}) %collective-permute-start.34) | collective-permute-done | bytes 98336 | tf_op jit(solution)/shard_map/ppermute | solution.py:283
  139.2 1.2 collective-permute-done.35
  140.7 1.7 %collective-permute-start.36 = (bf16[64,768]{1,0:T(8,128)(2,1)S(1)}, bf16[64,768]{1,0:T(8,128)(2,1)S(1)}, u32[]{:S(2)}, u32[]{:S(2)}) collective-permute-start(bf16[64,768]{1,0:T(8,128)(2,1)S(1)} %get-tuple-element.65), channel_id=1, source_target_pairs={{0,4},{4,0},{8,12},{12,8},{16,20},{20,16},{24,28},{28,24},{32,36},... | collective-permute-start | bytes 294920 | tf_op jit(solution)/shard_map/ppermute | solution.py:283
  142.4 0.9 collective-permute-done.36
  143.6 0.9 pad_maximum_fusion
  (110 shorter events, 5.8 us)
Async XLA Ops:
  2.4 32.2 %slice-start.4 = ((s8[4718592]{0:T(1024)(128)(4,1)}), s8[524288]{0:T(1024)(128)(4,1)S(1)}, s32[]{:S(2)}) async-start(s8[4718592]{0:T(1024)(128)(4,1)} %bitcast.26), calls=%async_computation.6 | async-start | bytes 1048576
  2.6 32.0 %collective-permute-start = (bf16[264,768]{1,0:T(8,128)(2,1)S(1)}, bf16[264,768]{1,0:T(8,128)(2,1)S(1)}, u32[]{:S(2)}, u32[]{:S(2)}) collective-permute-start(bf16[264,768]{1,0:T(8,128)(2,1)S(1)} %centre.1.refs_1_), channel_id=1, source_target_pairs={{0,1},{1,2},{2,3},{3,0},{4,5},{5,6},{6,7},{7,4},{8,9},{9,10},{10,1... | collective-permute-start | bytes 1216520 | tf_op jit(solution)/shard_map/ppermute | solution.py:44
  4.7 29.8 %collective-permute-start.1 = (bf16[264,768]{1,0:T(8,128)(2,1)S(1)}, bf16[264,768]{1,0:T(8,128)(2,1)S(1)}, u32[]{:S(2)}, u32[]{:S(2)}) collective-permute-start(bf16[264,768]{1,0:T(8,128)(2,1)S(1)} %centre.1.refs_1_), channel_id=1, source_target_pairs={{0,2},{1,3},{2,0},{3,1},{4,6},{5,7},{6,4},{7,5},{8,10},{9,11},{10,... | collective-permute-start | bytes 1216520 | tf_op jit(solution)/shard_map/ppermute | solution.py:43
  7.4 27.2 %collective-permute-start.2 = (bf16[264,768]{1,0:T(8,128)(2,1)S(1)}, bf16[264,768]{1,0:T(8,128)(2,1)S(1)}, u32[]{:S(2)}, u32[]{:S(2)}) collective-permute-start(bf16[264,768]{1,0:T(8,128)(2,1)S(1)} %centre.1.refs_1_), channel_id=1, source_target_pairs={{0,3},{1,0},{2,1},{3,2},{4,7},{5,4},{6,5},{7,6},{8,11},{9,8},{10,9... | collective-permute-start | bytes 1216520 | tf_op jit(solution)/shard_map/ppermute | solution.py:44
  8.4 16.3 %all-to-all-start = ((s32[32,1,2]{2,1,0:T(1,128)}), s32[32,1,2]{2,1,0:T(1,128)S(1)}, u32[]{:S(2)}, u32[]{:S(2)}) async-start(s32[32,1,2]{2,1,0:T(1,128)} %broadcast_in_dim.52), calls=%async_computation | async-start | bytes 32768 | tf_op jit(solution)/shard_map/all_to_all | solution.py:262
  26.0 8.6 %copy-start = (bf16[3072,3,768]{2,0,1:T(8,128)(2,1)S(1)}, bf16[3072,3,768]{2,0,1:T(8,128)(2,1)}, u32[]{:S(2)}) copy-start(bf16[3072,3,768]{2,0,1:T(8,128)(2,1)} %param.9) | copy-start | bytes 42467332
  26.0 8.6 %slice-start.5 = ((s8[4718592]{0:T(1024)(128)(4,1)}), s8[4194304]{0:T(1024)(128)(4,1)S(1)}, s32[]{:S(2)}) async-start(s8[4718592]{0:T(1024)(128)(4,1)} %bitcast.26), calls=%async_computation.7 | async-start | bytes 8388608
  44.5 6.3 %collective-permute-start.3 = (bf16[128,768]{1,0:T(8,128)(2,1)}, bf16[128,768]{1,0:T(8,128)(2,1)S(1)}, u32[]{:S(2)}, u32[]{:S(2)}) collective-permute-start(bf16[128,768]{1,0:T(8,128)(2,1)} %get-tuple-element.37), channel_id=1, source_target_pairs={{0,2},{1,3},{2,0},{3,1},{4,6},{5,7},{6,4},{7,5},{8,10},{9,11},{10,... | collective-permute-start | bytes 589832 | tf_op jit(solution)/shard_map/ppermute | solution.py:274
  45.4 11.4 %collective-permute-start.4 = (bf16[128,768]{1,0:T(8,128)(2,1)}, bf16[128,768]{1,0:T(8,128)(2,1)S(1)}, u32[]{:S(2)}, u32[]{:S(2)}) collective-permute-start(bf16[128,768]{1,0:T(8,128)(2,1)} %get-tuple-element.38), channel_id=1, source_target_pairs={{0,1},{1,2},{2,3},{3,0},{4,5},{5,6},{6,7},{7,4},{8,9},{9,10},{10,1... | collective-permute-start | bytes 589832 | tf_op jit(solution)/shard_map/ppermute | solution.py:274
  46.0 10.8 %collective-permute-start.5 = (bf16[128,768]{1,0:T(8,128)(2,1)}, bf16[128,768]{1,0:T(8,128)(2,1)S(1)}, u32[]{:S(2)}, u32[]{:S(2)}) collective-permute-start(bf16[128,768]{1,0:T(8,128)(2,1)} %get-tuple-element.39), channel_id=1, source_target_pairs={{0,3},{1,0},{2,1},{3,2},{4,7},{5,4},{6,5},{7,6},{8,11},{9,8},{10,9... | collective-permute-start | bytes 589832 | tf_op jit(solution)/shard_map/ppermute | solution.py:274
  57.9 4.8 %copy-start.14 = (bf16[128,768]{1,0:T(8,128)(2,1)}, bf16[128,768]{1,0:T(8,128)(2,1)S(1)}, u32[]{:S(2)}) copy-start(bf16[128,768]{1,0:T(8,128)(2,1)S(1)} %fusion.15) | copy-start | bytes 589828
  57.9 4.7 %collective-permute-start.6 = (bf16[128,768]{1,0:T(8,128)(2,1)S(1)}, bf16[128,768]{1,0:T(8,128)(2,1)S(1)}, u32[]{:S(2)}, u32[]{:S(2)}) collective-permute-start(bf16[128,768]{1,0:T(8,128)(2,1)S(1)} %fusion.15), channel_id=1, source_target_pairs={{0,4},{4,0},{8,12},{12,8},{16,20},{20,16},{24,28},{28,24},{32,36},... | collective-permute-start | bytes 589832 | tf_op jit(solution)/shard_map/ppermute | solution.py:283
  58.9 8.2 %collective-permute-start.10 = (bf16[128,768]{1,0:T(8,128)(2,1)}, bf16[128,768]{1,0:T(8,128)(2,1)S(1)}, u32[]{:S(2)}, u32[]{:S(2)}) collective-permute-start(bf16[128,768]{1,0:T(8,128)(2,1)} %copy-done.5), channel_id=1, source_target_pairs={{0,2},{1,3},{2,0},{3,1},{4,6},{5,7},{6,4},{7,5},{8,10},{9,11},{10,... | collective-permute-start | bytes 589832 | tf_op jit(solution)/shard_map/ppermute | solution.py:274
  59.9 11.9 %collective-permute-start.11 = (bf16[128,768]{1,0:T(8,128)(2,1)S(1)}, bf16[128,768]{1,0:T(8,128)(2,1)S(1)}, u32[]{:S(2)}, u32[]{:S(2)}) collective-permute-start(bf16[128,768]{1,0:T(8,128)(2,1)S(1)} %get-tuple-element.48), channel_id=1, source_target_pairs={{0,1},{1,2},{2,3},{3,0},{4,5},{5,6},{6,7},{7,4},{8,9},{9,10},{10,1... | collective-permute-start | bytes 589832 | tf_op jit(solution)/shard_map/ppermute | solution.py:274
  60.7 11.0 %collective-permute-start.12 = (bf16[128,768]{1,0:T(8,128)(2,1)S(1)}, bf16[128,768]{1,0:T(8,128)(2,1)S(1)}, u32[]{:S(2)}, u32[]{:S(2)}) collective-permute-start(bf16[128,768]{1,0:T(8,128)(2,1)S(1)} %get-tuple-element.49), channel_id=1, source_target_pairs={{0,3},{1,0},{2,1},{3,2},{4,7},{5,4},{6,5},{7,6},{8,11},{9,8},{10,9... | collective-permute-start | bytes 589832 | tf_op jit(solution)/shard_map/ppermute | solution.py:274
  62.6 19.9 %copy-start.8 = (bf16[128,768]{1,0:T(8,128)(2,1)}, bf16[128,768]{1,0:T(8,128)(2,1)S(1)}, u32[]{:S(2)}) copy-start(bf16[128,768]{1,0:T(8,128)(2,1)S(1)} %collective-permute-done.6) | copy-start | bytes 589828
  62.6 19.8 %copy-start.6 = (f32[128,768]{1,0:T(8,128)}, f32[128,768]{1,0:T(8,128)S(1)}, u32[]{:S(2)}) copy-start(f32[128,768]{1,0:T(8,128)S(1)} %convert_add_fusion.1) | copy-start | bytes 1179652
  62.7 9.1 %collective-permute-start.7 = (bf16[64,768]{1,0:T(8,128)(2,1)S(1)}, bf16[64,768]{1,0:T(8,128)(2,1)S(1)}, u32[]{:S(2)}, u32[]{:S(2)}) collective-permute-start(bf16[64,768]{1,0:T(8,128)(2,1)S(1)} %fusion.16), channel_id=1, source_target_pairs={{0,8},{4,12},{8,16},{12,20},{16,24},{20,28},{24,0},{28,4},{32,40},... | collective-permute-start | bytes 294920 | tf_op jit(solution)/shard_map/ppermute | solution.py:283
  63.1 8.8 %collective-permute-start.8 = (bf16[64,768]{1,0:T(8,128)(2,1)S(1)}, bf16[64,768]{1,0:T(8,128)(2,1)S(1)}, u32[]{:S(2)}, u32[]{:S(2)}) collective-permute-start(bf16[64,768]{1,0:T(8,128)(2,1)S(1)} %fusion.16), channel_id=1, source_target_pairs={{0,16},{4,20},{8,24},{12,28},{16,0},{20,4},{24,8},{28,12},{32,48},... | collective-permute-start | bytes 294920 | tf_op jit(solution)/shard_map/ppermute | solution.py:283
  67.2 4.7 %collective-permute-start.9 = (bf16[64,768]{1,0:T(8,128)(2,1)S(1)}, bf16[64,768]{1,0:T(8,128)(2,1)S(1)}, u32[]{:S(2)}, u32[]{:S(2)}) collective-permute-start(bf16[64,768]{1,0:T(8,128)(2,1)S(1)} %fusion.16), channel_id=1, source_target_pairs={{0,24},{4,28},{8,0},{12,4},{16,8},{20,12},{24,16},{28,20},{32,56},... | collective-permute-start | bytes 294920 | tf_op jit(solution)/shard_map/ppermute | solution.py:283
  71.9 10.6 %copy-start.10 = (bf16[64,768]{1,0:T(8,128)(2,1)}, bf16[64,768]{1,0:T(8,128)(2,1)S(1)}, u32[]{:S(2)}) copy-start(bf16[64,768]{1,0:T(8,128)(2,1)S(1)} %collective-permute-done.8) | copy-start | bytes 294916
  71.9 10.6 %copy-start.12 = (bf16[64,768]{1,0:T(8,128)(2,1)}, bf16[64,768]{1,0:T(8,128)(2,1)S(1)}, u32[]{:S(2)}) copy-start(bf16[64,768]{1,0:T(8,128)(2,1)S(1)} %collective-permute-done.9) | copy-start | bytes 294916
  71.9 10.5 %copy-start.16 = (bf16[64,768]{1,0:T(8,128)(2,1)}, bf16[64,768]{1,0:T(8,128)(2,1)S(1)}, u32[]{:S(2)}) copy-start(bf16[64,768]{1,0:T(8,128)(2,1)S(1)} %convert_add_fusion.8) | copy-start | bytes 294916
  72.0 5.5 %collective-permute-start.13 = (bf16[64,768]{1,0:T(8,128)(2,1)S(1)}, bf16[64,768]{1,0:T(8,128)(2,1)S(1)}, u32[]{:S(2)}, u32[]{:S(2)}) collective-permute-start(bf16[64,768]{1,0:T(8,128)(2,1)S(1)} %convert_add_fusion.8), channel_id=1, source_target_pairs={{0,32},{4,36},{8,40},{12,44},{16,48},{20,52},{24,56},{28,60},{32,6... | collective-permute-start | bytes 294920 | tf_op jit(solution)/shard_map/ppermute | solution.py:283
  72.4 5.6 %collective-permute-start.14 = (bf16[64,768]{1,0:T(8,128)(2,1)S(1)}, bf16[64,768]{1,0:T(8,128)(2,1)S(1)}, u32[]{:S(2)}, u32[]{:S(2)}) collective-permute-start(bf16[64,768]{1,0:T(8,128)(2,1)S(1)} %convert_add_fusion.8), channel_id=1, source_target_pairs={{0,64},{4,68},{8,72},{12,76},{16,80},{20,84},{24,88},{28,92},{32,9... | collective-permute-start | bytes 294920 | tf_op jit(solution)/shard_map/ppermute | solution.py:283
  74.1 4.6 %collective-permute-start.15 = (bf16[64,768]{1,0:T(8,128)(2,1)S(1)}, bf16[64,768]{1,0:T(8,128)(2,1)S(1)}, u32[]{:S(2)}, u32[]{:S(2)}) collective-permute-start(bf16[64,768]{1,0:T(8,128)(2,1)S(1)} %convert_add_fusion.8), channel_id=1, source_target_pairs={{0,96},{4,100},{8,104},{12,108},{16,112},{20,116},{24,120},{28,124... | collective-permute-start | bytes 294920 | tf_op jit(solution)/shard_map/ppermute | solution.py:283
  77.5 4.8 %copy-start.18 = (bf16[64,768]{1,0:T(8,128)(2,1)}, bf16[64,768]{1,0:T(8,128)(2,1)S(1)}, u32[]{:S(2)}) copy-start(bf16[64,768]{1,0:T(8,128)(2,1)S(1)} %collective-permute-done.13) | copy-start | bytes 294916
  78.8 3.5 %collective-permute-start.16 = (bf16[64,768]{1,0:T(8,128)(2,1)S(1)}, bf16[64,768]{1,0:T(8,128)(2,1)S(1)}, u32[]{:S(2)}, u32[]{:S(2)}) collective-permute-start(bf16[64,768]{1,0:T(8,128)(2,1)S(1)} %get-tuple-element.67), channel_id=1, source_target_pairs={{0,4},{4,0},{8,12},{12,8},{16,20},{20,16},{24,28},{28,24},{32,36},... | collective-permute-start | bytes 294920 | tf_op jit(solution)/shard_map/ppermute | solution.py:283
  82.5 12.4 %slice-start = ((s8[14155776]{0:T(1024)(128)(4,1)}), s8[4194304]{0:T(1024)(128)(4,1)S(1)}, s32[]{:S(2)}) async-start(s8[14155776]{0:T(1024)(128)(4,1)} %bitcast.22), calls=%async_computation.2 | async-start | bytes 8388608
  82.5 12.4 %slice-start.6 = ((s8[4718592]{0:T(1024)(128)(4,1)}), s8[4194304]{0:T(1024)(128)(4,1)S(1)}, s32[]{:S(2)}) async-start(s8[4718592]{0:T(1024)(128)(4,1)} %bitcast.28), calls=%async_computation.8 | async-start | bytes 8388608
  82.5 12.4 %slice-start.1 = ((s8[14155776]{0:T(1024)(128)(4,1)}), s8[4194304]{0:T(1024)(128)(4,1)S(1)}, s32[]{:S(2)}) async-start(s8[14155776]{0:T(1024)(128)(4,1)} %bitcast.22), calls=%async_computation.3 | async-start | bytes 8388608
  82.5 12.4 %slice-start.2 = ((s8[14155776]{0:T(1024)(128)(4,1)}), s8[4194304]{0:T(1024)(128)(4,1)S(1)}, s32[]{:S(2)}) async-start(s8[14155776]{0:T(1024)(128)(4,1)} %bitcast.22), calls=%async_computation.4 | async-start | bytes 8388608
  82.5 12.4 %slice-start.3 = ((s8[14155776]{0:T(1024)(128)(4,1)}), s8[1572864]{0:T(1024)(128)(4,1)S(1)}, s32[]{:S(2)}) async-start(s8[14155776]{0:T(1024)(128)(4,1)} %bitcast.22), calls=%async_computation.5 | async-start | bytes 3145728
  82.5 12.4 %slice-start.7 = ((s8[4718592]{0:T(1024)(128)(4,1)}), s8[524288]{0:T(1024)(128)(4,1)S(1)}, s32[]{:S(2)}) async-start(s8[4718592]{0:T(1024)(128)(4,1)} %bitcast.28), calls=%async_computation.9 | async-start | bytes 1048576
  82.5 7.8 %collective-permute-start.20 = (bf16[128,768]{1,0:T(8,128)(2,1)S(1)}, bf16[128,768]{1,0:T(8,128)(2,1)S(1)}, u32[]{:S(2)}, u32[]{:S(2)}) collective-permute-start(bf16[128,768]{1,0:T(8,128)(2,1)S(1)} %get-tuple-element.70.after.refs_1_), channel_id=1, source_target_pairs={{0,1},{1,2},{2,3},{3,0},{4,5},{5,6},{6,7},{7,4},{8,9},{9,10},{10,1... | collective-permute-start | bytes 589832 | tf_op jit(solution)/shard_map/ppermute | solution.py:44
  82.9 11.0 %collective-permute-start.21 = (bf16[128,768]{1,0:T(8,128)(2,1)S(1)}, bf16[128,768]{1,0:T(8,128)(2,1)S(1)}, u32[]{:S(2)}, u32[]{:S(2)}) collective-permute-start(bf16[128,768]{1,0:T(8,128)(2,1)S(1)} %get-tuple-element.70.after.refs_1_), channel_id=1, source_target_pairs={{0,2},{1,3},{2,0},{3,1},{4,6},{5,7},{6,4},{7,5},{8,10},{9,11},{10,... | collective-permute-start | bytes 589832 | tf_op jit(solution)/shard_map/ppermute | solution.py:43
  84.9 10.0 %collective-permute-start.22 = (bf16[128,768]{1,0:T(8,128)(2,1)S(1)}, bf16[128,768]{1,0:T(8,128)(2,1)S(1)}, u32[]{:S(2)}, u32[]{:S(2)}) collective-permute-start(bf16[128,768]{1,0:T(8,128)(2,1)S(1)} %get-tuple-element.70.after.refs_1_), channel_id=1, source_target_pairs={{0,3},{1,0},{2,1},{3,2},{4,7},{5,4},{6,5},{7,6},{8,11},{9,8},{10,9... | collective-permute-start | bytes 589832 | tf_op jit(solution)/shard_map/ppermute | solution.py:44
  86.8 17.1 %collective-permute-start.17 = (bf16[128,768]{1,0:T(8,128)(2,1)S(1)}, bf16[128,768]{1,0:T(8,128)(2,1)S(1)}, u32[]{:S(2)}, u32[]{:S(2)}) collective-permute-start(bf16[128,768]{1,0:T(8,128)(2,1)S(1)} %get-tuple-element.69.refs_1_), channel_id=1, source_target_pairs={{0,1},{1,2},{2,3},{3,0},{4,5},{5,6},{6,7},{7,4},{8,9},{9,10},{10,1... | collective-permute-start | bytes 589832 | tf_op jit(solution)/shard_map/ppermute | solution.py:44
  87.6 16.2 %collective-permute-start.18 = (bf16[128,768]{1,0:T(8,128)(2,1)S(1)}, bf16[128,768]{1,0:T(8,128)(2,1)S(1)}, u32[]{:S(2)}, u32[]{:S(2)}) collective-permute-start(bf16[128,768]{1,0:T(8,128)(2,1)S(1)} %get-tuple-element.69.refs_1_), channel_id=1, source_target_pairs={{0,2},{1,3},{2,0},{3,1},{4,6},{5,7},{6,4},{7,5},{8,10},{9,11},{10,... | collective-permute-start | bytes 589832 | tf_op jit(solution)/shard_map/ppermute | solution.py:43
  90.3 13.5 %collective-permute-start.19 = (bf16[128,768]{1,0:T(8,128)(2,1)S(1)}, bf16[128,768]{1,0:T(8,128)(2,1)S(1)}, u32[]{:S(2)}, u32[]{:S(2)}) collective-permute-start(bf16[128,768]{1,0:T(8,128)(2,1)S(1)} %get-tuple-element.69.refs_1_), channel_id=1, source_target_pairs={{0,3},{1,0},{2,1},{3,2},{4,7},{5,4},{6,5},{7,6},{8,11},{9,8},{10,9... | collective-permute-start | bytes 589832 | tf_op jit(solution)/shard_map/ppermute | solution.py:44
  99.2 12.0 %collective-permute-start.26 = (bf16[128,768]{1,0:T(8,128)(2,1)S(1)}, bf16[128,768]{1,0:T(8,128)(2,1)S(1)}, u32[]{:S(2)}, u32[]{:S(2)}) collective-permute-start(bf16[128,768]{1,0:T(8,128)(2,1)S(1)} %get-tuple-element.58), channel_id=1, source_target_pairs={{0,2},{1,3},{2,0},{3,1},{4,6},{5,7},{6,4},{7,5},{8,10},{9,11},{10,... | collective-permute-start | bytes 589832 | tf_op jit(solution)/shard_map/ppermute | solution.py:274
  100.2 12.6 %collective-permute-start.27 = (bf16[128,768]{1,0:T(8,128)(2,1)S(1)}, bf16[128,768]{1,0:T(8,128)(2,1)S(1)}, u32[]{:S(2)}, u32[]{:S(2)}) collective-permute-start(bf16[128,768]{1,0:T(8,128)(2,1)S(1)} %get-tuple-element.59), channel_id=1, source_target_pairs={{0,1},{1,2},{2,3},{3,0},{4,5},{5,6},{6,7},{7,4},{8,9},{9,10},{10,1... | collective-permute-start | bytes 589832 | tf_op jit(solution)/shard_map/ppermute | solution.py:274
  103.8 9.0 %collective-permute-start.28 = (bf16[128,768]{1,0:T(8,128)(2,1)S(1)}, bf16[128,768]{1,0:T(8,128)(2,1)S(1)}, u32[]{:S(2)}, u32[]{:S(2)}) collective-permute-start(bf16[128,768]{1,0:T(8,128)(2,1)S(1)} %get-tuple-element.60), channel_id=1, source_target_pairs={{0,3},{1,0},{2,1},{3,2},{4,7},{5,4},{6,5},{7,6},{8,11},{9,8},{10,9... | collective-permute-start | bytes 589832 | tf_op jit(solution)/shard_map/ppermute | solution.py:274
  103.8 17.3 %copy-start.2 = (f32[2,128,768]{2,1,0:T(8,128)S(1)}, f32[2,128,768]{2,1,0:T(8,128)}, u32[]{:S(2)}) copy-start(f32[2,128,768]{2,1,0:T(8,128)} %param.6) | copy-start | bytes 2359300
  103.9 17.3 %copy-start.15 = (bf16[128,768]{1,0:T(8,128)(2,1)S(1)}, bf16[128,768]{1,0:T(8,128)(2,1)}, u32[]{:S(2)}) copy-start(bf16[128,768]{1,0:T(8,128)(2,1)} %copy-done.14) | copy-start | bytes 589828
  103.9 19.9 %copy-start.9 = (bf16[128,768]{1,0:T(8,128)(2,1)S(1)}, bf16[128,768]{1,0:T(8,128)(2,1)}, u32[]{:S(2)}) copy-start(bf16[128,768]{1,0:T(8,128)(2,1)} %copy-done.8) | copy-start | bytes 589828
  108.2 15.7 %copy-start.7 = (f32[128,768]{1,0:T(8,128)S(1)}, f32[128,768]{1,0:T(8,128)}, u32[]{:S(2)}) copy-start(f32[128,768]{1,0:T(8,128)} %copy-done.6) | copy-start | bytes 1179652
  108.2 23.8 %copy-start.11 = (bf16[64,768]{1,0:T(8,128)(2,1)S(1)}, bf16[64,768]{1,0:T(8,128)(2,1)}, u32[]{:S(2)}) copy-start(bf16[64,768]{1,0:T(8,128)(2,1)} %copy-done.10) | copy-start | bytes 294916
  108.2 23.8 %copy-start.13 = (bf16[64,768]{1,0:T(8,128)(2,1)S(1)}, bf16[64,768]{1,0:T(8,128)(2,1)}, u32[]{:S(2)}) copy-start(bf16[64,768]{1,0:T(8,128)(2,1)} %copy-done.12) | copy-start | bytes 294916
  108.2 23.9 %copy-start.17 = (bf16[64,768]{1,0:T(8,128)(2,1)S(1)}, bf16[64,768]{1,0:T(8,128)(2,1)}, u32[]{:S(2)}) copy-start(bf16[64,768]{1,0:T(8,128)(2,1)} %copy-done.16) | copy-start | bytes 294916
  108.2 32.2 %copy-start.19 = (bf16[64,768]{1,0:T(8,128)(2,1)S(1)}, bf16[64,768]{1,0:T(8,128)(2,1)}, u32[]{:S(2)}) copy-start(bf16[64,768]{1,0:T(8,128)(2,1)} %copy-done.18) | copy-start | bytes 294916
  108.2 32.2 %copy-start.21 = (bf16[64,768]{1,0:T(8,128)(2,1)S(1)}, bf16[64,768]{1,0:T(8,128)(2,1)}, u32[]{:S(2)}) copy-start(bf16[64,768]{1,0:T(8,128)(2,1)} %copy-done.20) | copy-start | bytes 294916
  108.3 32.2 %copy-start.23 = (bf16[64,768]{1,0:T(8,128)(2,1)S(1)}, bf16[64,768]{1,0:T(8,128)(2,1)}, u32[]{:S(2)}) copy-start(bf16[64,768]{1,0:T(8,128)(2,1)} %copy-done.22) | copy-start | bytes 294916
  108.3 6.2 %collective-permute-start.23 = (bf16[128,768]{1,0:T(8,128)(2,1)S(1)}, bf16[128,768]{1,0:T(8,128)(2,1)S(1)}, u32[]{:S(2)}, u32[]{:S(2)}) collective-permute-start(bf16[128,768]{1,0:T(8,128)(2,1)S(1)} %get-tuple-element.54), channel_id=1, source_target_pairs={{0,2},{1,3},{2,0},{3,1},{4,6},{5,7},{6,4},{7,5},{8,10},{9,11},{10,... | collective-permute-start | bytes 589832 | tf_op jit(solution)/shard_map/ppermute | solution.py:274
  110.1 9.8 %collective-permute-start.24 = (bf16[128,768]{1,0:T(8,128)(2,1)S(1)}, bf16[128,768]{1,0:T(8,128)(2,1)S(1)}, u32[]{:S(2)}, u32[]{:S(2)}) collective-permute-start(bf16[128,768]{1,0:T(8,128)(2,1)S(1)} %get-tuple-element.55), channel_id=1, source_target_pairs={{0,1},{1,2},{2,3},{3,0},{4,5},{5,6},{6,7},{7,4},{8,9},{9,10},{10,1... | collective-permute-start | bytes 589832 | tf_op jit(solution)/shard_map/ppermute | solution.py:274
  111.2 9.8 %collective-permute-start.25 = (bf16[128,768]{1,0:T(8,128)(2,1)S(1)}, bf16[128,768]{1,0:T(8,128)(2,1)S(1)}, u32[]{:S(2)}, u32[]{:S(2)}) collective-permute-start(bf16[128,768]{1,0:T(8,128)(2,1)S(1)} %get-tuple-element.56), channel_id=1, source_target_pairs={{0,3},{1,0},{2,1},{3,2},{4,7},{5,4},{6,5},{7,6},{8,11},{9,8},{10,9... | collective-permute-start | bytes 589832 | tf_op jit(solution)/shard_map/ppermute | solution.py:274
  121.2 2.5 %collective-permute-start.29 = (bf16[128,768]{1,0:T(8,128)(2,1)S(1)}, bf16[128,768]{1,0:T(8,128)(2,1)S(1)}, u32[]{:S(2)}, u32[]{:S(2)}) collective-permute-start(bf16[128,768]{1,0:T(8,128)(2,1)S(1)} %subtract_convert_fusion), channel_id=1, source_target_pairs={{0,4},{4,0},{8,12},{12,8},{16,20},{20,16},{24,28},{28,24},{32,36},... | collective-permute-start | bytes 589832 | tf_op jit(solution)/shard_map/ppermute | solution.py:283
  123.9 5.3 %collective-permute-start.30 = (bf16[64,768]{1,0:T(8,128)(2,1)S(1)}, bf16[64,768]{1,0:T(8,128)(2,1)S(1)}, u32[]{:S(2)}, u32[]{:S(2)}) collective-permute-start(bf16[64,768]{1,0:T(8,128)(2,1)S(1)} %subtract_convert_fusion.3), channel_id=1, source_target_pairs={{0,8},{4,12},{8,16},{12,20},{16,24},{20,28},{24,0},{28,4},{32,40},... | collective-permute-start | bytes 294920 | tf_op jit(solution)/shard_map/ppermute | solution.py:283
  124.3 7.5 %collective-permute-start.31 = (bf16[64,768]{1,0:T(8,128)(2,1)S(1)}, bf16[64,768]{1,0:T(8,128)(2,1)S(1)}, u32[]{:S(2)}, u32[]{:S(2)}) collective-permute-start(bf16[64,768]{1,0:T(8,128)(2,1)S(1)} %subtract_convert_fusion.3), channel_id=1, source_target_pairs={{0,16},{4,20},{8,24},{12,28},{16,0},{20,4},{24,8},{28,12},{32,48},... | collective-permute-start | bytes 294920 | tf_op jit(solution)/shard_map/ppermute | solution.py:283
  127.2 4.8 %collective-permute-start.32 = (bf16[64,768]{1,0:T(8,128)(2,1)S(1)}, bf16[64,768]{1,0:T(8,128)(2,1)S(1)}, u32[]{:S(2)}, u32[]{:S(2)}) collective-permute-start(bf16[64,768]{1,0:T(8,128)(2,1)S(1)} %subtract_convert_fusion.3), channel_id=1, source_target_pairs={{0,24},{4,28},{8,0},{12,4},{16,8},{20,12},{24,16},{28,20},{32,56},... | collective-permute-start | bytes 294920 | tf_op jit(solution)/shard_map/ppermute | solution.py:283
  132.1 4.7 %collective-permute-start.33 = (bf16[64,768]{1,0:T(8,128)(2,1)S(1)}, bf16[64,768]{1,0:T(8,128)(2,1)S(1)}, u32[]{:S(2)}, u32[]{:S(2)}) collective-permute-start(bf16[64,768]{1,0:T(8,128)(2,1)S(1)} %subtract_convert_fusion.2), channel_id=1, source_target_pairs={{0,32},{4,36},{8,40},{12,44},{16,48},{20,52},{24,56},{28,60},{32,6... | collective-permute-start | bytes 294920 | tf_op jit(solution)/shard_map/ppermute | solution.py:283
  132.8 6.4 %collective-permute-start.34 = (bf16[64,768]{1,0:T(8,128)(2,1)S(1)}, bf16[64,768]{1,0:T(8,128)(2,1)S(1)}, u32[]{:S(2)}, u32[]{:S(2)}) collective-permute-start(bf16[64,768]{1,0:T(8,128)(2,1)S(1)} %subtract_convert_fusion.2), channel_id=1, source_target_pairs={{0,64},{4,68},{8,72},{12,76},{16,80},{20,84},{24,88},{28,92},{32,9... | collective-permute-start | bytes 294920 | tf_op jit(solution)/shard_map/ppermute | solution.py:283
  135.8 4.7 %collective-permute-start.35 = (bf16[64,768]{1,0:T(8,128)(2,1)S(1)}, bf16[64,768]{1,0:T(8,128)(2,1)S(1)}, u32[]{:S(2)}, u32[]{:S(2)}) collective-permute-start(bf16[64,768]{1,0:T(8,128)(2,1)S(1)} %subtract_convert_fusion.2), channel_id=1, source_target_pairs={{0,96},{4,100},{8,104},{12,108},{16,112},{20,116},{24,120},{28,124... | collective-permute-start | bytes 294920 | tf_op jit(solution)/shard_map/ppermute | solution.py:283
  140.7 2.7 %collective-permute-start.36 = (bf16[64,768]{1,0:T(8,128)(2,1)S(1)}, bf16[64,768]{1,0:T(8,128)(2,1)S(1)}, u32[]{:S(2)}, u32[]{:S(2)}) collective-permute-start(bf16[64,768]{1,0:T(8,128)(2,1)S(1)} %get-tuple-element.65), channel_id=1, source_target_pairs={{0,4},{4,0},{8,12},{12,8},{16,20},{20,16},{24,28},{28,24},{32,36},... | collective-permute-start | bytes 294920 | tf_op jit(solution)/shard_map/ppermute | solution.py:283
  (6 other events, 11.7 us)
